TPU v7x, 32 devices: a whole 2x2x4 slice. The times are simulated.
32 devices in a mesh: groups: 2 (over y), row: 16 (over z, x, core).
Axes of the slice: x: 2, y: 2, z: 4, core: 2. Of those that a mesh axis runs over, the one named last changes fastest.
Arguments:
- grad: bfloat16 [512, 15360], P(('groups', 'row')), parts along dimension 0, may hold values from -0.875 to 0.875
- stats: float32 [256, 1024, 1024], P(('groups', 'row')), parts along dimension 0, may hold values from -6 to 6
- roots: bfloat16 [256, 1024, 1024], P(('groups', 'row')), parts along dimension 0, may hold values from -0.1875 to 0.1875
- tile_slot: int32 [128], replicated, may hold values from -1 to 119, as said below
Outputs:
- new_stats: float32 [256, 1024, 1024], P(('groups', 'row')), parts along dimension 0
- precond: bfloat16 [512, 15360], P(('groups', 'row')), parts along dimension 0
There are 2 independent parts, one for each index of `groups`. A program takes and returns all parts, laid end to end along the dimension named above; an argument that names none is the same for every part. Nothing has to cross between parts.
Inputs may be any that keep to these rules, and one draw needn't show every extreme that they name: `tile_slot`: every number 0 to 119 appears exactly once; -1 marks an empty slot.
All inputs are finite; a program needn't handle non-finite values.
Results may differ from a plain program's by a relative error of at most 0.0049.
Values may be sent and summed in bfloat16 or wider, within the bound.
No kernel may reach another device: no remote copies, remote signals or barrier semaphores. Data moves between devices by JAX's collectives and lax.ppermute only.
A program may use at most 256 MiB of HBM per device.

v0:
```python
import jax
import jax.numpy as jnp
import numpy as np
from jax import lax
from jax.sharding import PartitionSpec as P

BETA = 0.9


def tile_tables(grid_len):
    first_list = []
    second_list = []
    for row_index in range(grid_len):
        for col_index in range(row_index, grid_len):
            first_list.append(row_index)
            second_list.append(col_index)
    return (np.array(first_list, np.int32), np.array(second_list, np.int32))


def lookup(tile_slot, grid_len):
    first_table, second_table = tile_tables(grid_len)
    tile_total = first_table.shape[0]
    clipped = jnp.maximum(tile_slot, 0)
    matches = clipped[:, None] == jnp.arange(tile_total, dtype=jnp.int32)[None, :]
    first_panel = jnp.sum(jnp.where(matches, jnp.asarray(first_table)[None, :], 0), axis=1).astype(
        jnp.int32
    )
    second_panel = jnp.sum(
        jnp.where(matches, jnp.asarray(second_table)[None, :], 0), axis=1
    ).astype(jnp.int32)
    return (first_panel, second_panel, tile_slot >= 0)


def root_times_second(second_arrived, roots, keep_first):
    result = lax.dot_general(
        second_arrived, roots, (((2,), (2,)), ((0,), (0,))), preferred_element_type=jnp.float32
    )
    return (result * keep_first[:, None, None]).astype(jnp.bfloat16)


def body(grad, stats, roots, tile_slot):
    col_width, order_len = grad.shape
    slot_count, tile_len = (stats.shape[0], stats.shape[1])
    grid_len = order_len // tile_len
    devices = lax.axis_size("row")
    all_cols = devices * col_width
    first_panel, second_panel, live_mask = lookup(tile_slot, grid_len)
    panels = grad.reshape(col_width, grid_len, tile_len)

    def outgoing(which_panel):
        picked = jnp.take(panels, which_panel, axis=1)
        return jnp.transpose(picked.reshape(col_width, devices, slot_count, tile_len), (2, 1, 0, 3))

    my_start = lax.axis_index("row") * slot_count
    my_first = lax.dynamic_slice_in_dim(first_panel, my_start, slot_count)
    my_second = lax.dynamic_slice_in_dim(second_panel, my_start, slot_count)
    my_live = lax.dynamic_slice_in_dim(live_mask, my_start, slot_count)
    keep_first = my_live.astype(jnp.float32)
    keep_second = (my_live & (my_first != my_second)).astype(jnp.float32)
    stacked = jnp.stack((outgoing(first_panel), outgoing(second_panel)), 1)
    arrived = lax.all_to_all(stacked, "row", split_axis=2, concat_axis=2, tiled=True).reshape(
        slot_count, 2, all_cols, tile_len
    )
    first_arrived = arrived[:, 0]
    second_arrived = arrived[:, 1]
    part_first = root_times_second(second_arrived, roots, keep_first)
    products = lax.dot_general(
        first_arrived,
        second_arrived,
        (((1,), (1,)), ((0,), (0,))),
        preferred_element_type=jnp.float32,
    )
    new_stats = jnp.where(my_live[:, None, None], BETA * stats + (1.0 - BETA) * products, stats)
    part_second = lax.dot_general(
        first_arrived, roots, (((2,), (1,)), ((0,), (0,))), preferred_element_type=jnp.float32
    )
    part_second = (part_second * keep_second[:, None, None]).astype(jnp.bfloat16)
    outgoing_parts = jnp.stack((part_first, part_second), 1)
    returned = lax.all_to_all(outgoing_parts, "row", split_axis=2, concat_axis=0, tiled=True)
    targets = jnp.stack((first_panel, second_panel), 1)
    selector = (targets[:, :, None] == jnp.arange(grid_len, dtype=jnp.int32)[None, None, :]).astype(
        jnp.bfloat16
    )
    summed = jnp.einsum("gkp,gkct->cpt", selector, returned, preferred_element_type=jnp.float32)
    return (new_stats, summed.reshape(col_width, order_len).astype(jnp.bfloat16))


def solution(mesh):
    placed = (
        P(("groups", "row"), None),
        P(("groups", "row"), None, None),
        P(("groups", "row"), None, None),
        P(),
    )
    return jax.shard_map(
        body,
        mesh=mesh,
        in_specs=placed,
        out_specs=(P(("groups", "row"), None, None), P(("groups", "row"), None)),
        check_vma=False,
    )
```

profile of v0, /device:TPU:11, one launch (start us, length us, event | category | flops | bytes accessed | tf_op | source)
XLA Modules:
  0.0 474.7 jit_solution(5533861113724775891)
XLA Ops:
  0.6 0.7 broadcast_maximum_fusion
  1.3 0.8 select_reduce_fusion.1
  2.1 1.1 copy.52
  3.2 2.8 gather_fusion.1
  6.0 2.6 select_bitcast_fusion
  8.7 4.3 copy.50
  13.0 2.8 gather_fusion
  15.8 0.0 copy-start
  15.8 2.8 select_bitcast_fusion.1
  18.5 4.3 copy.51
  22.8 0.0 copy-done
  22.8 6.3 %pad_maximum_fusion = bf16[8,2,16,16,1024]{4,0,2,3,1:T(8,128)(2,1)} fusion(bf16[8,1,16,16,1024]{4,0,2,3,1:T(8,128)(2,1)S(1)} %bitcast.69, bf16[8,1,16,16,1024]{4,0,2,3,1:T(8,128)(2,1)} %bitcast.70), kind=kLoop, calls=%fused_computation.3 | loop fusion | flops 4194304 | bytes 16777216 | tf_op jit(solution)/shard_map/stack | solution.py:60
  29.2 8.0 %copy.30 = bf16[8,2,16,16,1024]{4,0,3,1,2:T(8,128)(2,1)} copy(bf16[8,2,16,16,1024]{4,0,2,3,1:T(8,128)(2,1)} %pad_maximum_fusion) | data formatting | bytes 16777216 | tf_op jit(solution)/shard_map/stack | solution.py:60
  37.2 0.0 copy-start.1
  37.2 6.7 %all-to-all-start = ((bf16[8,2,16,16,1024]{4,0,3,1,2:T(8,128)(2,1)}), bf16[8,2,16,16,1024]{4,0,3,1,2:T(8,128)(2,1)}, u32[]{:S(2)}, u32[]{:S(2)}) async-start(bf16[8,2,16,16,1024]{4,0,3,1,2:T(8,128)(2,1)} %copy.30), calls=%async_computation | async-start | bytes 16777216 | tf_op jit(solution)/shard_map/all_to_all | solution.py:61
  43.9 0.0 copy-done.1
  43.9 0.1 fusion.16
  44.0 0.1 and_convert_fusion
  44.1 182.2 %all-to-all-done = bf16[8,2,16,16,1024]{4,0,3,1,2:T(8,128)(2,1)} async-done(((bf16[8,2,16,16,1024]{4,0,3,1,2:T(8,128)(2,1)}), bf16[8,2,16,16,1024]{4,0,3,1,2:T(8,128)(2,1)}, u32[]{:S(2)}, u32[]{:S(2)}) %all-to-all-start) | async-done | bytes 8388640 | tf_op jit(solution)/shard_map/all_to_all | solution.py:61
  226.2 11.3 %copy.31 = bf16[8,2,16,16,1024]{4,3,2,0,1:T(8,128)(2,1)} copy(bf16[8,2,16,16,1024]{4,0,3,1,2:T(8,128)(2,1)} %all-to-all-done) | data formatting | bytes 16777216 | tf_op jit(solution)/shard_map/all_to_all | solution.py:61
  237.5 13.5 %fusion.4 = bf16[8,1,256,1024]{3,2,0,1:T(8,128)(2,1)} fusion(f32[8]{0:T(128)S(1)} %and_convert_fusion, bf16[8,1024,1024]{2,1,0:T(8,128)(2,1)} %param.10, bf16[8,2,256,1024]{3,2,0,1:T(8,128)(2,1)} %bitcast.66), kind=kOutput, calls=%fused_computation.11 | convolution fusion | flops 4299161600 | bytes 25165856 | tf_op jit(solution)/shard_map/dot_general | solution.py:74
  251.0 10.8 %fusion.3 = bf16[8,1,256,1024]{3,2,0,1:T(8,128)(2,1)} fusion(f32[8]{0:T(128)S(1)} %get-tuple-element.5, bf16[8,1024,1024]{2,1,0:T(8,128)(2,1)} %param.10, bf16[8,2,256,1024]{3,2,0,1:T(8,128)(2,1)} %bitcast.67), kind=kOutput, calls=%fused_computation.10 | convolution fusion | flops 4299161600 | bytes 25165856 | tf_op jit(solution)/shard_map/dot_general | solution.py:35
  261.9 7.6 %pad_maximum_fusion.1 = bf16[8,2,256,1024]{3,2,0,1:T(8,128)(2,1)} fusion(bf16[8,1,256,1024]{3,2,0,1:T(8,128)(2,1)} %fusion.4, bf16[8,1,256,1024]{3,2,0,1:T(8,128)(2,1)} %fusion.3), kind=kLoop, calls=%fused_computation.4 | loop fusion | flops 4194304 | bytes 16777216 | tf_op jit(solution)/shard_map/stack | solution.py:78
  269.5 11.3 %copy.33 = bf16[8,2,256,1024]{3,0,1,2:T(8,128)(2,1)} copy(bf16[8,2,256,1024]{3,2,0,1:T(8,128)(2,1)} %pad_maximum_fusion.1) | data formatting | bytes 16777216 | tf_op jit(solution)/shard_map/stack | solution.py:78
  280.8 4.9 %all-to-all-start.1 = ((bf16[8,2,256,1024]{3,0,1,2:T(8,128)(2,1)}), bf16[8,2,256,1024]{3,0,1,2:T(8,128)(2,1)}, u32[]{:S(2)}, u32[]{:S(2)}) async-start(bf16[8,2,256,1024]{3,0,1,2:T(8,128)(2,1)} %copy.33), calls=%async_computation.1 | async-start | bytes 16777216 | tf_op jit(solution)/shard_map/all_to_all | solution.py:79
  285.7 26.2 %add_select_fusion = f32[8,1024,1024]{2,1,0:T(8,128)} fusion(f32[8,1024,1024]{2,1,0:T(8,128)} %param.9, pred[8]{0:T(512)(128)(4,1)S(1)} %get-tuple-element.6, bf16[8,2,256,1024]{3,2,0,1:T(8,128)(2,1)} %bitcast.68), kind=kOutput, calls=%fused_computation.2 | convolution fusion | flops 4328521728 | bytes 75497480 | tf_op jit(solution)/shard_map/dot_general | solution.py:67
  311.9 156.1 %all-to-all-done.1 = bf16[8,2,256,1024]{3,0,1,2:T(8,128)(2,1)} async-done(((bf16[8,2,256,1024]{3,0,1,2:T(8,128)(2,1)}), bf16[8,2,256,1024]{3,0,1,2:T(8,128)(2,1)}, u32[]{:S(2)}, u32[]{:S(2)}) %all-to-all-start.1) | async-done | bytes 8388640 | tf_op jit(solution)/shard_map/all_to_all | solution.py:79
  468.0 5.5 %fusion.10 = bf16[16,1024,15]{1,2,0:T(8,128)(2,1)S(1)} fusion(bf16[8,2,16,16,1024]{4,0,1,3,2:T(8,128)(2,1)} %bitcast.13, s32[128,2]{0,1:T(2,128)S(1)} %pad_add_fusion), kind=kOutput, calls=%fused_computation.21 | convolution fusion | flops 126078720 | bytes 8881152 | tf_op jit(solution)/shard_map/gkp,gkct->cpt/dot_general | solution.py:84
  473.6 1.1 copy.38
  (6 shorter events, 0.0 us)
Async XLA Ops:
  15.8 7.1 %copy-start = (bf16[16,128,1024]{2,1,0:T(8,128)(2,1)S(1)}, bf16[16,128,1024]{2,1,0:T(8,128)(2,1)}, u32[]{:S(2)}) copy-start(bf16[16,128,1024]{2,1,0:T(8,128)(2,1)} %copy.50) | copy-start | bytes 12582916
  37.2 6.7 %copy-start.1 = (s32[128]{0:T(128)S(1)}, s32[128]{0:T(128)}, u32[]{:S(2)}) copy-start(s32[128]{0:T(128)} %param.11) | copy-start | bytes 1540
  37.2 189.0 %all-to-all-start = ((bf16[8,2,16,16,1024]{4,0,3,1,2:T(8,128)(2,1)}), bf16[8,2,16,16,1024]{4,0,3,1,2:T(8,128)(2,1)}, u32[]{:S(2)}, u32[]{:S(2)}) async-start(bf16[8,2,16,16,1024]{4,0,3,1,2:T(8,128)(2,1)} %copy.30), calls=%async_computation | async-start | bytes 16777216 | tf_op jit(solution)/shard_map/all_to_all | solution.py:61
  280.8 187.2 %all-to-all-start.1 = ((bf16[8,2,256,1024]{3,0,1,2:T(8,128)(2,1)}), bf16[8,2,256,1024]{3,0,1,2:T(8,128)(2,1)}, u32[]{:S(2)}, u32[]{:S(2)}) async-start(bf16[8,2,256,1024]{3,0,1,2:T(8,128)(2,1)} %copy.33), calls=%async_computation.1 | async-start | bytes 16777216 | tf_op jit(solution)/shard_map/all_to_all | solution.py:79
where the time goes:
time: 475 us
  waiting for transfers between devices  338 us (71%)
  matrix products  56.1 us (12%)
  local copies, waits for them, and re-layouts  47 us (10%)
  other arithmetic  21 us (4%)
  starting transfers between devices  11.6 us (2%)
    all_to_all x1, waiting for transfers between devices, body(): lax.all_to_all(stacked, 'row', split_axis=2, concat_axis=2, tiled=True)  182 us
    all_to_all x1, waiting for transfers between devices, body(): lax.all_to_all(outgoing_parts, 'row', split_axis=2, concat_axis=0, tiled=...  156 us
    dot_general x1, matrix products, body(): lax.dot_general(first_arrived, second_arrived, (((1,), (1,)), ((0,), (0,)...  26.2 us
    dot_general x1, matrix products, body(): lax.dot_general(first_arrived, roots, (((2,), (1,)), ((0,), (0,))), prefe...  13.5 us
    all_to_all x1, local copies, waits for them, and re-layouts, body(): lax.all_to_all(stacked, 'row', split_axis=2, concat_axis=2, tiled=True)  11.3 us
    another operation x1, local copies, waits for them, and re-layouts, body(): outgoing_parts = jnp.stack((part_first, part_second), 1)  11.3 us
    dot_general x1, matrix products, root_times_second(): lax.dot_general(second_arrived, roots, (((2,), (2,)), ((0,), (0,))), pref...  10.8 us
  transfers between devices with their start and end apart: 2, of which 2 were waited for; matrix products, arithmetic and copies ran while one was open for 6% of the time, Pallas kernels for 0%

commit v1 on v0

v1 whole, which is shorter than its diff:
```python
import functools

import jax
import jax.numpy as jnp
from jax import lax
from jax.experimental import pallas as pl
from jax.experimental.pallas import tpu as pltpu
from jax.sharding import PartitionSpec as P

BETA = 0.9
F32 = jnp.float32
BF16 = jnp.bfloat16


def panels_of(tiles, grid_len):
    number = jnp.maximum(tiles, 0)
    first = jnp.zeros_like(number)
    for row_index in range(1, grid_len):
        first = first + (number >= row_index * grid_len - row_index * (row_index - 1) // 2)
    start = first * grid_len - first * (first - 1) // 2
    return first, number - start + first, (tiles >= 0).astype(jnp.int32)


def chip_cycle(chips):
    slow = 4 if chips % 4 == 0 else 1
    fast = chips // slow
    walk = [(row, 0) for row in range(slow)]
    for step, row in enumerate(reversed(range(slow))):
        span = range(1, fast) if step % 2 == 0 else reversed(range(1, fast))
        walk += [(row, col) for col in span]
    return [row * fast + col for row, col in walk]


def slab(refs, start, size):
    columns = pl.ds(pl.multiple_of(start, size), size)
    return jnp.concatenate([ref[:, columns] for ref in refs], 0)


def part_kernel(count, first_ref, second_ref, live_ref, own_ref, *refs):
    rest, root_ref, outs = refs[: count - 1], refs[count - 1], refs[count : 2 * count]
    acc, held, own, sems, own_sem = refs[2 * count :]
    slots, tile, _ = root_ref.shape
    depth = held.shape[0]
    grads = [*rest, own]

    def fetch(slot):
        at = lax.rem(slot, depth)
        return pltpu.make_async_copy(root_ref.at[slot], held.at[at], sems.at[at])

    own_copy = pltpu.make_async_copy(own_ref, own, own_sem)
    own_copy.start()
    for slot in range(min(depth, slots)):
        fetch(slot).start()
    acc[...] = jnp.zeros_like(acc)
    own_copy.wait()

    def step(slot, _):
        fetch(slot).wait()
        at = lax.rem(slot, depth)
        first, second = first_ref[slot] * tile, second_ref[slot] * tile

        @pl.when(live_ref[slot] > 0)
        def _():
            part = lax.dot_general(
                slab(grads, second, tile), held[at], (((1,), (1,)), ((), ())), preferred_element_type=F32
            )
            acc[:, pl.ds(pl.multiple_of(first, tile), tile)] += part.astype(BF16).astype(F32)

        @pl.when((live_ref[slot] > 0) & (first != second))
        def _():
            part = lax.dot_general(
                slab(grads, first, tile), held[at], (((1,), (0,)), ((), ())), preferred_element_type=F32
            )
            acc[:, pl.ds(pl.multiple_of(second, tile), tile)] += part.astype(BF16).astype(F32)

        @pl.when(slot + depth < slots)
        def _():
            fetch(slot + depth).start()

        return 0

    lax.fori_loop(0, slots, step, 0)
    at = 0
    for out in outs:
        out[...] = acc[at : at + out.shape[0], :].astype(BF16)
        at += out.shape[0]


SMEM_SPEC = pl.BlockSpec(memory_space=pltpu.SMEM)
VMEM_SPEC = pl.BlockSpec(memory_space=pltpu.VMEM)
ANY_SPEC = pl.BlockSpec(memory_space=pl.ANY)
HBM_SPEC = pl.BlockSpec(memory_space=pltpu.HBM)


def partial_sums(tables, own, rest, roots):
    slots, tile, _ = roots.shape
    order = own.shape[1]
    kinds = [*rest, own]
    rows = sum(g.shape[0] for g in kinds)
    depth = 2
    return pl.pallas_call(
        functools.partial(part_kernel, len(kinds)),
        out_shape=[jax.ShapeDtypeStruct(g.shape, BF16) for g in kinds],
        in_specs=[SMEM_SPEC] * 3 + [HBM_SPEC] + [VMEM_SPEC] * len(rest) + [ANY_SPEC],
        out_specs=[VMEM_SPEC] * len(kinds),
        scratch_shapes=[
            pltpu.VMEM((rows, order), F32),
            pltpu.VMEM((depth, tile, tile), BF16),
            pltpu.VMEM(own.shape, BF16),
            pltpu.SemaphoreType.DMA((depth,)),
            pltpu.SemaphoreType.DMA,
        ],
        compiler_params=pltpu.CompilerParams(vmem_limit_bytes=34 << 20),
        cost_estimate=pl.CostEstimate(
            flops=slots * 4 * rows * tile * tile, bytes_accessed=2 * slots * tile * tile, transcendentals=0
        ),
    )(*tables, own, *rest, roots)


def stat_kernel(count, base, length, first_ref, second_ref, live_ref, own_ref, *refs):
    rest, stat_ref = refs[: count - 1], refs[count - 1]
    out_ref, taken, made, own, in_sems, out_sems, own_sem = refs[-7:]
    depth, height, tile = taken.shape
    cut = tile // height
    total = length * cut
    grads = [*rest, own]

    def piece(ref, i):
        return ref.at[base + i // cut, pl.ds(pl.multiple_of(lax.rem(i, cut) * height, height), height), :]

    def fetch(i):
        at = lax.rem(i, depth)
        return pltpu.make_async_copy(piece(stat_ref, i), taken.at[at], in_sems.at[at])

    def store(i):
        at = lax.rem(i, depth)
        return pltpu.make_async_copy(made.at[at], piece(out_ref, i), out_sems.at[at])

    own_copy = pltpu.make_async_copy(own_ref, own, own_sem)
    own_copy.start()
    for i in range(min(depth, total)):
        fetch(i).start()
    own_copy.wait()

    def step(i, _):
        at = lax.rem(i, depth)
        slot = base + i // cut
        fetch(i).wait()

        @pl.when(i >= depth)
        def _():
            store(i - depth).wait()

        @pl.when(live_ref[slot] > 0)
        def _():
            left = slab(grads, first_ref[slot] * tile + lax.rem(i, cut) * height, height)
            right = slab(grads, second_ref[slot] * tile, tile)
            product = lax.dot_general(left, right, (((0,), (0,)), ((), ())), preferred_element_type=F32)
            made[at] = BETA * taken[at] + (1.0 - BETA) * product

        @pl.when(live_ref[slot] <= 0)
        def _():
            made[at] = taken[at]

        store(i).start()

        @pl.when(i + depth < total)
        def _():
            fetch(i + depth).start()

        return 0

    lax.fori_loop(0, total, step, 0)
    for i in range(max(total - depth, 0), total):
        store(i).wait()


def update_stats(tables, own, rest, stats, base, length, done):
    slots, tile, _ = stats.shape
    rows = own.shape[0] + sum(g.shape[0] for g in rest)
    depth, height = 4, tile // 4
    operands = [*tables, own, *rest, stats]
    in_specs = [SMEM_SPEC] * 3 + [HBM_SPEC] + [VMEM_SPEC] * len(rest) + [ANY_SPEC]
    aliases = {}
    if done is not None:
        aliases = {len(operands): 0}
        operands.append(done)
        in_specs.append(ANY_SPEC)
    return pl.pallas_call(
        functools.partial(stat_kernel, 1 + len(rest), base, length),
        out_shape=jax.ShapeDtypeStruct(stats.shape, F32),
        in_specs=in_specs,
        out_specs=ANY_SPEC,
        scratch_shapes=[
            pltpu.VMEM((depth, height, tile), F32),
            pltpu.VMEM((depth, height, tile), F32),
            pltpu.VMEM(own.shape, BF16),
            pltpu.SemaphoreType.DMA((depth,)),
            pltpu.SemaphoreType.DMA((depth,)),
            pltpu.SemaphoreType.DMA,
        ],
        input_output_aliases=aliases,
        compiler_params=pltpu.CompilerParams(vmem_limit_bytes=34 << 20),
        cost_estimate=pl.CostEstimate(
            flops=length * 2 * rows * tile * tile, bytes_accessed=8 * length * tile * tile, transcendentals=0
        ),
    )(*operands)


def body(grad, stats, roots, tile_slot):
    width, order = grad.shape
    slots, tile, _ = stats.shape
    devices = lax.axis_size("row")
    chips, half = devices // 2, width // 2
    mine = lax.dynamic_slice_in_dim(tile_slot, lax.axis_index("row") * slots, slots)
    tables = panels_of(mine, order // tile)

    if half % 8:
        everything = lax.all_gather(grad, "row", axis=0, tiled=True)
        (sums,) = partial_sums(tables, everything, [], roots)
        new_stats = update_stats(tables, everything, [], stats, 0, slots, None)
        total = lax.psum_scatter(sums.astype(F32), "row", scatter_dimension=0, tiled=True)
        return new_stats, total.astype(BF16)

    walk = chip_cycle(chips)
    forward, backward = [], []
    for here, there in zip(walk, walk[1:] + walk[:1]):
        for core in range(2):
            forward.append((2 * here + core, 2 * there + core))
            backward.append((2 * there + core, 2 * here + core))
    ahead = lambda v: lax.ppermute(v, "row", forward)
    back = lambda v: lax.ppermute(v, "row", backward)
    swap = lambda v: lax.ppermute(v, "row", [(i, i ^ 1) for i in range(devices)])

    reach = (chips - 1) // 2
    chunk = {0: grad}
    for step in range(1, reach + 1):
        chunk[-step], chunk[step] = ahead(chunk[1 - step]), back(chunk[step - 1])
        if step == 1:
            chunk[-1], tables = lax.optimization_barrier((chunk[-1], tables))
    chunk["low"], chunk["high"] = ahead(chunk[-reach][:half]), back(chunk[reach][half:])
    names = ["low", "high"]
    for step in range(reach, 0, -1):
        names += [-step, step]
    rest = [swap(chunk[k]) for k in [*names, 0]] + [chunk[k] for k in names]
    outs = partial_sums(tables, grad, rest, roots)
    names.append(0)
    other, own = dict(zip(names, outs)), dict(zip(names, outs[len(names) :]))

    here = lambda k: own[k].astype(F32) + swap(other[k]).astype(F32)
    sent = here("low").astype(BF16), here("high").astype(BF16)
    shares = [slots * part // 8 for part in (0, 1, 3, 6, 8)] if reach == 3 else [0] * (reach + 1) + [slots]
    done = None
    for step in range(reach, -1, -1):
        low, high = back(sent[0]), ahead(sent[1])
        base, stop = shares[reach - step : reach - step + 2]
        if stop > base:
            now = lax.optimization_barrier((*tables, *sent))[: len(tables)]
            done = update_stats(now, grad, rest, stats, base, stop - base, done)
            low, high, done = lax.optimization_barrier((low, high, done))
        low, high = low.astype(F32), high.astype(F32)
        if step == reach:
            low = jnp.pad(low, ((0, width - half), (0, 0)))
            high = jnp.pad(high, ((half, 0), (0, 0)))
        if step:
            sent = (here(-step) + low).astype(BF16), (here(step) + high).astype(BF16)
    return done, (here(0) + low + high).astype(BF16)


def solution(mesh):
    placed = (
        P(("groups", "row"), None),
        P(("groups", "row"), None, None),
        P(("groups", "row"), None, None),
        P(),
    )
    return jax.shard_map(
        body,
        mesh=mesh,
        in_specs=placed,
        out_specs=(P(("groups", "row"), None, None), P(("groups", "row"), None)),
        check_vma=False,
    )
```

time: 475 us -> 123 us (0.26)
  the two profiles are of different devices: /device:TPU:11 before, /device:TPU:0 now
where the time goes in v1:
time: 123 us
  waiting for transfers between devices  49.9 us (41%)
  Pallas kernels  46.2 us (38%)
  starting transfers between devices  21.4 us (17%)
  other arithmetic  3.69 us (3%)
    ppermute x8, waiting for transfers between devices, body(): back = lambda v: lax.ppermute(v, 'row', backward)  39.4 us
    pallas_call x4, Pallas kernels, update_stats(): pl.pallas_call(functools.partial(stat_kernel, 1 + len(rest), base, length...  31.5 us
    pallas_call x1, Pallas kernels, partial_sums(): pl.pallas_call(functools.partial(part_kernel, len(kinds)), out_shape=[jax...  14.7 us
    ppermute x8, starting transfers between devices, body(): back = lambda v: lax.ppermute(v, 'row', backward)  13.2 us
    ppermute x8, waiting for transfers between devices, body(): ahead = lambda v: lax.ppermute(v, 'row', forward)  8.31 us
    ppermute x8, starting transfers between devices, body(): ahead = lambda v: lax.ppermute(v, 'row', forward)  4.66 us
    ppermute x18, starting transfers between devices, body(): lax.ppermute(v, 'row', [(i, i ^ 1) for i in range(devices)])  3.52 us
  transfers between devices with their start and end apart: 34, of which 16 were waited for; matrix products, arithmetic and copies ran while one was open for 2% of the time, Pallas kernels for 26%

profile of v1, /device:TPU:0, one launch (start us, length us, event | category | flops | bytes accessed | tf_op | source)
XLA Modules:
  0.0 123.0 jit_solution(13274157071715499114)
XLA Ops:
  0.6 3.0 %collective-permute-start.5 = (bf16[16,15360]{1,0:T(8,128)(2,1)}, bf16[16,15360]{1,0:T(8,128)(2,1)S(1)}, u32[]{:S(2)}, u32[]{:S(2)}) collective-permute-start(bf16[16,15360]{1,0:T(8,128)(2,1)} %own_ref.9), channel_id=1, source_target_pairs={{4,0},{5,1},{8,4},{9,5},{12,8},{13,9},{14,12},{15,13},{10,14},{11,... | collective-permute-start | bytes 1474568 | tf_op jit(solution)/shard_map/ppermute | solution.py:232
  3.8 11.4 %collective-permute-done.5.refs_16_ = bf16[16,15360]{1,0:T(8,128)(2,1)S(1)} collective-permute-done((bf16[16,15360]{1,0:T(8,128)(2,1)}, bf16[16,15360]{1,0:T(8,128)(2,1)S(1)}, u32[]{:S(2)}, u32[]{:S(2)}) %collective-permute-start.5) | collective-permute-done | bytes 491552 | tf_op jit(solution)/shard_map/ppermute | solution.py:232
  15.1 1.7 %collective-permute-start.6 = (bf16[16,15360]{1,0:T(8,128)(2,1)S(1)}, bf16[16,15360]{1,0:T(8,128)(2,1)S(1)}, u32[]{:S(2)}, u32[]{:S(2)}) collective-permute-start(bf16[16,15360]{1,0:T(8,128)(2,1)S(1)} %collective-permute-done.5.refs_16_), channel_id=1, source_target_pairs={{4,0},{5,1},{8,4},{9,5},{12,8},{13,9},{14,12},{15,13},{10,14},{11,... | collective-permute-start | bytes 1474568 | tf_op jit(solution)/shard_map/ppermute | solution.py:232
  16.8 0.7 compare_convert_fusion.live_ref
  17.5 0.8 subtract_add_fusion
  18.3 0.4 collective-permute-start.1
  18.7 8.8 %collective-permute-done.6.refs_14_ = bf16[16,15360]{1,0:T(8,128)(2,1)S(1)} collective-permute-done((bf16[16,15360]{1,0:T(8,128)(2,1)S(1)}, bf16[16,15360]{1,0:T(8,128)(2,1)S(1)}, u32[]{:S(2)}, u32[]{:S(2)}) %collective-permute-start.6) | collective-permute-done | bytes 491552 | tf_op jit(solution)/shard_map/ppermute | solution.py:232
  27.5 1.3 %collective-permute-start.7 = (bf16[16,15360]{1,0:T(8,128)(2,1)S(1)}, bf16[16,15360]{1,0:T(8,128)(2,1)S(1)}, u32[]{:S(2)}, u32[]{:S(2)}) collective-permute-start(bf16[16,15360]{1,0:T(8,128)(2,1)S(1)} %collective-permute-done.6.refs_14_), channel_id=1, source_target_pairs={{4,0},{5,1},{8,4},{9,5},{12,8},{13,9},{14,12},{15,13},{10,14},{11,... | collective-permute-start | bytes 1474568 | tf_op jit(solution)/shard_map/ppermute | solution.py:232
  28.9 1.3 %collective-permute-done.1.refs_13_ = bf16[16,15360]{1,0:T(8,128)(2,1)S(1)} collective-permute-done((bf16[16,15360]{1,0:T(8,128)(2,1)S(1)}, bf16[16,15360]{1,0:T(8,128)(2,1)S(1)}, u32[]{:S(2)}, u32[]{:S(2)}) %collective-permute-start.1) | collective-permute-done | bytes 491552 | tf_op jit(solution)/shard_map/ppermute | solution.py:231
  30.1 0.7 collective-permute-start.2
  30.8 0.5 collective-permute-start.15
  31.4 7.7 %collective-permute-done.7.refs_12_ = bf16[16,15360]{1,0:T(8,128)(2,1)S(1)} collective-permute-done((bf16[16,15360]{1,0:T(8,128)(2,1)S(1)}, bf16[16,15360]{1,0:T(8,128)(2,1)S(1)}, u32[]{:S(2)}, u32[]{:S(2)}) %collective-permute-start.7) | collective-permute-done | bytes 491552 | tf_op jit(solution)/shard_map/ppermute | solution.py:232
  39.1 2.0 %collective-permute-done.2.refs_11_ = bf16[16,15360]{1,0:T(8,128)(2,1)S(1)} collective-permute-done((bf16[16,15360]{1,0:T(8,128)(2,1)S(1)}, bf16[16,15360]{1,0:T(8,128)(2,1)S(1)}, u32[]{:S(2)}, u32[]{:S(2)}) %collective-permute-start.2) | collective-permute-done | bytes 491552 | tf_op jit(solution)/shard_map/ppermute | solution.py:231
  41.1 1.6 %collective-permute-start.8 = (bf16[8,15360]{1,0:T(8,128)(2,1)S(1)}, bf16[8,15360]{1,0:T(8,128)(2,1)S(1)}, u32[]{:S(2)}, u32[]{:S(2)}) collective-permute-start(bf16[8,15360]{1,0:T(8,128)(2,1)S(1)} %slice.9), channel_id=1, source_target_pairs={{4,0},{5,1},{8,4},{9,5},{12,8},{13,9},{14,12},{15,13},{10,14},{11,... | collective-permute-start | bytes 737288 | tf_op jit(solution)/shard_map/ppermute | solution.py:232
  42.7 0.5 collective-permute-start.3
  43.2 0.5 collective-permute-start.10
  43.7 5.8 %collective-permute-done.8.refs_10_ = bf16[8,15360]{1,0:T(8,128)(2,1)S(1)} collective-permute-done((bf16[8,15360]{1,0:T(8,128)(2,1)S(1)}, bf16[8,15360]{1,0:T(8,128)(2,1)S(1)}, u32[]{:S(2)}, u32[]{:S(2)}) %collective-permute-start.8) | collective-permute-done | bytes 245792 | tf_op jit(solution)/shard_map/ppermute | solution.py:232
  49.5 1.3 %collective-permute-done.3.refs_9_ = bf16[8,15360]{1,0:T(8,128)(2,1)S(1)} collective-permute-done((bf16[8,15360]{1,0:T(8,128)(2,1)S(1)}, bf16[8,15360]{1,0:T(8,128)(2,1)S(1)}, u32[]{:S(2)}, u32[]{:S(2)}) %collective-permute-start.3) | collective-permute-done | bytes 245792 | tf_op jit(solution)/shard_map/ppermute | solution.py:231
  50.8 0.2 collective-permute-done.9.refs_1_
  51.0 1.3 %collective-permute-done.4.refs_0_ = bf16[8,15360]{1,0:T(8,128)(2,1)S(1)} collective-permute-done((bf16[8,15360]{1,0:T(8,128)(2,1)S(1)}, bf16[8,15360]{1,0:T(8,128)(2,1)S(1)}, u32[]{:S(2)}, u32[]{:S(2)}) %collective-permute-start.4) | collective-permute-done | bytes 245792 | tf_op jit(solution)/shard_map/ppermute | solution.py:233
  52.3 1.0 copy-done
  53.3 14.7 %shard_map.59 = (bf16[8,15360]{1,0:T(8,128)(2,1)S(1)}, bf16[8,15360]{1,0:T(8,128)(2,1)S(1)}, bf16[16,15360]{1,0:T(8,128)(2,1)S(1)}, bf16[16,15360]{1,0:T(8,128)(...) custom-call(s32[8]{0:T(128)S(1)} %get-tuple-element.85.first_ref, ...), custom_call_target="tpu_custom_call" | custom-call | flops 8589934592 | bytes 16777216 | tf_op jit(solution)/shard_map/pallas_call | solution.py:101
  68.1 1.0 collective-permute-start.20
  69.1 0.4 collective-permute-start.19
  69.5 0.6 collective-permute-done.20
  70.2 1.8 %collective-permute-start.21 = (bf16[8,15360]{1,0:T(8,128)(2,1)S(1)}, bf16[8,15360]{1,0:T(8,128)(2,1)S(1)}, u32[]{:S(2)}, u32[]{:S(2)}) collective-permute-start(bf16[8,15360]{1,0:T(8,128)(2,1)S(1)} %add_convert_fusion.8), channel_id=1, source_target_pairs={{4,0},{5,1},{8,4},{9,5},{12,8},{13,9},{14,12},{15,13},{10,14},{11,... | collective-permute-start | bytes 737288 | tf_op jit(solution)/shard_map/ppermute | solution.py:232
  72.1 0.3 collective-permute-start.23
  72.4 4.7 %shard_map.60.refs_18_ = f32[8,1024,1024]{2,1,0:T(8,128)} custom-call(s32[8]{0:T(128)S(1)} %get-tuple-element.85.first_ref, s32[8]{0:T(128)S(1)} %get-tuple-element.86.second_ref, s32[8]{0:T(128)S(1)} %compare_convert_fusion.live_ref, bf16[16,15360]{1,0:T(8,128)(2,1)S(1)} %copy-done, bf16[8,15360]{1,0:T(8,128)(2,1)S(1)} %collective-permute-done.4.refs_0_, ...), custom_call_target="tpu_custom_call" | custom-call | flops 536870912 | bytes 8388608 | tf_op jit(solution)/shard_map/pallas_call | solution.py:189
  77.1 1.3 %collective-permute-done.21 = bf16[8,15360]{1,0:T(8,128)(2,1)S(1)} collective-permute-done((bf16[8,15360]{1,0:T(8,128)(2,1)S(1)}, bf16[8,15360]{1,0:T(8,128)(2,1)S(1)}, u32[]{:S(2)}, u32[]{:S(2)}) %collective-permute-start.21) | collective-permute-done | bytes 245792 | tf_op jit(solution)/shard_map/ppermute | solution.py:232
  78.5 1.4 %collective-permute-done.23 = bf16[8,15360]{1,0:T(8,128)(2,1)S(1)} collective-permute-done((bf16[8,15360]{1,0:T(8,128)(2,1)S(1)}, bf16[8,15360]{1,0:T(8,128)(2,1)S(1)}, u32[]{:S(2)}, u32[]{:S(2)}) %collective-permute-start.23) | collective-permute-done | bytes 245792 | tf_op jit(solution)/shard_map/ppermute | solution.py:231
  80.0 1.6 %collective-permute-start.24 = (bf16[16,15360]{1,0:T(8,128)(2,1)S(1)}, bf16[16,15360]{1,0:T(8,128)(2,1)S(1)}, u32[]{:S(2)}, u32[]{:S(2)}) collective-permute-start(bf16[16,15360]{1,0:T(8,128)(2,1)S(1)} %add_convert_fusion.6), channel_id=1, source_target_pairs={{4,0},{5,1},{8,4},{9,5},{12,8},{13,9},{14,12},{15,13},{10,14},{11,... | collective-permute-start | bytes 1474568 | tf_op jit(solution)/shard_map/ppermute | solution.py:232
  81.8 0.5 collective-permute-start.26
  82.3 0.5 collective-permute-start.28
  82.8 8.0 %shard_map.61.refs_18_ = f32[8,1024,1024]{2,1,0:T(8,128)} custom-call(s32[8]{0:T(128)S(1)} %get-tuple-element.85.first_ref, s32[8]{0:T(128)S(1)} %get-tuple-element.86.second_ref, s32[8]{0:T(128)S(1)} %compare_convert_fusion.live_ref, bf16[16,15360]{1,0:T(8,128)(2,1)S(1)} %copy-done, ...), custom_call_target="tpu_custom_call", output_to_operand_aliasing={{}: (22, {})} | custom-call | flops 1073741824 | bytes 16777216 | tf_op jit(solution)/shard_map/pallas_call | solution.py:189
  90.9 1.3 %collective-permute-done.24 = bf16[16,15360]{1,0:T(8,128)(2,1)S(1)} collective-permute-done((bf16[16,15360]{1,0:T(8,128)(2,1)S(1)}, bf16[16,15360]{1,0:T(8,128)(2,1)S(1)}, u32[]{:S(2)}, u32[]{:S(2)}) %collective-permute-start.24) | collective-permute-done | bytes 491552 | tf_op jit(solution)/shard_map/ppermute | solution.py:232
  92.2 1.5 %collective-permute-done.26 = bf16[16,15360]{1,0:T(8,128)(2,1)S(1)} collective-permute-done((bf16[16,15360]{1,0:T(8,128)(2,1)S(1)}, bf16[16,15360]{1,0:T(8,128)(2,1)S(1)}, u32[]{:S(2)}, u32[]{:S(2)}) %collective-permute-start.26) | collective-permute-done | bytes 491552 | tf_op jit(solution)/shard_map/ppermute | solution.py:231
  93.7 0.2 add_convert_fusion.4
  93.9 0.9 collective-permute-start.27
  95.1 1.2 collective-permute-start.29
  96.3 0.5 collective-permute-start.31
  96.8 10.7 %shard_map.62.refs_18_ = f32[8,1024,1024]{2,1,0:T(8,128)} custom-call(s32[8]{0:T(128)S(1)} %get-tuple-element.85.first_ref, s32[8]{0:T(128)S(1)} %get-tuple-element.86.second_ref, s32[8]{0:T(128)S(1)} %compare_convert_fusion.live_ref, bf16[16,15360]{1,0:T(8,128)(2,1)S(1)} %copy-done, ...), custom_call_target="tpu_custom_call", output_to_operand_aliasing={{}: (22, {})} | custom-call | flops 1610612736 | bytes 25165824 | tf_op jit(solution)/shard_map/pallas_call | solution.py:189
  107.5 0.2 add_convert_fusion.2
  107.7 1.2 collective-permute-start.30
  109.1 1.0 collective-permute-start.32
  110.1 8.0 %shard_map.63 = f32[8,1024,1024]{2,1,0:T(8,128)} custom-call(s32[8]{0:T(128)S(1)} %get-tuple-element.85.first_ref, s32[8]{0:T(128)S(1)} %get-tuple-element.86.second_ref, s32[8]{0:T(128)S(1)} %compare_convert_fusion.live_ref, bf16[16,15360]{1,0:T(8,128)(2,1)S(1)} %copy-done, ...), custom_call_target="tpu_custom_call", output_to_operand_aliasing={{}: (22, {})} | custom-call | flops 1073741824 | bytes 16777216 | tf_op jit(solution)/shard_map/pallas_call | solution.py:189
  118.1 3.0 %collective-permute-done.30 = bf16[16,15360]{1,0:T(8,128)(2,1)S(1)} collective-permute-done((bf16[16,15360]{1,0:T(8,128)(2,1)S(1)}, bf16[16,15360]{1,0:T(8,128)(2,1)S(1)}, u32[]{:S(2)}, u32[]{:S(2)}) %collective-permute-start.30) | collective-permute-done | bytes 491552 | tf_op jit(solution)/shard_map/ppermute | solution.py:232
  121.2 0.9 collective-permute-done.32
  122.0 1.0 add_convert_fusion
  (40 shorter events, 1.1 us)
Async XLA Ops:
  0.6 14.5 %collective-permute-start.5 = (bf16[16,15360]{1,0:T(8,128)(2,1)}, bf16[16,15360]{1,0:T(8,128)(2,1)S(1)}, u32[]{:S(2)}, u32[]{:S(2)}) collective-permute-start(bf16[16,15360]{1,0:T(8,128)(2,1)} %own_ref.9), channel_id=1, source_target_pairs={{4,0},{5,1},{8,4},{9,5},{12,8},{13,9},{14,12},{15,13},{10,14},{11,... | collective-permute-start | bytes 1474568 | tf_op jit(solution)/shard_map/ppermute | solution.py:232
  3.6 14.7 %collective-permute-start = (bf16[16,15360]{1,0:T(8,128)(2,1)}, bf16[16,15360]{1,0:T(8,128)(2,1)S(1)}, u32[]{:S(2)}, u32[]{:S(2)}) collective-permute-start(bf16[16,15360]{1,0:T(8,128)(2,1)} %own_ref.9), channel_id=1, source_target_pairs={{0,4},{1,5},{4,8},{5,9},{8,12},{9,13},{12,14},{13,15},{14,10},{15,... | collective-permute-start | bytes 1474568 | tf_op jit(solution)/shard_map/ppermute | solution.py:231
  15.1 12.4 %collective-permute-start.6 = (bf16[16,15360]{1,0:T(8,128)(2,1)S(1)}, bf16[16,15360]{1,0:T(8,128)(2,1)S(1)}, u32[]{:S(2)}, u32[]{:S(2)}) collective-permute-start(bf16[16,15360]{1,0:T(8,128)(2,1)S(1)} %collective-permute-done.5.refs_16_), channel_id=1, source_target_pairs={{4,0},{5,1},{8,4},{9,5},{12,8},{13,9},{14,12},{15,13},{10,14},{11,... | collective-permute-start | bytes 1474568 | tf_op jit(solution)/shard_map/ppermute | solution.py:232
  18.3 11.9 %collective-permute-start.1 = (bf16[16,15360]{1,0:T(8,128)(2,1)S(1)}, bf16[16,15360]{1,0:T(8,128)(2,1)S(1)}, u32[]{:S(2)}, u32[]{:S(2)}) collective-permute-start(bf16[16,15360]{1,0:T(8,128)(2,1)S(1)} %collective-permute-done.refs_15_), channel_id=1, source_target_pairs={{0,4},{1,5},{4,8},{5,9},{8,12},{9,13},{12,14},{13,15},{14,10},{15,... | collective-permute-start | bytes 1474568 | tf_op jit(solution)/shard_map/ppermute | solution.py:231
  27.5 11.5 %collective-permute-start.7 = (bf16[16,15360]{1,0:T(8,128)(2,1)S(1)}, bf16[16,15360]{1,0:T(8,128)(2,1)S(1)}, u32[]{:S(2)}, u32[]{:S(2)}) collective-permute-start(bf16[16,15360]{1,0:T(8,128)(2,1)S(1)} %collective-permute-done.6.refs_14_), channel_id=1, source_target_pairs={{4,0},{5,1},{8,4},{9,5},{12,8},{13,9},{14,12},{15,13},{10,14},{11,... | collective-permute-start | bytes 1474568 | tf_op jit(solution)/shard_map/ppermute | solution.py:232
  30.1 10.9 %collective-permute-start.2 = (bf16[16,15360]{1,0:T(8,128)(2,1)S(1)}, bf16[16,15360]{1,0:T(8,128)(2,1)S(1)}, u32[]{:S(2)}, u32[]{:S(2)}) collective-permute-start(bf16[16,15360]{1,0:T(8,128)(2,1)S(1)} %collective-permute-done.1.refs_13_), channel_id=1, source_target_pairs={{0,4},{1,5},{4,8},{5,9},{8,12},{9,13},{12,14},{13,15},{14,10},{15,... | collective-permute-start | bytes 1474568 | tf_op jit(solution)/shard_map/ppermute | solution.py:231
  30.8 10.2 %collective-permute-start.16 = (bf16[16,15360]{1,0:T(8,128)(2,1)}, bf16[16,15360]{1,0:T(8,128)(2,1)S(1)}, u32[]{:S(2)}, u32[]{:S(2)}) collective-permute-start(bf16[16,15360]{1,0:T(8,128)(2,1)} %own_ref.9), channel_id=1, source_target_pairs={{0,1},{1,0},{2,3},{3,2},{4,5},{5,4},{6,7},{7,6},{8,9},{9,8},{10,11... | collective-permute-start | bytes 1474568 | tf_op jit(solution)/shard_map/ppermute | solution.py:233
  30.8 11.9 %collective-permute-start.15 = (bf16[16,15360]{1,0:T(8,128)(2,1)S(1)}, bf16[16,15360]{1,0:T(8,128)(2,1)S(1)}, u32[]{:S(2)}, u32[]{:S(2)}) collective-permute-start(bf16[16,15360]{1,0:T(8,128)(2,1)S(1)} %collective-permute-done.5.refs_16_), channel_id=1, source_target_pairs={{0,1},{1,0},{2,3},{3,2},{4,5},{5,4},{6,7},{7,6},{8,9},{9,8},{10,11... | collective-permute-start | bytes 1474568 | tf_op jit(solution)/shard_map/ppermute | solution.py:233
  31.4 11.8 %collective-permute-start.14 = (bf16[16,15360]{1,0:T(8,128)(2,1)S(1)}, bf16[16,15360]{1,0:T(8,128)(2,1)S(1)}, u32[]{:S(2)}, u32[]{:S(2)}) collective-permute-start(bf16[16,15360]{1,0:T(8,128)(2,1)S(1)} %collective-permute-done.refs_15_), channel_id=1, source_target_pairs={{0,1},{1,0},{2,3},{3,2},{4,5},{5,4},{6,7},{7,6},{8,9},{9,8},{10,11... | collective-permute-start | bytes 1474568 | tf_op jit(solution)/shard_map/ppermute | solution.py:233
  39.0 4.1 %collective-permute-start.13 = (bf16[16,15360]{1,0:T(8,128)(2,1)S(1)}, bf16[16,15360]{1,0:T(8,128)(2,1)S(1)}, u32[]{:S(2)}, u32[]{:S(2)}) collective-permute-start(bf16[16,15360]{1,0:T(8,128)(2,1)S(1)} %collective-permute-done.6.refs_14_), channel_id=1, source_target_pairs={{0,1},{1,0},{2,3},{3,2},{4,5},{5,4},{6,7},{7,6},{8,9},{9,8},{10,11... | collective-permute-start | bytes 1474568 | tf_op jit(solution)/shard_map/ppermute | solution.py:233
  41.0 9.8 %collective-permute-start.12 = (bf16[16,15360]{1,0:T(8,128)(2,1)S(1)}, bf16[16,15360]{1,0:T(8,128)(2,1)S(1)}, u32[]{:S(2)}, u32[]{:S(2)}) collective-permute-start(bf16[16,15360]{1,0:T(8,128)(2,1)S(1)} %collective-permute-done.1.refs_13_), channel_id=1, source_target_pairs={{0,1},{1,0},{2,3},{3,2},{4,5},{5,4},{6,7},{7,6},{8,9},{9,8},{10,11... | collective-permute-start | bytes 1474568 | tf_op jit(solution)/shard_map/ppermute | solution.py:233
  41.1 8.4 %collective-permute-start.8 = (bf16[8,15360]{1,0:T(8,128)(2,1)S(1)}, bf16[8,15360]{1,0:T(8,128)(2,1)S(1)}, u32[]{:S(2)}, u32[]{:S(2)}) collective-permute-start(bf16[8,15360]{1,0:T(8,128)(2,1)S(1)} %slice.9), channel_id=1, source_target_pairs={{4,0},{5,1},{8,4},{9,5},{12,8},{13,9},{14,12},{15,13},{10,14},{11,... | collective-permute-start | bytes 737288 | tf_op jit(solution)/shard_map/ppermute | solution.py:232
  42.7 8.1 %collective-permute-start.3 = (bf16[8,15360]{1,0:T(8,128)(2,1)S(1)}, bf16[8,15360]{1,0:T(8,128)(2,1)S(1)}, u32[]{:S(2)}, u32[]{:S(2)}) collective-permute-start(bf16[8,15360]{1,0:T(8,128)(2,1)S(1)} %slice.8), channel_id=1, source_target_pairs={{0,4},{1,5},{4,8},{5,9},{8,12},{9,13},{12,14},{13,15},{14,10},{15,... | collective-permute-start | bytes 737288 | tf_op jit(solution)/shard_map/ppermute | solution.py:231
  43.2 7.8 %collective-permute-start.11 = (bf16[16,15360]{1,0:T(8,128)(2,1)S(1)}, bf16[16,15360]{1,0:T(8,128)(2,1)S(1)}, u32[]{:S(2)}, u32[]{:S(2)}) collective-permute-start(bf16[16,15360]{1,0:T(8,128)(2,1)S(1)} %collective-permute-done.7.refs_12_), channel_id=1, source_target_pairs={{0,1},{1,0},{2,3},{3,2},{4,5},{5,4},{6,7},{7,6},{8,9},{9,8},{10,11... | collective-permute-start | bytes 1474568 | tf_op jit(solution)/shard_map/ppermute | solution.py:233
  43.2 9.1 %collective-permute-start.10 = (bf16[16,15360]{1,0:T(8,128)(2,1)S(1)}, bf16[16,15360]{1,0:T(8,128)(2,1)S(1)}, u32[]{:S(2)}, u32[]{:S(2)}) collective-permute-start(bf16[16,15360]{1,0:T(8,128)(2,1)S(1)} %collective-permute-done.2.refs_11_), channel_id=1, source_target_pairs={{0,1},{1,0},{2,3},{3,2},{4,5},{5,4},{6,7},{7,6},{8,9},{9,8},{10,11... | collective-permute-start | bytes 1474568 | tf_op jit(solution)/shard_map/ppermute | solution.py:233
  49.5 1.5 %collective-permute-start.9 = (bf16[8,15360]{1,0:T(8,128)(2,1)S(1)}, bf16[8,15360]{1,0:T(8,128)(2,1)S(1)}, u32[]{:S(2)}, u32[]{:S(2)}) collective-permute-start(bf16[8,15360]{1,0:T(8,128)(2,1)S(1)} %collective-permute-done.8.refs_10_), channel_id=1, source_target_pairs={{0,1},{1,0},{2,3},{3,2},{4,5},{5,4},{6,7},{7,6},{8,9},{9,8},{10,11... | collective-permute-start | bytes 737288 | tf_op jit(solution)/shard_map/ppermute | solution.py:233
  50.8 1.5 %collective-permute-start.4 = (bf16[8,15360]{1,0:T(8,128)(2,1)S(1)}, bf16[8,15360]{1,0:T(8,128)(2,1)S(1)}, u32[]{:S(2)}, u32[]{:S(2)}) collective-permute-start(bf16[8,15360]{1,0:T(8,128)(2,1)S(1)} %collective-permute-done.3.refs_9_), channel_id=1, source_target_pairs={{0,1},{1,0},{2,3},{3,2},{4,5},{5,4},{6,7},{7,6},{8,9},{9,8},{10,11... | collective-permute-start | bytes 737288 | tf_op jit(solution)/shard_map/ppermute | solution.py:233
  52.3 1.0 copy-start
  68.1 2.1 %collective-permute-start.20 = (bf16[8,15360]{1,0:T(8,128)(2,1)S(1)}, bf16[8,15360]{1,0:T(8,128)(2,1)S(1)}, u32[]{:S(2)}, u32[]{:S(2)}) collective-permute-start(bf16[8,15360]{1,0:T(8,128)(2,1)S(1)} %get-tuple-element.59), channel_id=1, source_target_pairs={{0,1},{1,0},{2,3},{3,2},{4,5},{5,4},{6,7},{7,6},{8,9},{9,8},{10,11... | collective-permute-start | bytes 737288 | tf_op jit(solution)/shard_map/ppermute | solution.py:233
  69.0 3.0 %collective-permute-start.22 = (bf16[8,15360]{1,0:T(8,128)(2,1)S(1)}, bf16[8,15360]{1,0:T(8,128)(2,1)S(1)}, u32[]{:S(2)}, u32[]{:S(2)}) collective-permute-start(bf16[8,15360]{1,0:T(8,128)(2,1)S(1)} %get-tuple-element.61), channel_id=1, source_target_pairs={{0,1},{1,0},{2,3},{3,2},{4,5},{5,4},{6,7},{7,6},{8,9},{9,8},{10,11... | collective-permute-start | bytes 737288 | tf_op jit(solution)/shard_map/ppermute | solution.py:233
  69.1 10.8 %collective-permute-start.19 = (bf16[16,15360]{1,0:T(8,128)(2,1)S(1)}, bf16[16,15360]{1,0:T(8,128)(2,1)S(1)}, u32[]{:S(2)}, u32[]{:S(2)}) collective-permute-start(bf16[16,15360]{1,0:T(8,128)(2,1)S(1)} %get-tuple-element.57), channel_id=1, source_target_pairs={{0,1},{1,0},{2,3},{3,2},{4,5},{5,4},{6,7},{7,6},{8,9},{9,8},{10,11... | collective-permute-start | bytes 1474568 | tf_op jit(solution)/shard_map/ppermute | solution.py:233
  70.2 8.3 %collective-permute-start.21 = (bf16[8,15360]{1,0:T(8,128)(2,1)S(1)}, bf16[8,15360]{1,0:T(8,128)(2,1)S(1)}, u32[]{:S(2)}, u32[]{:S(2)}) collective-permute-start(bf16[8,15360]{1,0:T(8,128)(2,1)S(1)} %add_convert_fusion.8), channel_id=1, source_target_pairs={{4,0},{5,1},{8,4},{9,5},{12,8},{13,9},{14,12},{15,13},{10,14},{11,... | collective-permute-start | bytes 737288 | tf_op jit(solution)/shard_map/ppermute | solution.py:232
  72.1 7.8 %collective-permute-start.23 = (bf16[8,15360]{1,0:T(8,128)(2,1)S(1)}, bf16[8,15360]{1,0:T(8,128)(2,1)S(1)}, u32[]{:S(2)}, u32[]{:S(2)}) collective-permute-start(bf16[8,15360]{1,0:T(8,128)(2,1)S(1)} %add_convert_fusion.7), channel_id=1, source_target_pairs={{0,4},{1,5},{4,8},{5,9},{8,12},{9,13},{12,14},{13,15},{14,10},{15,... | collective-permute-start | bytes 737288 | tf_op jit(solution)/shard_map/ppermute | solution.py:231
  72.4 9.3 %collective-permute-start.25 = (bf16[16,15360]{1,0:T(8,128)(2,1)S(1)}, bf16[16,15360]{1,0:T(8,128)(2,1)S(1)}, u32[]{:S(2)}, u32[]{:S(2)}) collective-permute-start(bf16[16,15360]{1,0:T(8,128)(2,1)S(1)} %get-tuple-element.67), channel_id=1, source_target_pairs={{0,1},{1,0},{2,3},{3,2},{4,5},{5,4},{6,7},{7,6},{8,9},{9,8},{10,11... | collective-permute-start | bytes 1474568 | tf_op jit(solution)/shard_map/ppermute | solution.py:233
  80.0 12.2 %collective-permute-start.24 = (bf16[16,15360]{1,0:T(8,128)(2,1)S(1)}, bf16[16,15360]{1,0:T(8,128)(2,1)S(1)}, u32[]{:S(2)}, u32[]{:S(2)}) collective-permute-start(bf16[16,15360]{1,0:T(8,128)(2,1)S(1)} %add_convert_fusion.6), channel_id=1, source_target_pairs={{4,0},{5,1},{8,4},{9,5},{12,8},{13,9},{14,12},{15,13},{10,14},{11,... | collective-permute-start | bytes 1474568 | tf_op jit(solution)/shard_map/ppermute | solution.py:232
  81.8 11.9 %collective-permute-start.26 = (bf16[16,15360]{1,0:T(8,128)(2,1)S(1)}, bf16[16,15360]{1,0:T(8,128)(2,1)S(1)}, u32[]{:S(2)}, u32[]{:S(2)}) collective-permute-start(bf16[16,15360]{1,0:T(8,128)(2,1)S(1)} %add_convert_fusion.5), channel_id=1, source_target_pairs={{0,4},{1,5},{4,8},{5,9},{8,12},{9,13},{12,14},{13,15},{14,10},{15,... | collective-permute-start | bytes 1474568 | tf_op jit(solution)/shard_map/ppermute | solution.py:231
  82.3 11.4 %collective-permute-start.18 = (bf16[16,15360]{1,0:T(8,128)(2,1)S(1)}, bf16[16,15360]{1,0:T(8,128)(2,1)S(1)}, u32[]{:S(2)}, u32[]{:S(2)}) collective-permute-start(bf16[16,15360]{1,0:T(8,128)(2,1)S(1)} %get-tuple-element.55), channel_id=1, source_target_pairs={{0,1},{1,0},{2,3},{3,2},{4,5},{5,4},{6,7},{7,6},{8,9},{9,8},{10,11... | collective-permute-start | bytes 1474568 | tf_op jit(solution)/shard_map/ppermute | solution.py:233
  82.3 12.5 %collective-permute-start.28 = (bf16[16,15360]{1,0:T(8,128)(2,1)S(1)}, bf16[16,15360]{1,0:T(8,128)(2,1)S(1)}, u32[]{:S(2)}, u32[]{:S(2)}) collective-permute-start(bf16[16,15360]{1,0:T(8,128)(2,1)S(1)} %get-tuple-element.75), channel_id=1, source_target_pairs={{0,1},{1,0},{2,3},{3,2},{4,5},{5,4},{6,7},{7,6},{8,9},{9,8},{10,11... | collective-permute-start | bytes 1474568 | tf_op jit(solution)/shard_map/ppermute | solution.py:233
  93.9 13.6 %collective-permute-start.27 = (bf16[16,15360]{1,0:T(8,128)(2,1)S(1)}, bf16[16,15360]{1,0:T(8,128)(2,1)S(1)}, u32[]{:S(2)}, u32[]{:S(2)}) collective-permute-start(bf16[16,15360]{1,0:T(8,128)(2,1)S(1)} %add_convert_fusion.4), channel_id=1, source_target_pairs={{4,0},{5,1},{8,4},{9,5},{12,8},{13,9},{14,12},{15,13},{10,14},{11,... | collective-permute-start | bytes 1474568 | tf_op jit(solution)/shard_map/ppermute | solution.py:232
  95.1 12.5 %collective-permute-start.29 = (bf16[16,15360]{1,0:T(8,128)(2,1)S(1)}, bf16[16,15360]{1,0:T(8,128)(2,1)S(1)}, u32[]{:S(2)}, u32[]{:S(2)}) collective-permute-start(bf16[16,15360]{1,0:T(8,128)(2,1)S(1)} %add_convert_fusion.3), channel_id=1, source_target_pairs={{0,4},{1,5},{4,8},{5,9},{8,12},{9,13},{12,14},{13,15},{14,10},{15,... | collective-permute-start | bytes 1474568 | tf_op jit(solution)/shard_map/ppermute | solution.py:231
  96.3 11.3 %collective-permute-start.17 = (bf16[16,15360]{1,0:T(8,128)(2,1)S(1)}, bf16[16,15360]{1,0:T(8,128)(2,1)S(1)}, u32[]{:S(2)}, u32[]{:S(2)}) collective-permute-start(bf16[16,15360]{1,0:T(8,128)(2,1)S(1)} %get-tuple-element.53), channel_id=1, source_target_pairs={{0,1},{1,0},{2,3},{3,2},{4,5},{5,4},{6,7},{7,6},{8,9},{9,8},{10,11... | collective-permute-start | bytes 1474568 | tf_op jit(solution)/shard_map/ppermute | solution.py:233
  96.3 12.7 %collective-permute-start.31 = (bf16[16,15360]{1,0:T(8,128)(2,1)S(1)}, bf16[16,15360]{1,0:T(8,128)(2,1)S(1)}, u32[]{:S(2)}, u32[]{:S(2)}) collective-permute-start(bf16[16,15360]{1,0:T(8,128)(2,1)S(1)} %get-tuple-element.83), channel_id=1, source_target_pairs={{0,1},{1,0},{2,3},{3,2},{4,5},{5,4},{6,7},{7,6},{8,9},{9,8},{10,11... | collective-permute-start | bytes 1474568 | tf_op jit(solution)/shard_map/ppermute | solution.py:233
  107.7 13.4 %collective-permute-start.30 = (bf16[16,15360]{1,0:T(8,128)(2,1)S(1)}, bf16[16,15360]{1,0:T(8,128)(2,1)S(1)}, u32[]{:S(2)}, u32[]{:S(2)}) collective-permute-start(bf16[16,15360]{1,0:T(8,128)(2,1)S(1)} %add_convert_fusion.2), channel_id=1, source_target_pairs={{4,0},{5,1},{8,4},{9,5},{12,8},{13,9},{14,12},{15,13},{10,14},{11,... | collective-permute-start | bytes 1474568 | tf_op jit(solution)/shard_map/ppermute | solution.py:232
  109.1 12.9 %collective-permute-start.32 = (bf16[16,15360]{1,0:T(8,128)(2,1)S(1)}, bf16[16,15360]{1,0:T(8,128)(2,1)S(1)}, u32[]{:S(2)}, u32[]{:S(2)}) collective-permute-start(bf16[16,15360]{1,0:T(8,128)(2,1)S(1)} %add_convert_fusion.1), channel_id=1, source_target_pairs={{0,4},{1,5},{4,8},{5,9},{8,12},{9,13},{12,14},{13,15},{14,10},{15,... | collective-permute-start | bytes 1474568 | tf_op jit(solution)/shard_map/ppermute | solution.py:231
  110.1 11.9 %collective-permute-start.33 = (bf16[16,15360]{1,0:T(8,128)(2,1)S(1)}, bf16[16,15360]{1,0:T(8,128)(2,1)S(1)}, u32[]{:S(2)}, u32[]{:S(2)}) collective-permute-start(bf16[16,15360]{1,0:T(8,128)(2,1)S(1)} %get-tuple-element.91), channel_id=1, source_target_pairs={{0,1},{1,0},{2,3},{3,2},{4,5},{5,4},{6,7},{7,6},{8,9},{9,8},{10,11... | collective-permute-start | bytes 1474568 | tf_op jit(solution)/shard_map/ppermute | solution.py:233

commit v2 on v1

--- a/solution.py
+++ b/solution.py
@@ -36,23 +36,19 @@
     return jnp.concatenate([ref[:, columns] for ref in refs], 0)
 
 
-def part_kernel(count, first_ref, second_ref, live_ref, own_ref, *refs):
-    rest, root_ref, outs = refs[: count - 1], refs[count - 1], refs[count : 2 * count]
-    acc, held, own, sems, own_sem = refs[2 * count :]
+def part_kernel(count, first_ref, second_ref, live_ref, *refs):
+    grads, root_ref, outs = refs[:count], refs[count], refs[count + 1 : -3]
+    acc, held, sems = refs[-3:]
     slots, tile, _ = root_ref.shape
     depth = held.shape[0]
-    grads = [*rest, own]
 
     def fetch(slot):
         at = lax.rem(slot, depth)
         return pltpu.make_async_copy(root_ref.at[slot], held.at[at], sems.at[at])
 
-    own_copy = pltpu.make_async_copy(own_ref, own, own_sem)
-    own_copy.start()
     for slot in range(min(depth, slots)):
         fetch(slot).start()
     acc[...] = jnp.zeros_like(acc)
-    own_copy.wait()
 
     def step(slot, _):
         fetch(slot).wait()
@@ -92,41 +88,39 @@
 HBM_SPEC = pl.BlockSpec(memory_space=pltpu.HBM)
 
 
-def partial_sums(tables, own, rest, roots):
+def partial_sums(tables, grads, heights, roots):
     slots, tile, _ = roots.shape
-    order = own.shape[1]
-    kinds = [*rest, own]
-    rows = sum(g.shape[0] for g in kinds)
+    rows, order = sum(heights), grads[0].shape[1]
     depth = 2
     return pl.pallas_call(
-        functools.partial(part_kernel, len(kinds)),
-        out_shape=[jax.ShapeDtypeStruct(g.shape, BF16) for g in kinds],
-        in_specs=[SMEM_SPEC] * 3 + [HBM_SPEC] + [VMEM_SPEC] * len(rest) + [ANY_SPEC],
-        out_specs=[VMEM_SPEC] * len(kinds),
+        functools.partial(part_kernel, len(grads)),
+        out_shape=[jax.ShapeDtypeStruct((height, order), BF16) for height in heights],
+        in_specs=[SMEM_SPEC] * 3 + [VMEM_SPEC] * len(grads) + [ANY_SPEC],
+        out_specs=[VMEM_SPEC] * len(heights),
         scratch_shapes=[
             pltpu.VMEM((rows, order), F32),
             pltpu.VMEM((depth, tile, tile), BF16),
-            pltpu.VMEM(own.shape, BF16),
             pltpu.SemaphoreType.DMA((depth,)),
-            pltpu.SemaphoreType.DMA,
         ],
         compiler_params=pltpu.CompilerParams(vmem_limit_bytes=34 << 20),
         cost_estimate=pl.CostEstimate(
             flops=slots * 4 * rows * tile * tile, bytes_accessed=2 * slots * tile * tile, transcendentals=0
         ),
-    )(*tables, own, *rest, roots)
-
-
-def stat_kernel(count, base, length, first_ref, second_ref, live_ref, own_ref, *refs):
-    rest, stat_ref = refs[: count - 1], refs[count - 1]
-    out_ref, taken, made, own, in_sems, out_sems, own_sem = refs[-7:]
+    )(*tables, *grads, roots)
+
+
+def stat_kernel(count, base, total, first_ref, second_ref, live_ref, *refs):
+    grads, stat_ref = refs[:count], refs[count]
+    out_ref, taken, made, in_sems, out_sems = refs[-5:]
     depth, height, tile = taken.shape
     cut = tile // height
-    total = length * cut
-    grads = [*rest, own]
+
+    def place(i):
+        return (base + i) // cut, lax.rem(base + i, cut) * height
 
     def piece(ref, i):
-        return ref.at[base + i // cut, pl.ds(pl.multiple_of(lax.rem(i, cut) * height, height), height), :]
+        slot, row = place(i)
+        return ref.at[slot, pl.ds(pl.multiple_of(row, height), height), :]
 
     def fetch(i):
         at = lax.rem(i, depth)
@@ -136,15 +130,12 @@
         at = lax.rem(i, depth)
         return pltpu.make_async_copy(made.at[at], piece(out_ref, i), out_sems.at[at])
 
-    own_copy = pltpu.make_async_copy(own_ref, own, own_sem)
-    own_copy.start()
     for i in range(min(depth, total)):
         fetch(i).start()
-    own_copy.wait()
 
     def step(i, _):
         at = lax.rem(i, depth)
-        slot = base + i // cut
+        slot, row = place(i)
         fetch(i).wait()
 
         @pl.when(i >= depth)
@@ -153,7 +144,7 @@
 
         @pl.when(live_ref[slot] > 0)
         def _():
-            left = slab(grads, first_ref[slot] * tile + lax.rem(i, cut) * height, height)
+            left = slab(grads, first_ref[slot] * tile + row, height)
             right = slab(grads, second_ref[slot] * tile, tile)
             product = lax.dot_general(left, right, (((0,), (0,)), ((), ())), preferred_element_type=F32)
             made[at] = BETA * taken[at] + (1.0 - BETA) * product
@@ -175,34 +166,35 @@
         store(i).wait()
 
 
-def update_stats(tables, own, rest, stats, base, length, done):
+CUT = 4
+
+
+def update_stats(tables, grads, stats, base, length, done):
     slots, tile, _ = stats.shape
-    rows = own.shape[0] + sum(g.shape[0] for g in rest)
-    depth, height = 4, tile // 4
-    operands = [*tables, own, *rest, stats]
-    in_specs = [SMEM_SPEC] * 3 + [HBM_SPEC] + [VMEM_SPEC] * len(rest) + [ANY_SPEC]
+    rows = sum(g.shape[0] for g in grads)
+    depth, height = 4, tile // CUT
+    operands = [*tables, *grads, stats]
+    in_specs = [SMEM_SPEC] * 3 + [VMEM_SPEC] * len(grads) + [ANY_SPEC]
     aliases = {}
     if done is not None:
         aliases = {len(operands): 0}
         operands.append(done)
         in_specs.append(ANY_SPEC)
     return pl.pallas_call(
-        functools.partial(stat_kernel, 1 + len(rest), base, length),
+        functools.partial(stat_kernel, len(grads), base, length),
         out_shape=jax.ShapeDtypeStruct(stats.shape, F32),
         in_specs=in_specs,
         out_specs=ANY_SPEC,
         scratch_shapes=[
             pltpu.VMEM((depth, height, tile), F32),
             pltpu.VMEM((depth, height, tile), F32),
-            pltpu.VMEM(own.shape, BF16),
             pltpu.SemaphoreType.DMA((depth,)),
             pltpu.SemaphoreType.DMA((depth,)),
-            pltpu.SemaphoreType.DMA,
         ],
         input_output_aliases=aliases,
         compiler_params=pltpu.CompilerParams(vmem_limit_bytes=34 << 20),
         cost_estimate=pl.CostEstimate(
-            flops=length * 2 * rows * tile * tile, bytes_accessed=8 * length * tile * tile, transcendentals=0
+            flops=length * 2 * rows * height * tile, bytes_accessed=8 * length * height * tile, transcendentals=0
         ),
     )(*operands)
 
@@ -217,9 +209,10 @@
 
     if half % 8:
         everything = lax.all_gather(grad, "row", axis=0, tiled=True)
-        (sums,) = partial_sums(tables, everything, [], roots)
-        new_stats = update_stats(tables, everything, [], stats, 0, slots, None)
-        total = lax.psum_scatter(sums.astype(F32), "row", scatter_dimension=0, tiled=True)
+        (sums,) = partial_sums(tables, [everything], everything.shape[:1], roots)
+        new_stats = update_stats(tables, [everything], stats, 0, slots * CUT, None)
+        terms = lax.all_to_all(sums, "row", split_axis=0, concat_axis=0, tiled=True)
+        total = jnp.sum(terms.reshape(devices, width, order), axis=0, dtype=F32)
         return new_stats, total.astype(BF16)
 
     walk = chip_cycle(chips)
@@ -233,30 +226,44 @@
     swap = lambda v: lax.ppermute(v, "row", [(i, i ^ 1) for i in range(devices)])
 
     reach = (chips - 1) // 2
-    chunk = {0: grad}
+    low, high = {0: grad[:half]}, {0: grad[half:]}
+    chunk = {}
     for step in range(1, reach + 1):
-        chunk[-step], chunk[step] = ahead(chunk[1 - step]), back(chunk[step - 1])
+        low[-step], high[step] = ahead(low[1 - step]), back(high[step - 1])
+        high[-step], low[step] = ahead(high[1 - step]), back(low[step - 1])
         if step == 1:
-            chunk[-1], tables = lax.optimization_barrier((chunk[-1], tables))
-    chunk["low"], chunk["high"] = ahead(chunk[-reach][:half]), back(chunk[reach][half:])
-    names = ["low", "high"]
-    for step in range(reach, 0, -1):
-        names += [-step, step]
-    rest = [swap(chunk[k]) for k in [*names, 0]] + [chunk[k] for k in names]
-    outs = partial_sums(tables, grad, rest, roots)
-    names.append(0)
+            low[-1], tables = lax.optimization_barrier((low[-1], tables))
+    chunk["low"], chunk["high"] = ahead(low[-reach]), back(high[reach])
+    for step in range(1, reach + 1):
+        halves = low[-step], high[-step], low[step], high[step]
+        if step < reach:
+            halves = lax.optimization_barrier((*halves, low[-reach], high[reach]))[:4]
+        chunk[-step], chunk[step] = jnp.concatenate(halves[:2], 0), jnp.concatenate(halves[2:], 0)
+    near = [k for step in range(reach, 0, -1) for k in (-step, step)]
+    names = ["low", "high", *near, 0]
+    other = {k: swap(chunk[k]) for k in near}
+    other[0] = swap(grad)
+    far = lax.optimization_barrier((chunk["low"], chunk["high"], *other.values()))
+    chunk["low"], chunk["high"] = far[:2]
+    other = dict(zip(other, far[2:]))
+    other["low"], other["high"] = swap(chunk["low"]), swap(chunk["high"])
+    rows = [other[k] for k in names] + [chunk[k] for k in names[:-1]] + [low[0], high[0]]
+    heights = [other[k].shape[0] for k in names]
+    outs = partial_sums(tables, rows, heights * 2, roots)
     other, own = dict(zip(names, outs)), dict(zip(names, outs[len(names) :]))
 
     here = lambda k: own[k].astype(F32) + swap(other[k]).astype(F32)
     sent = here("low").astype(BF16), here("high").astype(BF16)
-    shares = [slots * part // 8 for part in (0, 1, 3, 6, 8)] if reach == 3 else [0] * (reach + 1) + [slots]
+    pieces = slots * CUT
+    shares = [0] + [pieces - pieces * 9 * step // 32 for step in range(3, -1, -1)]
+    shares = [0] * (reach - 3) + shares if reach >= 3 else [0] * (reach + 1) + [pieces]
     done = None
     for step in range(reach, -1, -1):
         low, high = back(sent[0]), ahead(sent[1])
         base, stop = shares[reach - step : reach - step + 2]
         if stop > base:
             now = lax.optimization_barrier((*tables, *sent))[: len(tables)]
-            done = update_stats(now, grad, rest, stats, base, stop - base, done)
+            done = update_stats(now, rows, stats, base, stop - base, done)
             low, high, done = lax.optimization_barrier((low, high, done))
         low, high = low.astype(F32), high.astype(F32)
         if step == reach:

time: 123 us -> 119 us (0.967)
  waiting for transfers between devices: 49.9 us -> 40.8 us
  starting transfers between devices: 21.4 us -> 27.8 us
  Pallas kernels: 46.2 us -> 44.3 us
    ppermute x8 -> x11, waiting for transfers between devices: 39.4 us -> 21.2 us  [body(): back = lambda v: lax.ppermute(v, 'row', backward)]
    ppermute x8 -> x11, starting transfers between devices: 4.66 us -> 15.5 us  [body(): ahead = lambda v: lax.ppermute(v, 'row', forward)]
    ppermute x8 -> x11, waiting for transfers between devices: 8.31 us -> 15.3 us  [body(): ahead = lambda v: lax.ppermute(v, 'row', forward)]
    ppermute x8 -> x11, starting transfers between devices: 13.2 us -> 8.72 us  [body(): back = lambda v: lax.ppermute(v, 'row', backward)]
    ppermute x18, waiting for transfers between devices: 2.17 us -> 4.35 us  [body(): lax.ppermute(v, 'row', [(i, i ^ 1) for i in range(devices)])]
    pallas_call x5, Pallas kernels: 46.2 us -> 44.3 us  [the longest x4 29.9 us: update_stats(): pl.pallas_call(functools.partial(stat_kernel, len(grads), base, length),...]
  transfers between devices with their start and end apart: 34 -> 40, of which waited for: 16 -> 21; matrix products, arithmetic and copies ran while one was open for 2% -> 2% of each run, Pallas kernels for 26% -> 25%
where the time goes in v2:
time: 119 us
  Pallas kernels  44.3 us (37%)
  waiting for transfers between devices  40.8 us (34%)
  starting transfers between devices  27.8 us (23%)
  other arithmetic  3.68 us (3%)
  local copies, waits for them, and re-layouts  1.31 us (1%)
    pallas_call x4, Pallas kernels, update_stats(): pl.pallas_call(functools.partial(stat_kernel, len(grads), base, length),...  29.9 us
    ppermute x11, waiting for transfers between devices, body(): back = lambda v: lax.ppermute(v, 'row', backward)  21.2 us
    ppermute x11, starting transfers between devices, body(): ahead = lambda v: lax.ppermute(v, 'row', forward)  15.5 us
    ppermute x11, waiting for transfers between devices, body(): ahead = lambda v: lax.ppermute(v, 'row', forward)  15.3 us
    pallas_call x1, Pallas kernels, partial_sums(): pl.pallas_call(functools.partial(part_kernel, len(grads)), out_shape=[jax...  14.4 us
    ppermute x11, starting transfers between devices, body(): back = lambda v: lax.ppermute(v, 'row', backward)  8.72 us
    ppermute x18, waiting for transfers between devices, body(): lax.ppermute(v, 'row', [(i, i ^ 1) for i in range(devices)])  4.35 us
    ppermute x18, starting transfers between devices, body(): lax.ppermute(v, 'row', [(i, i ^ 1) for i in range(devices)])  3.54 us
  transfers between devices with their start and end apart: 40, of which 21 were waited for; matrix products, arithmetic and copies ran while one was open for 2% of the time, Pallas kernels for 25%

profile of v2, /device:TPU:0, one launch (start us, length us, event | category | flops | bytes accessed | tf_op | source)
XLA Modules:
  0.0 118.7 jit_solution(16484382178974679036)
XLA Ops:
  0.6 1.1 fusion.14
  1.7 3.1 %collective-permute-start = (bf16[8,15360]{1,0:T(8,128)(2,1)S(1)}, bf16[8,15360]{1,0:T(8,128)(2,1)S(1)}, u32[]{:S(2)}, u32[]{:S(2)}) collective-permute-start(bf16[8,15360]{1,0:T(8,128)(2,1)S(1)} %get-tuple-element.131.refs_17_), channel_id=1, source_target_pairs={{0,4},{1,5},{4,8},{5,9},{8,12},{9,13},{12,14},{13,15},{14,10},{15,... | collective-permute-start | bytes 737288 | tf_op jit(solution)/shard_map/ppermute | solution.py:224
  4.8 2.0 %collective-permute-start.8 = (bf16[8,15360]{1,0:T(8,128)(2,1)S(1)}, bf16[8,15360]{1,0:T(8,128)(2,1)S(1)}, u32[]{:S(2)}, u32[]{:S(2)}) collective-permute-start(bf16[8,15360]{1,0:T(8,128)(2,1)S(1)} %get-tuple-element.130.refs_18_), channel_id=1, source_target_pairs={{0,4},{1,5},{4,8},{5,9},{8,12},{9,13},{12,14},{13,15},{14,10},{15,... | collective-permute-start | bytes 737288 | tf_op jit(solution)/shard_map/ppermute | solution.py:224
  6.8 0.7 compare_convert_fusion.live_ref
  7.6 0.8 subtract_add_fusion
  8.3 3.2 %collective-permute-done = bf16[8,15360]{1,0:T(8,128)(2,1)S(1)} collective-permute-done((bf16[8,15360]{1,0:T(8,128)(2,1)S(1)}, bf16[8,15360]{1,0:T(8,128)(2,1)S(1)}, u32[]{:S(2)}, u32[]{:S(2)}) %collective-permute-start) | collective-permute-done | bytes 245792 | tf_op jit(solution)/shard_map/ppermute | solution.py:224
  11.5 2.2 %collective-permute-done.4 = bf16[8,15360]{1,0:T(8,128)(2,1)S(1)} collective-permute-done((bf16[8,15360]{1,0:T(8,128)(2,1)S(1)}, bf16[8,15360]{1,0:T(8,128)(2,1)S(1)}, u32[]{:S(2)}, u32[]{:S(2)}) %collective-permute-start.4) | collective-permute-done | bytes 245792 | tf_op jit(solution)/shard_map/ppermute | solution.py:225
  13.7 2.0 %collective-permute-start.1 = (bf16[8,15360]{1,0:T(8,128)(2,1)S(1)}, bf16[8,15360]{1,0:T(8,128)(2,1)S(1)}, u32[]{:S(2)}, u32[]{:S(2)}) collective-permute-start(bf16[8,15360]{1,0:T(8,128)(2,1)S(1)} %collective-permute-done), channel_id=1, source_target_pairs={{0,4},{1,5},{4,8},{5,9},{8,12},{9,13},{12,14},{13,15},{14,10},{15,... | collective-permute-start | bytes 737288 | tf_op jit(solution)/shard_map/ppermute | solution.py:224
  15.7 1.1 collective-permute-done.8
  16.8 2.1 %collective-permute-start.9 = (bf16[8,15360]{1,0:T(8,128)(2,1)S(1)}, bf16[8,15360]{1,0:T(8,128)(2,1)S(1)}, u32[]{:S(2)}, u32[]{:S(2)}) collective-permute-start(bf16[8,15360]{1,0:T(8,128)(2,1)S(1)} %collective-permute-done.8), channel_id=1, source_target_pairs={{0,4},{1,5},{4,8},{5,9},{8,12},{9,13},{12,14},{13,15},{14,10},{15,... | collective-permute-start | bytes 737288 | tf_op jit(solution)/shard_map/ppermute | solution.py:224
  19.0 5.3 %collective-permute-done.5 = bf16[8,15360]{1,0:T(8,128)(2,1)S(1)} collective-permute-done((bf16[8,15360]{1,0:T(8,128)(2,1)S(1)}, bf16[8,15360]{1,0:T(8,128)(2,1)S(1)}, u32[]{:S(2)}, u32[]{:S(2)}) %collective-permute-start.5) | collective-permute-done | bytes 245792 | tf_op jit(solution)/shard_map/ppermute | solution.py:225
  24.2 2.0 %collective-permute-start.2 = (bf16[8,15360]{1,0:T(8,128)(2,1)S(1)}, bf16[8,15360]{1,0:T(8,128)(2,1)S(1)}, u32[]{:S(2)}, u32[]{:S(2)}) collective-permute-start(bf16[8,15360]{1,0:T(8,128)(2,1)S(1)} %collective-permute-done.1), channel_id=1, source_target_pairs={{0,4},{1,5},{4,8},{5,9},{8,12},{9,13},{12,14},{13,15},{14,10},{15,... | collective-permute-start | bytes 737288 | tf_op jit(solution)/shard_map/ppermute | solution.py:224
  26.3 1.6 %collective-permute-done.9 = bf16[8,15360]{1,0:T(8,128)(2,1)S(1)} collective-permute-done((bf16[8,15360]{1,0:T(8,128)(2,1)S(1)}, bf16[8,15360]{1,0:T(8,128)(2,1)S(1)}, u32[]{:S(2)}, u32[]{:S(2)}) %collective-permute-start.9) | collective-permute-done | bytes 245792 | tf_op jit(solution)/shard_map/ppermute | solution.py:224
  27.9 2.0 %collective-permute-start.10 = (bf16[8,15360]{1,0:T(8,128)(2,1)S(1)}, bf16[8,15360]{1,0:T(8,128)(2,1)S(1)}, u32[]{:S(2)}, u32[]{:S(2)}) collective-permute-start(bf16[8,15360]{1,0:T(8,128)(2,1)S(1)} %collective-permute-done.9), channel_id=1, source_target_pairs={{0,4},{1,5},{4,8},{5,9},{8,12},{9,13},{12,14},{13,15},{14,10},{15,... | collective-permute-start | bytes 737288 | tf_op jit(solution)/shard_map/ppermute | solution.py:224
  29.9 4.9 %collective-permute-done.6 = bf16[8,15360]{1,0:T(8,128)(2,1)S(1)} collective-permute-done((bf16[8,15360]{1,0:T(8,128)(2,1)S(1)}, bf16[8,15360]{1,0:T(8,128)(2,1)S(1)}, u32[]{:S(2)}, u32[]{:S(2)}) %collective-permute-start.6) | collective-permute-done | bytes 245792 | tf_op jit(solution)/shard_map/ppermute | solution.py:225
  34.9 2.1 %collective-permute-done.10 = bf16[8,15360]{1,0:T(8,128)(2,1)S(1)} collective-permute-done((bf16[8,15360]{1,0:T(8,128)(2,1)S(1)}, bf16[8,15360]{1,0:T(8,128)(2,1)S(1)}, u32[]{:S(2)}, u32[]{:S(2)}) %collective-permute-start.10) | collective-permute-done | bytes 245792 | tf_op jit(solution)/shard_map/ppermute | solution.py:224
  37.1 0.6 collective-permute-start.19
  37.8 1.8 %collective-permute-start.7 = (bf16[8,15360]{1,0:T(8,128)(2,1)S(1)}, bf16[8,15360]{1,0:T(8,128)(2,1)S(1)}, u32[]{:S(2)}, u32[]{:S(2)}) collective-permute-start(bf16[8,15360]{1,0:T(8,128)(2,1)S(1)} %collective-permute-done.6), channel_id=1, source_target_pairs={{4,0},{5,1},{8,4},{9,5},{12,8},{13,9},{14,12},{15,13},{10,14},{11,... | collective-permute-start | bytes 737288 | tf_op jit(solution)/shard_map/ppermute | solution.py:225
  39.6 0.6 collective-permute-start.3
  40.3 5.5 %collective-permute-done.7.refs_10_ = bf16[8,15360]{1,0:T(8,128)(2,1)S(1)} collective-permute-done((bf16[8,15360]{1,0:T(8,128)(2,1)S(1)}, bf16[8,15360]{1,0:T(8,128)(2,1)S(1)}, u32[]{:S(2)}, u32[]{:S(2)}) %collective-permute-start.7) | collective-permute-done | bytes 245792 | tf_op jit(solution)/shard_map/ppermute | solution.py:225
  45.8 1.4 %collective-permute-done.3.refs_9_ = bf16[8,15360]{1,0:T(8,128)(2,1)S(1)} collective-permute-done((bf16[8,15360]{1,0:T(8,128)(2,1)S(1)}, bf16[8,15360]{1,0:T(8,128)(2,1)S(1)}, u32[]{:S(2)}, u32[]{:S(2)}) %collective-permute-start.3) | collective-permute-done | bytes 245792 | tf_op jit(solution)/shard_map/ppermute | solution.py:224
  47.2 0.5 collective-permute-start.15
  47.7 1.3 %collective-permute-done.16.refs_4_ = bf16[16,15360]{1,0:T(8,128)(2,1)S(1)} collective-permute-done((bf16[16,15360]{1,0:T(8,128)(2,1)S(1)}, bf16[16,15360]{1,0:T(8,128)(2,1)S(1)}, u32[]{:S(2)}, u32[]{:S(2)}) %collective-permute-start.16) | collective-permute-done | bytes 491552 | tf_op jit(solution)/shard_map/ppermute | solution.py:226
  49.0 0.7 collective-permute-done.15.refs_3_
  49.9 0.4 collective-permute-start.22
  50.2 1.0 collective-permute-done.21.refs_0_
  51.6 14.4 %shard_map.59 = (bf16[8,15360]{1,0:T(8,128)(2,1)S(1)}, bf16[8,15360]{1,0:T(8,128)(2,1)S(1)}, bf16[16,15360]{1,0:T(8,128)(2,1)S(1)}, bf16[16,15360]{1,0:T(8,128)(...) custom-call(s32[8]{0:T(128)S(1)} %get-tuple-element.119.first_ref, ...), custom_call_target="tpu_custom_call" | custom-call | flops 8589934592 | bytes 16777216 | tf_op jit(solution)/shard_map/pallas_call | solution.py:95
  66.1 0.5 collective-permute-start.28
  66.7 0.9 collective-permute-done.26
  67.7 2.1 %collective-permute-start.27 = (bf16[8,15360]{1,0:T(8,128)(2,1)S(1)}, bf16[8,15360]{1,0:T(8,128)(2,1)S(1)}, u32[]{:S(2)}, u32[]{:S(2)}) collective-permute-start(bf16[8,15360]{1,0:T(8,128)(2,1)S(1)} %add_convert_fusion.8), channel_id=1, source_target_pairs={{4,0},{5,1},{8,4},{9,5},{12,8},{13,9},{14,12},{15,13},{10,14},{11,... | collective-permute-start | bytes 737288 | tf_op jit(solution)/shard_map/ppermute | solution.py:225
  70.1 5.7 %shard_map.60.refs_20_ = f32[8,1024,1024]{2,1,0:T(8,128)} custom-call(s32[8]{0:T(128)S(1)} %get-tuple-element.119.first_ref, s32[8]{0:T(128)S(1)} %get-tuple-element.120.second_ref, s32[8]{0:T(128)S(1)} %compare_convert_fusion.live_ref, bf16[8,15360]{1,0:T(8,128)(2,1)S(1)} %collective-permute-done.21.refs_0_, ...), custom_call_target="tpu_custom_call" | custom-call | flops 671088640 | bytes 10485760 | tf_op jit(solution)/shard_map/pallas_call | solution.py:183
  75.7 2.1 %collective-permute-done.29 = bf16[8,15360]{1,0:T(8,128)(2,1)S(1)} collective-permute-done((bf16[8,15360]{1,0:T(8,128)(2,1)S(1)}, bf16[8,15360]{1,0:T(8,128)(2,1)S(1)}, u32[]{:S(2)}, u32[]{:S(2)}) %collective-permute-start.29) | collective-permute-done | bytes 245792 | tf_op jit(solution)/shard_map/ppermute | solution.py:224
  78.0 1.4 %collective-permute-start.30 = (bf16[16,15360]{1,0:T(8,128)(2,1)S(1)}, bf16[16,15360]{1,0:T(8,128)(2,1)S(1)}, u32[]{:S(2)}, u32[]{:S(2)}) collective-permute-start(bf16[16,15360]{1,0:T(8,128)(2,1)S(1)} %add_convert_fusion.6), channel_id=1, source_target_pairs={{4,0},{5,1},{8,4},{9,5},{12,8},{13,9},{14,12},{15,13},{10,14},{11,... | collective-permute-start | bytes 1474568 | tf_op jit(solution)/shard_map/ppermute | solution.py:225
  79.6 0.7 collective-permute-start.32
  80.3 0.5 collective-permute-start.34
  80.8 8.1 %shard_map.61.refs_20_ = f32[8,1024,1024]{2,1,0:T(8,128)} custom-call(s32[8]{0:T(128)S(1)} %get-tuple-element.119.first_ref, s32[8]{0:T(128)S(1)} %get-tuple-element.120.second_ref, s32[8]{0:T(128)S(1)} %compare_convert_fusion.live_ref, bf16[8,15360]{1,0:T(8,128)(2,1)S(1)} %collective-permute-done.21.refs_0_, ...), custom_call_target="tpu_custom_call", output_to_operand_aliasing={{}: (23, {})} | custom-call | flops 1207959552 | bytes 18874368 | tf_op jit(solution)/shard_map/pallas_call | solution.py:183
  88.9 1.5 %collective-permute-done.30 = bf16[16,15360]{1,0:T(8,128)(2,1)S(1)} collective-permute-done((bf16[16,15360]{1,0:T(8,128)(2,1)S(1)}, bf16[16,15360]{1,0:T(8,128)(2,1)S(1)}, u32[]{:S(2)}, u32[]{:S(2)}) %collective-permute-start.30) | collective-permute-done | bytes 491552 | tf_op jit(solution)/shard_map/ppermute | solution.py:225
  90.4 1.4 %collective-permute-done.32 = bf16[16,15360]{1,0:T(8,128)(2,1)S(1)} collective-permute-done((bf16[16,15360]{1,0:T(8,128)(2,1)S(1)}, bf16[16,15360]{1,0:T(8,128)(2,1)S(1)}, u32[]{:S(2)}, u32[]{:S(2)}) %collective-permute-start.32) | collective-permute-done | bytes 491552 | tf_op jit(solution)/shard_map/ppermute | solution.py:224
  92.0 1.5 %collective-permute-start.33 = (bf16[16,15360]{1,0:T(8,128)(2,1)S(1)}, bf16[16,15360]{1,0:T(8,128)(2,1)S(1)}, u32[]{:S(2)}, u32[]{:S(2)}) collective-permute-start(bf16[16,15360]{1,0:T(8,128)(2,1)S(1)} %add_convert_fusion.4), channel_id=1, source_target_pairs={{4,0},{5,1},{8,4},{9,5},{12,8},{13,9},{14,12},{15,13},{10,14},{11,... | collective-permute-start | bytes 1474568 | tf_op jit(solution)/shard_map/ppermute | solution.py:225
  93.6 0.7 collective-permute-start.35
  94.3 0.5 collective-permute-start.37
  94.8 8.1 %shard_map.62.refs_20_ = f32[8,1024,1024]{2,1,0:T(8,128)} custom-call(s32[8]{0:T(128)S(1)} %get-tuple-element.119.first_ref, s32[8]{0:T(128)S(1)} %get-tuple-element.120.second_ref, s32[8]{0:T(128)S(1)} %compare_convert_fusion.live_ref, bf16[8,15360]{1,0:T(8,128)(2,1)S(1)} %collective-permute-done.21.refs_0_, ...), custom_call_target="tpu_custom_call", output_to_operand_aliasing={{}: (23, {})} | custom-call | flops 1207959552 | bytes 18874368 | tf_op jit(solution)/shard_map/pallas_call | solution.py:183
  103.3 1.1 collective-permute-done.35
  104.5 1.9 %collective-permute-start.36 = (bf16[16,15360]{1,0:T(8,128)(2,1)S(1)}, bf16[16,15360]{1,0:T(8,128)(2,1)S(1)}, u32[]{:S(2)}, u32[]{:S(2)}) collective-permute-start(bf16[16,15360]{1,0:T(8,128)(2,1)S(1)} %add_convert_fusion.2), channel_id=1, source_target_pairs={{4,0},{5,1},{8,4},{9,5},{12,8},{13,9},{14,12},{15,13},{10,14},{11,... | collective-permute-start | bytes 1474568 | tf_op jit(solution)/shard_map/ppermute | solution.py:225
  106.9 8.1 %shard_map.63 = f32[8,1024,1024]{2,1,0:T(8,128)} custom-call(s32[8]{0:T(128)S(1)} %get-tuple-element.119.first_ref, s32[8]{0:T(128)S(1)} %get-tuple-element.120.second_ref, s32[8]{0:T(128)S(1)} %compare_convert_fusion.live_ref, bf16[8,15360]{1,0:T(8,128)(2,1)S(1)} %collective-permute-done.21.refs_0_, ...), custom_call_target="tpu_custom_call", output_to_operand_aliasing={{}: (23, {})} | custom-call | flops 1207959552 | bytes 18874368 | tf_op jit(solution)/shard_map/pallas_call | solution.py:183
  114.9 1.4 %collective-permute-done.36 = bf16[16,15360]{1,0:T(8,128)(2,1)S(1)} collective-permute-done((bf16[16,15360]{1,0:T(8,128)(2,1)S(1)}, bf16[16,15360]{1,0:T(8,128)(2,1)S(1)}, u32[]{:S(2)}, u32[]{:S(2)}) %collective-permute-start.36) | collective-permute-done | bytes 491552 | tf_op jit(solution)/shard_map/ppermute | solution.py:225
  116.3 1.4 %collective-permute-done.38 = bf16[16,15360]{1,0:T(8,128)(2,1)S(1)} collective-permute-done((bf16[16,15360]{1,0:T(8,128)(2,1)S(1)}, bf16[16,15360]{1,0:T(8,128)(2,1)S(1)}, u32[]{:S(2)}, u32[]{:S(2)}) %collective-permute-start.38) | collective-permute-done | bytes 491552 | tf_op jit(solution)/shard_map/ppermute | solution.py:224
  117.7 1.0 add_convert_fusion
  (61 shorter events, 3.1 us)
Async XLA Ops:
  1.7 9.8 %collective-permute-start = (bf16[8,15360]{1,0:T(8,128)(2,1)S(1)}, bf16[8,15360]{1,0:T(8,128)(2,1)S(1)}, u32[]{:S(2)}, u32[]{:S(2)}) collective-permute-start(bf16[8,15360]{1,0:T(8,128)(2,1)S(1)} %get-tuple-element.131.refs_17_), channel_id=1, source_target_pairs={{0,4},{1,5},{4,8},{5,9},{8,12},{9,13},{12,14},{13,15},{14,10},{15,... | collective-permute-start | bytes 737288 | tf_op jit(solution)/shard_map/ppermute | solution.py:224
  4.8 8.9 %collective-permute-start.4 = (bf16[8,15360]{1,0:T(8,128)(2,1)S(1)}, bf16[8,15360]{1,0:T(8,128)(2,1)S(1)}, u32[]{:S(2)}, u32[]{:S(2)}) collective-permute-start(bf16[8,15360]{1,0:T(8,128)(2,1)S(1)} %get-tuple-element.130.refs_18_), channel_id=1, source_target_pairs={{4,0},{5,1},{8,4},{9,5},{12,8},{13,9},{14,12},{15,13},{10,14},{11,... | collective-permute-start | bytes 737288 | tf_op jit(solution)/shard_map/ppermute | solution.py:225
  4.8 12.0 %collective-permute-start.8 = (bf16[8,15360]{1,0:T(8,128)(2,1)S(1)}, bf16[8,15360]{1,0:T(8,128)(2,1)S(1)}, u32[]{:S(2)}, u32[]{:S(2)}) collective-permute-start(bf16[8,15360]{1,0:T(8,128)(2,1)S(1)} %get-tuple-element.130.refs_18_), channel_id=1, source_target_pairs={{0,4},{1,5},{4,8},{5,9},{8,12},{9,13},{12,14},{13,15},{14,10},{15,... | collective-permute-start | bytes 737288 | tf_op jit(solution)/shard_map/ppermute | solution.py:224
  6.8 12.1 %collective-permute-start.12 = (bf16[8,15360]{1,0:T(8,128)(2,1)S(1)}, bf16[8,15360]{1,0:T(8,128)(2,1)S(1)}, u32[]{:S(2)}, u32[]{:S(2)}) collective-permute-start(bf16[8,15360]{1,0:T(8,128)(2,1)S(1)} %get-tuple-element.131.refs_17_), channel_id=1, source_target_pairs={{4,0},{5,1},{8,4},{9,5},{12,8},{13,9},{14,12},{15,13},{10,14},{11,... | collective-permute-start | bytes 737288 | tf_op jit(solution)/shard_map/ppermute | solution.py:225
  13.7 10.5 %collective-permute-start.5 = (bf16[8,15360]{1,0:T(8,128)(2,1)S(1)}, bf16[8,15360]{1,0:T(8,128)(2,1)S(1)}, u32[]{:S(2)}, u32[]{:S(2)}) collective-permute-start(bf16[8,15360]{1,0:T(8,128)(2,1)S(1)} %collective-permute-done.4), channel_id=1, source_target_pairs={{4,0},{5,1},{8,4},{9,5},{12,8},{13,9},{14,12},{15,13},{10,14},{11,... | collective-permute-start | bytes 737288 | tf_op jit(solution)/shard_map/ppermute | solution.py:225
  13.7 10.5 %collective-permute-start.1 = (bf16[8,15360]{1,0:T(8,128)(2,1)S(1)}, bf16[8,15360]{1,0:T(8,128)(2,1)S(1)}, u32[]{:S(2)}, u32[]{:S(2)}) collective-permute-start(bf16[8,15360]{1,0:T(8,128)(2,1)S(1)} %collective-permute-done), channel_id=1, source_target_pairs={{0,4},{1,5},{4,8},{5,9},{8,12},{9,13},{12,14},{13,15},{14,10},{15,... | collective-permute-start | bytes 737288 | tf_op jit(solution)/shard_map/ppermute | solution.py:224
  16.8 11.1 %collective-permute-start.9 = (bf16[8,15360]{1,0:T(8,128)(2,1)S(1)}, bf16[8,15360]{1,0:T(8,128)(2,1)S(1)}, u32[]{:S(2)}, u32[]{:S(2)}) collective-permute-start(bf16[8,15360]{1,0:T(8,128)(2,1)S(1)} %collective-permute-done.8), channel_id=1, source_target_pairs={{0,4},{1,5},{4,8},{5,9},{8,12},{9,13},{12,14},{13,15},{14,10},{15,... | collective-permute-start | bytes 737288 | tf_op jit(solution)/shard_map/ppermute | solution.py:224
  19.0 10.9 %collective-permute-start.13 = (bf16[8,15360]{1,0:T(8,128)(2,1)S(1)}, bf16[8,15360]{1,0:T(8,128)(2,1)S(1)}, u32[]{:S(2)}, u32[]{:S(2)}) collective-permute-start(bf16[8,15360]{1,0:T(8,128)(2,1)S(1)} %collective-permute-done.12), channel_id=1, source_target_pairs={{4,0},{5,1},{8,4},{9,5},{12,8},{13,9},{14,12},{15,13},{10,14},{11,... | collective-permute-start | bytes 737288 | tf_op jit(solution)/shard_map/ppermute | solution.py:225
  24.2 10.5 %collective-permute-start.6 = (bf16[8,15360]{1,0:T(8,128)(2,1)S(1)}, bf16[8,15360]{1,0:T(8,128)(2,1)S(1)}, u32[]{:S(2)}, u32[]{:S(2)}) collective-permute-start(bf16[8,15360]{1,0:T(8,128)(2,1)S(1)} %collective-permute-done.5), channel_id=1, source_target_pairs={{4,0},{5,1},{8,4},{9,5},{12,8},{13,9},{14,12},{15,13},{10,14},{11,... | collective-permute-start | bytes 737288 | tf_op jit(solution)/shard_map/ppermute | solution.py:225
  24.2 10.5 %collective-permute-start.2 = (bf16[8,15360]{1,0:T(8,128)(2,1)S(1)}, bf16[8,15360]{1,0:T(8,128)(2,1)S(1)}, u32[]{:S(2)}, u32[]{:S(2)}) collective-permute-start(bf16[8,15360]{1,0:T(8,128)(2,1)S(1)} %collective-permute-done.1), channel_id=1, source_target_pairs={{0,4},{1,5},{4,8},{5,9},{8,12},{9,13},{12,14},{13,15},{14,10},{15,... | collective-permute-start | bytes 737288 | tf_op jit(solution)/shard_map/ppermute | solution.py:224
  26.3 13.9 %collective-permute-start.20 = (bf16[16,15360]{1,0:T(8,128)(2,1)}, bf16[16,15360]{1,0:T(8,128)(2,1)S(1)}, u32[]{:S(2)}, u32[]{:S(2)}) collective-permute-start(bf16[16,15360]{1,0:T(8,128)(2,1)} %param.4), channel_id=1, source_target_pairs={{0,1},{1,0},{2,3},{3,2},{4,5},{5,4},{6,7},{7,6},{8,9},{9,8},{10,11... | collective-permute-start | bytes 1474568 | tf_op jit(solution)/shard_map/ppermute | solution.py:226
  27.9 9.2 %collective-permute-start.10 = (bf16[8,15360]{1,0:T(8,128)(2,1)S(1)}, bf16[8,15360]{1,0:T(8,128)(2,1)S(1)}, u32[]{:S(2)}, u32[]{:S(2)}) collective-permute-start(bf16[8,15360]{1,0:T(8,128)(2,1)S(1)} %collective-permute-done.9), channel_id=1, source_target_pairs={{0,4},{1,5},{4,8},{5,9},{8,12},{9,13},{12,14},{13,15},{14,10},{15,... | collective-permute-start | bytes 737288 | tf_op jit(solution)/shard_map/ppermute | solution.py:224
  29.9 9.7 %collective-permute-start.14 = (bf16[8,15360]{1,0:T(8,128)(2,1)S(1)}, bf16[8,15360]{1,0:T(8,128)(2,1)S(1)}, u32[]{:S(2)}, u32[]{:S(2)}) collective-permute-start(bf16[8,15360]{1,0:T(8,128)(2,1)S(1)} %collective-permute-done.13), channel_id=1, source_target_pairs={{4,0},{5,1},{8,4},{9,5},{12,8},{13,9},{14,12},{15,13},{10,14},{11,... | collective-permute-start | bytes 737288 | tf_op jit(solution)/shard_map/ppermute | solution.py:225
  37.0 10.1 %collective-permute-start.11 = (bf16[16,15360]{1,0:T(8,128)(2,1)S(1)}, bf16[16,15360]{1,0:T(8,128)(2,1)S(1)}, u32[]{:S(2)}, u32[]{:S(2)}) collective-permute-start(bf16[16,15360]{1,0:T(8,128)(2,1)S(1)} %constant_dynamic-update-slice_fusion.refs_11_), channel_id=1, source_target_pairs={{0,1},{1,0},{2,3},{3,2},{4,5},{5,4},{6,7},{7,6},{8,9},{9,8},{10,11... | collective-permute-start | bytes 1474568 | tf_op jit(solution)/shard_map/ppermute | solution.py:226
  37.1 10.5 %collective-permute-start.19 = (bf16[16,15360]{1,0:T(8,128)(2,1)S(1)}, bf16[16,15360]{1,0:T(8,128)(2,1)S(1)}, u32[]{:S(2)}, u32[]{:S(2)}) collective-permute-start(bf16[16,15360]{1,0:T(8,128)(2,1)S(1)} %constant_dynamic-update-slice_fusion.10.refs_16_), channel_id=1, source_target_pairs={{0,1},{1,0},{2,3},{3,2},{4,5},{5,4},{6,7},{7,6},{8,9},{9,8},{10,11... | collective-permute-start | bytes 1474568 | tf_op jit(solution)/shard_map/ppermute | solution.py:226
  37.8 8.0 %collective-permute-start.7 = (bf16[8,15360]{1,0:T(8,128)(2,1)S(1)}, bf16[8,15360]{1,0:T(8,128)(2,1)S(1)}, u32[]{:S(2)}, u32[]{:S(2)}) collective-permute-start(bf16[8,15360]{1,0:T(8,128)(2,1)S(1)} %collective-permute-done.6), channel_id=1, source_target_pairs={{4,0},{5,1},{8,4},{9,5},{12,8},{13,9},{14,12},{15,13},{10,14},{11,... | collective-permute-start | bytes 737288 | tf_op jit(solution)/shard_map/ppermute | solution.py:225
  39.6 7.6 %collective-permute-start.3 = (bf16[8,15360]{1,0:T(8,128)(2,1)S(1)}, bf16[8,15360]{1,0:T(8,128)(2,1)S(1)}, u32[]{:S(2)}, u32[]{:S(2)}) collective-permute-start(bf16[8,15360]{1,0:T(8,128)(2,1)S(1)} %collective-permute-done.2), channel_id=1, source_target_pairs={{0,4},{1,5},{4,8},{5,9},{8,12},{9,13},{12,14},{13,15},{14,10},{15,... | collective-permute-start | bytes 737288 | tf_op jit(solution)/shard_map/ppermute | solution.py:224
  40.2 7.5 %collective-permute-start.17 = (bf16[16,15360]{1,0:T(8,128)(2,1)S(1)}, bf16[16,15360]{1,0:T(8,128)(2,1)S(1)}, u32[]{:S(2)}, u32[]{:S(2)}) collective-permute-start(bf16[16,15360]{1,0:T(8,128)(2,1)S(1)} %constant_dynamic-update-slice_fusion.6.refs_14_), channel_id=1, source_target_pairs={{0,1},{1,0},{2,3},{3,2},{4,5},{5,4},{6,7},{7,6},{8,9},{9,8},{10,11... | collective-permute-start | bytes 1474568 | tf_op jit(solution)/shard_map/ppermute | solution.py:226
  45.8 1.9 %collective-permute-start.18 = (bf16[16,15360]{1,0:T(8,128)(2,1)S(1)}, bf16[16,15360]{1,0:T(8,128)(2,1)S(1)}, u32[]{:S(2)}, u32[]{:S(2)}) collective-permute-start(bf16[16,15360]{1,0:T(8,128)(2,1)S(1)} %constant_dynamic-update-slice_fusion.8.refs_15_), channel_id=1, source_target_pairs={{0,1},{1,0},{2,3},{3,2},{4,5},{5,4},{6,7},{7,6},{8,9},{9,8},{10,11... | collective-permute-start | bytes 1474568 | tf_op jit(solution)/shard_map/ppermute | solution.py:226
  47.2 1.9 %collective-permute-start.16 = (bf16[16,15360]{1,0:T(8,128)(2,1)S(1)}, bf16[16,15360]{1,0:T(8,128)(2,1)S(1)}, u32[]{:S(2)}, u32[]{:S(2)}) collective-permute-start(bf16[16,15360]{1,0:T(8,128)(2,1)S(1)} %constant_dynamic-update-slice_fusion.4.refs_13_), channel_id=1, source_target_pairs={{0,1},{1,0},{2,3},{3,2},{4,5},{5,4},{6,7},{7,6},{8,9},{9,8},{10,11... | collective-permute-start | bytes 1474568 | tf_op jit(solution)/shard_map/ppermute | solution.py:226
  47.2 2.6 %collective-permute-start.15 = (bf16[16,15360]{1,0:T(8,128)(2,1)S(1)}, bf16[16,15360]{1,0:T(8,128)(2,1)S(1)}, u32[]{:S(2)}, u32[]{:S(2)}) collective-permute-start(bf16[16,15360]{1,0:T(8,128)(2,1)S(1)} %constant_dynamic-update-slice_fusion.2.refs_12_), channel_id=1, source_target_pairs={{0,1},{1,0},{2,3},{3,2},{4,5},{5,4},{6,7},{7,6},{8,9},{9,8},{10,11... | collective-permute-start | bytes 1474568 | tf_op jit(solution)/shard_map/ppermute | solution.py:226
  49.7 1.5 %collective-permute-start.21 = (bf16[8,15360]{1,0:T(8,128)(2,1)S(1)}, bf16[8,15360]{1,0:T(8,128)(2,1)S(1)}, u32[]{:S(2)}, u32[]{:S(2)}) collective-permute-start(bf16[8,15360]{1,0:T(8,128)(2,1)S(1)} %collective-permute-done.3.refs_9_), channel_id=1, source_target_pairs={{0,1},{1,0},{2,3},{3,2},{4,5},{5,4},{6,7},{7,6},{8,9},{9,8},{10,11... | collective-permute-start | bytes 737288 | tf_op jit(solution)/shard_map/ppermute | solution.py:226
  49.9 1.7 %collective-permute-start.22 = (bf16[8,15360]{1,0:T(8,128)(2,1)S(1)}, bf16[8,15360]{1,0:T(8,128)(2,1)S(1)}, u32[]{:S(2)}, u32[]{:S(2)}) collective-permute-start(bf16[8,15360]{1,0:T(8,128)(2,1)S(1)} %collective-permute-done.7.refs_10_), channel_id=1, source_target_pairs={{0,1},{1,0},{2,3},{3,2},{4,5},{5,4},{6,7},{7,6},{8,9},{9,8},{10,11... | collective-permute-start | bytes 737288 | tf_op jit(solution)/shard_map/ppermute | solution.py:226
  66.0 1.6 %collective-permute-start.26 = (bf16[8,15360]{1,0:T(8,128)(2,1)S(1)}, bf16[8,15360]{1,0:T(8,128)(2,1)S(1)}, u32[]{:S(2)}, u32[]{:S(2)}) collective-permute-start(bf16[8,15360]{1,0:T(8,128)(2,1)S(1)} %get-tuple-element.93), channel_id=1, source_target_pairs={{0,1},{1,0},{2,3},{3,2},{4,5},{5,4},{6,7},{7,6},{8,9},{9,8},{10,11... | collective-permute-start | bytes 737288 | tf_op jit(solution)/shard_map/ppermute | solution.py:226
  66.1 3.7 %collective-permute-start.28 = (bf16[8,15360]{1,0:T(8,128)(2,1)S(1)}, bf16[8,15360]{1,0:T(8,128)(2,1)S(1)}, u32[]{:S(2)}, u32[]{:S(2)}) collective-permute-start(bf16[8,15360]{1,0:T(8,128)(2,1)S(1)} %get-tuple-element.95), channel_id=1, source_target_pairs={{0,1},{1,0},{2,3},{3,2},{4,5},{5,4},{6,7},{7,6},{8,9},{9,8},{10,11... | collective-permute-start | bytes 737288 | tf_op jit(solution)/shard_map/ppermute | solution.py:226
  66.6 11.3 %collective-permute-start.25 = (bf16[16,15360]{1,0:T(8,128)(2,1)S(1)}, bf16[16,15360]{1,0:T(8,128)(2,1)S(1)}, u32[]{:S(2)}, u32[]{:S(2)}) collective-permute-start(bf16[16,15360]{1,0:T(8,128)(2,1)S(1)} %get-tuple-element.91), channel_id=1, source_target_pairs={{0,1},{1,0},{2,3},{3,2},{4,5},{5,4},{6,7},{7,6},{8,9},{9,8},{10,11... | collective-permute-start | bytes 1474568 | tf_op jit(solution)/shard_map/ppermute | solution.py:226
  67.7 8.1 %collective-permute-start.27 = (bf16[8,15360]{1,0:T(8,128)(2,1)S(1)}, bf16[8,15360]{1,0:T(8,128)(2,1)S(1)}, u32[]{:S(2)}, u32[]{:S(2)}) collective-permute-start(bf16[8,15360]{1,0:T(8,128)(2,1)S(1)} %add_convert_fusion.8), channel_id=1, source_target_pairs={{4,0},{5,1},{8,4},{9,5},{12,8},{13,9},{14,12},{15,13},{10,14},{11,... | collective-permute-start | bytes 737288 | tf_op jit(solution)/shard_map/ppermute | solution.py:225
  69.8 8.0 %collective-permute-start.29 = (bf16[8,15360]{1,0:T(8,128)(2,1)S(1)}, bf16[8,15360]{1,0:T(8,128)(2,1)S(1)}, u32[]{:S(2)}, u32[]{:S(2)}) collective-permute-start(bf16[8,15360]{1,0:T(8,128)(2,1)S(1)} %add_convert_fusion.7), channel_id=1, source_target_pairs={{0,4},{1,5},{4,8},{5,9},{8,12},{9,13},{12,14},{13,15},{14,10},{15,... | collective-permute-start | bytes 737288 | tf_op jit(solution)/shard_map/ppermute | solution.py:224
  69.9 9.5 %collective-permute-start.31 = (bf16[16,15360]{1,0:T(8,128)(2,1)S(1)}, bf16[16,15360]{1,0:T(8,128)(2,1)S(1)}, u32[]{:S(2)}, u32[]{:S(2)}) collective-permute-start(bf16[16,15360]{1,0:T(8,128)(2,1)S(1)} %get-tuple-element.101), channel_id=1, source_target_pairs={{0,1},{1,0},{2,3},{3,2},{4,5},{5,4},{6,7},{7,6},{8,9},{9,8},{10,11... | collective-permute-start | bytes 1474568 | tf_op jit(solution)/shard_map/ppermute | solution.py:226
  78.0 12.4 %collective-permute-start.30 = (bf16[16,15360]{1,0:T(8,128)(2,1)S(1)}, bf16[16,15360]{1,0:T(8,128)(2,1)S(1)}, u32[]{:S(2)}, u32[]{:S(2)}) collective-permute-start(bf16[16,15360]{1,0:T(8,128)(2,1)S(1)} %add_convert_fusion.6), channel_id=1, source_target_pairs={{4,0},{5,1},{8,4},{9,5},{12,8},{13,9},{14,12},{15,13},{10,14},{11,... | collective-permute-start | bytes 1474568 | tf_op jit(solution)/shard_map/ppermute | solution.py:225
  79.6 12.2 %collective-permute-start.32 = (bf16[16,15360]{1,0:T(8,128)(2,1)S(1)}, bf16[16,15360]{1,0:T(8,128)(2,1)S(1)}, u32[]{:S(2)}, u32[]{:S(2)}) collective-permute-start(bf16[16,15360]{1,0:T(8,128)(2,1)S(1)} %add_convert_fusion.5), channel_id=1, source_target_pairs={{0,4},{1,5},{4,8},{5,9},{8,12},{9,13},{12,14},{13,15},{14,10},{15,... | collective-permute-start | bytes 1474568 | tf_op jit(solution)/shard_map/ppermute | solution.py:224
  80.3 11.5 %collective-permute-start.24 = (bf16[16,15360]{1,0:T(8,128)(2,1)S(1)}, bf16[16,15360]{1,0:T(8,128)(2,1)S(1)}, u32[]{:S(2)}, u32[]{:S(2)}) collective-permute-start(bf16[16,15360]{1,0:T(8,128)(2,1)S(1)} %get-tuple-element.89), channel_id=1, source_target_pairs={{0,1},{1,0},{2,3},{3,2},{4,5},{5,4},{6,7},{7,6},{8,9},{9,8},{10,11... | collective-permute-start | bytes 1474568 | tf_op jit(solution)/shard_map/ppermute | solution.py:226
  80.3 13.2 %collective-permute-start.34 = (bf16[16,15360]{1,0:T(8,128)(2,1)S(1)}, bf16[16,15360]{1,0:T(8,128)(2,1)S(1)}, u32[]{:S(2)}, u32[]{:S(2)}) collective-permute-start(bf16[16,15360]{1,0:T(8,128)(2,1)S(1)} %get-tuple-element.109), channel_id=1, source_target_pairs={{0,1},{1,0},{2,3},{3,2},{4,5},{5,4},{6,7},{7,6},{8,9},{9,8},{10,11... | collective-permute-start | bytes 1474568 | tf_op jit(solution)/shard_map/ppermute | solution.py:226
  92.0 11.3 %collective-permute-start.33 = (bf16[16,15360]{1,0:T(8,128)(2,1)S(1)}, bf16[16,15360]{1,0:T(8,128)(2,1)S(1)}, u32[]{:S(2)}, u32[]{:S(2)}) collective-permute-start(bf16[16,15360]{1,0:T(8,128)(2,1)S(1)} %add_convert_fusion.4), channel_id=1, source_target_pairs={{4,0},{5,1},{8,4},{9,5},{12,8},{13,9},{14,12},{15,13},{10,14},{11,... | collective-permute-start | bytes 1474568 | tf_op jit(solution)/shard_map/ppermute | solution.py:225
  93.6 10.7 %collective-permute-start.35 = (bf16[16,15360]{1,0:T(8,128)(2,1)S(1)}, bf16[16,15360]{1,0:T(8,128)(2,1)S(1)}, u32[]{:S(2)}, u32[]{:S(2)}) collective-permute-start(bf16[16,15360]{1,0:T(8,128)(2,1)S(1)} %add_convert_fusion.3), channel_id=1, source_target_pairs={{0,4},{1,5},{4,8},{5,9},{8,12},{9,13},{12,14},{13,15},{14,10},{15,... | collective-permute-start | bytes 1474568 | tf_op jit(solution)/shard_map/ppermute | solution.py:224
  94.3 10.0 %collective-permute-start.23 = (bf16[16,15360]{1,0:T(8,128)(2,1)S(1)}, bf16[16,15360]{1,0:T(8,128)(2,1)S(1)}, u32[]{:S(2)}, u32[]{:S(2)}) collective-permute-start(bf16[16,15360]{1,0:T(8,128)(2,1)S(1)} %get-tuple-element.87), channel_id=1, source_target_pairs={{0,1},{1,0},{2,3},{3,2},{4,5},{5,4},{6,7},{7,6},{8,9},{9,8},{10,11... | collective-permute-start | bytes 1474568 | tf_op jit(solution)/shard_map/ppermute | solution.py:226
  94.3 12.1 %collective-permute-start.37 = (bf16[16,15360]{1,0:T(8,128)(2,1)S(1)}, bf16[16,15360]{1,0:T(8,128)(2,1)S(1)}, u32[]{:S(2)}, u32[]{:S(2)}) collective-permute-start(bf16[16,15360]{1,0:T(8,128)(2,1)S(1)} %get-tuple-element.117), channel_id=1, source_target_pairs={{0,1},{1,0},{2,3},{3,2},{4,5},{5,4},{6,7},{7,6},{8,9},{9,8},{10,11... | collective-permute-start | bytes 1474568 | tf_op jit(solution)/shard_map/ppermute | solution.py:226
  104.5 11.8 %collective-permute-start.36 = (bf16[16,15360]{1,0:T(8,128)(2,1)S(1)}, bf16[16,15360]{1,0:T(8,128)(2,1)S(1)}, u32[]{:S(2)}, u32[]{:S(2)}) collective-permute-start(bf16[16,15360]{1,0:T(8,128)(2,1)S(1)} %add_convert_fusion.2), channel_id=1, source_target_pairs={{4,0},{5,1},{8,4},{9,5},{12,8},{13,9},{14,12},{15,13},{10,14},{11,... | collective-permute-start | bytes 1474568 | tf_op jit(solution)/shard_map/ppermute | solution.py:225
  106.6 11.1 %collective-permute-start.38 = (bf16[16,15360]{1,0:T(8,128)(2,1)S(1)}, bf16[16,15360]{1,0:T(8,128)(2,1)S(1)}, u32[]{:S(2)}, u32[]{:S(2)}) collective-permute-start(bf16[16,15360]{1,0:T(8,128)(2,1)S(1)} %add_convert_fusion.1), channel_id=1, source_target_pairs={{0,4},{1,5},{4,8},{5,9},{8,12},{9,13},{12,14},{13,15},{14,10},{15,... | collective-permute-start | bytes 1474568 | tf_op jit(solution)/shard_map/ppermute | solution.py:224
  106.9 10.8 %collective-permute-start.39 = (bf16[16,15360]{1,0:T(8,128)(2,1)S(1)}, bf16[16,15360]{1,0:T(8,128)(2,1)S(1)}, u32[]{:S(2)}, u32[]{:S(2)}) collective-permute-start(bf16[16,15360]{1,0:T(8,128)(2,1)S(1)} %get-tuple-element.125), channel_id=1, source_target_pairs={{0,1},{1,0},{2,3},{3,2},{4,5},{5,4},{6,7},{7,6},{8,9},{9,8},{10,11... | collective-permute-start | bytes 1474568 | tf_op jit(solution)/shard_map/ppermute | solution.py:226

commit v3 on v2

--- a/solution.py
+++ b/solution.py
@@ -37,37 +37,46 @@
 
 
 def part_kernel(count, first_ref, second_ref, live_ref, *refs):
-    grads, root_ref, outs = refs[:count], refs[count], refs[count + 1 : -3]
-    acc, held, sems = refs[-3:]
+    grads, early_ref, root_ref, outs = refs[:count], refs[count], refs[count + 1], refs[count + 2 : -4]
+    acc, held, seen, sems = refs[-4:]
     slots, tile, _ = root_ref.shape
-    depth = held.shape[0]
+    early, depth = early_ref.shape[0], held.shape[0]
+    panels = acc.shape[1] // tile
 
     def fetch(slot):
         at = lax.rem(slot, depth)
         return pltpu.make_async_copy(root_ref.at[slot], held.at[at], sems.at[at])
 
-    for slot in range(min(depth, slots)):
+    for slot in range(early, min(early + depth, slots)):
         fetch(slot).start()
-    acc[...] = jnp.zeros_like(acc)
+    for panel in range(panels):
+        seen[panel] = 0
+
+    def add(panel, part):
+        columns = pl.ds(pl.multiple_of(panel * tile, tile), tile)
+        acc[:, columns] = jnp.where(seen[panel] > 0, acc[:, columns], 0.0) + part.astype(BF16).astype(F32)
+        seen[panel] = 1
+
+    def use(slot, root):
+        first, second = first_ref[slot], second_ref[slot]
+
+        @pl.when(live_ref[slot] > 0)
+        def _():
+            rows = slab(grads, second * tile, tile)
+            add(first, lax.dot_general(rows, root[...], (((1,), (1,)), ((), ())), preferred_element_type=F32))
+
+        @pl.when((live_ref[slot] > 0) & (first != second))
+        def _():
+            rows = slab(grads, first * tile, tile)
+            add(second, lax.dot_general(rows, root[...], (((1,), (0,)), ((), ())), preferred_element_type=F32))
+
+    def early_step(slot, _):
+        use(slot, early_ref.at[slot])
+        return 0
 
     def step(slot, _):
         fetch(slot).wait()
-        at = lax.rem(slot, depth)
-        first, second = first_ref[slot] * tile, second_ref[slot] * tile
-
-        @pl.when(live_ref[slot] > 0)
-        def _():
-            part = lax.dot_general(
-                slab(grads, second, tile), held[at], (((1,), (1,)), ((), ())), preferred_element_type=F32
-            )
-            acc[:, pl.ds(pl.multiple_of(first, tile), tile)] += part.astype(BF16).astype(F32)
-
-        @pl.when((live_ref[slot] > 0) & (first != second))
-        def _():
-            part = lax.dot_general(
-                slab(grads, first, tile), held[at], (((1,), (0,)), ((), ())), preferred_element_type=F32
-            )
-            acc[:, pl.ds(pl.multiple_of(second, tile), tile)] += part.astype(BF16).astype(F32)
+        use(slot, held.at[lax.rem(slot, depth)])
 
         @pl.when(slot + depth < slots)
         def _():
@@ -75,7 +84,18 @@
 
         return 0
 
-    lax.fori_loop(0, slots, step, 0)
+    lax.fori_loop(0, early, early_step, 0)
+    lax.fori_loop(early, slots, step, 0)
+
+    def clear(panel, _):
+        @pl.when(seen[panel] == 0)
+        def _():
+            columns = pl.ds(pl.multiple_of(panel * tile, tile), tile)
+            acc[:, columns] = jnp.zeros((acc.shape[0], tile), F32)
+
+        return 0
+
+    lax.fori_loop(0, panels, clear, 0)
     at = 0
     for out in outs:
         out[...] = acc[at : at + out.shape[0], :].astype(BF16)
@@ -88,25 +108,50 @@
 HBM_SPEC = pl.BlockSpec(memory_space=pltpu.HBM)
 
 
-def partial_sums(tables, grads, heights, roots):
+def early_kernel(after_ref, root_ref, early_ref, token_ref, sem):
+    copy = pltpu.make_async_copy(root_ref.at[: early_ref.shape[0]], early_ref, sem)
+    copy.start()
+    for i in range(after_ref.shape[0]):
+        token_ref[i] = after_ref[i]
+    copy.wait()
+
+
+def early_roots(after, roots):
+    slots, tile, _ = roots.shape
+    return pl.pallas_call(
+        early_kernel,
+        out_shape=(
+            jax.ShapeDtypeStruct((min(2, slots), tile, tile), BF16),
+            jax.ShapeDtypeStruct(after.shape, after.dtype),
+        ),
+        in_specs=[SMEM_SPEC, ANY_SPEC],
+        out_specs=(VMEM_SPEC, SMEM_SPEC),
+        scratch_shapes=[pltpu.SemaphoreType.DMA],
+        cost_estimate=pl.CostEstimate(flops=0, bytes_accessed=4 * tile * tile, transcendentals=0),
+        compiler_params=pltpu.CompilerParams(vmem_limit_bytes=40 << 20),
+    )(after, roots)
+
+
+def partial_sums(tables, grads, heights, roots, early):
     slots, tile, _ = roots.shape
     rows, order = sum(heights), grads[0].shape[1]
     depth = 2
     return pl.pallas_call(
         functools.partial(part_kernel, len(grads)),
         out_shape=[jax.ShapeDtypeStruct((height, order), BF16) for height in heights],
-        in_specs=[SMEM_SPEC] * 3 + [VMEM_SPEC] * len(grads) + [ANY_SPEC],
+        in_specs=[SMEM_SPEC] * 3 + [VMEM_SPEC] * (len(grads) + 1) + [ANY_SPEC],
         out_specs=[VMEM_SPEC] * len(heights),
         scratch_shapes=[
             pltpu.VMEM((rows, order), F32),
             pltpu.VMEM((depth, tile, tile), BF16),
+            pltpu.SMEM((order // tile,), jnp.int32),
             pltpu.SemaphoreType.DMA((depth,)),
         ],
         compiler_params=pltpu.CompilerParams(vmem_limit_bytes=34 << 20),
         cost_estimate=pl.CostEstimate(
             flops=slots * 4 * rows * tile * tile, bytes_accessed=2 * slots * tile * tile, transcendentals=0
         ),
-    )(*tables, *grads, roots)
+    )(*tables, *grads, early, roots)
 
 
 def stat_kernel(count, base, total, first_ref, second_ref, live_ref, *refs):
@@ -209,7 +254,8 @@
 
     if half % 8:
         everything = lax.all_gather(grad, "row", axis=0, tiled=True)
-        (sums,) = partial_sums(tables, [everything], everything.shape[:1], roots)
+        early, _ = early_roots(tables[0], roots)
+        (sums,) = partial_sums(tables, [everything], everything.shape[:1], roots, early)
         new_stats = update_stats(tables, [everything], stats, 0, slots * CUT, None)
         terms = lax.all_to_all(sums, "row", split_axis=0, concat_axis=0, tiled=True)
         total = jnp.sum(terms.reshape(devices, width, order), axis=0, dtype=F32)
@@ -233,23 +279,28 @@
         high[-step], low[step] = ahead(high[1 - step]), back(low[step - 1])
         if step == 1:
             low[-1], tables = lax.optimization_barrier((low[-1], tables))
+    arrived = [half_rows[sign * (reach - 1)] for half_rows in (low, high) for sign in (-1, 1)]
+    late = lax.optimization_barrier((tables[0], *arrived))[0]
+    early, late = early_roots(late, roots)
+    low[-reach], high[reach], late = lax.optimization_barrier((low[-reach], high[reach], late))
+    tables = late, *tables[1:]
     chunk["low"], chunk["high"] = ahead(low[-reach]), back(high[reach])
-    for step in range(1, reach + 1):
+    other = {0: swap(grad)}
+
+    def join(step, *after):
         halves = low[-step], high[-step], low[step], high[step]
-        if step < reach:
-            halves = lax.optimization_barrier((*halves, low[-reach], high[reach]))[:4]
+        halves = lax.optimization_barrier((*halves, *after))[:4]
         chunk[-step], chunk[step] = jnp.concatenate(halves[:2], 0), jnp.concatenate(halves[2:], 0)
-    near = [k for step in range(reach, 0, -1) for k in (-step, step)]
-    names = ["low", "high", *near, 0]
-    other = {k: swap(chunk[k]) for k in near}
-    other[0] = swap(grad)
-    far = lax.optimization_barrier((chunk["low"], chunk["high"], *other.values()))
-    chunk["low"], chunk["high"] = far[:2]
-    other = dict(zip(other, far[2:]))
+        other[-step], other[step] = swap(chunk[-step]), swap(chunk[step])
+
+    for step in range(1, reach):
+        join(step, low[-reach], high[reach])
     other["low"], other["high"] = swap(chunk["low"]), swap(chunk["high"])
+    join(reach, chunk["low"], chunk["high"])
+    names = ["low", "high", *[k for step in range(reach, 0, -1) for k in (-step, step)], 0]
     rows = [other[k] for k in names] + [chunk[k] for k in names[:-1]] + [low[0], high[0]]
     heights = [other[k].shape[0] for k in names]
-    outs = partial_sums(tables, rows, heights * 2, roots)
+    outs = partial_sums(tables, rows, heights * 2, roots, early)
     other, own = dict(zip(names, outs)), dict(zip(names, outs[len(names) :]))
 
     here = lambda k: own[k].astype(F32) + swap(other[k]).astype(F32)

time: 119 us -> 114 us (0.958)
  waiting for transfers between devices: 40.8 us -> 33.6 us
  Pallas kernels: 44.3 us -> 47.2 us
    ppermute x11, starting transfers between devices: 8.72 us -> 4.02 us  [body(): back = lambda v: lax.ppermute(v, 'row', backward)]
    ppermute x11, waiting for transfers between devices: 21.2 us -> 16.7 us  [body(): back = lambda v: lax.ppermute(v, 'row', backward)]
    ppermute x11, starting transfers between devices: 15.5 us -> 19.8 us  [body(): ahead = lambda v: lax.ppermute(v, 'row', forward)]
    pallas_call x0 -> x1, Pallas kernels: none -> 3.33 us  [early_roots(): pl.pallas_call(early_kernel, out_shape=(jax.ShapeDtypeStruct((min(2, slot...]
    ppermute x11, waiting for transfers between devices: 15.3 us -> 12.4 us  [body(): ahead = lambda v: lax.ppermute(v, 'row', forward)]
  transfers between devices with their start and end apart: 40 -> 40, of which waited for: 21 -> 26; matrix products, arithmetic and copies ran while one was open for 2% -> 2% of each run, Pallas kernels for 25% -> 29%
where the time goes in v3:
time: 114 us
  Pallas kernels  47.2 us (41%)
  waiting for transfers between devices  33.6 us (29%)
  starting transfers between devices  26.9 us (24%)
  other arithmetic  3.63 us (3%)
  local copies, waits for them, and re-layouts  1.31 us (1%)
    pallas_call x4, Pallas kernels, update_stats(): pl.pallas_call(functools.partial(stat_kernel, len(grads), base, length),...  29.9 us
    ppermute x11, starting transfers between devices, body(): ahead = lambda v: lax.ppermute(v, 'row', forward)  19.8 us
    ppermute x11, waiting for transfers between devices, body(): back = lambda v: lax.ppermute(v, 'row', backward)  16.7 us
    pallas_call x1, Pallas kernels, partial_sums(): pl.pallas_call(functools.partial(part_kernel, len(grads)), out_shape=[jax...  14 us
    ppermute x11, waiting for transfers between devices, body(): ahead = lambda v: lax.ppermute(v, 'row', forward)  12.4 us
    ppermute x18, waiting for transfers between devices, body(): lax.ppermute(v, 'row', [(i, i ^ 1) for i in range(devices)])  4.45 us
    ppermute x11, starting transfers between devices, body(): back = lambda v: lax.ppermute(v, 'row', backward)  4.02 us
    pallas_call x1, Pallas kernels, early_roots(): pl.pallas_call(early_kernel, out_shape=(jax.ShapeDtypeStruct((min(2, slot...  3.33 us
  transfers between devices with their start and end apart: 40, of which 26 were waited for; matrix products, arithmetic and copies ran while one was open for 2% of the time, Pallas kernels for 29%

profile of v3, /device:TPU:0, one launch (start us, length us, event | category | flops | bytes accessed | tf_op | source)
XLA Modules:
  0.0 113.5 jit_solution(17512016063908525051)
XLA Ops:
  0.6 1.1 fusion.14
  1.7 3.1 %collective-permute-start = (bf16[8,15360]{1,0:T(8,128)(2,1)S(1)}, bf16[8,15360]{1,0:T(8,128)(2,1)S(1)}, u32[]{:S(2)}, u32[]{:S(2)}) collective-permute-start(bf16[8,15360]{1,0:T(8,128)(2,1)S(1)} %get-tuple-element.133.refs_17_), channel_id=1, source_target_pairs={{0,4},{1,5},{4,8},{5,9},{8,12},{9,13},{12,14},{13,15},{14,10},{15,... | collective-permute-start | bytes 737288 | tf_op jit(solution)/shard_map/ppermute | solution.py:270
  4.8 2.0 %collective-permute-start.8 = (bf16[8,15360]{1,0:T(8,128)(2,1)S(1)}, bf16[8,15360]{1,0:T(8,128)(2,1)S(1)}, u32[]{:S(2)}, u32[]{:S(2)}) collective-permute-start(bf16[8,15360]{1,0:T(8,128)(2,1)S(1)} %get-tuple-element.132.refs_18_), channel_id=1, source_target_pairs={{0,4},{1,5},{4,8},{5,9},{8,12},{9,13},{12,14},{13,15},{14,10},{15,... | collective-permute-start | bytes 737288 | tf_op jit(solution)/shard_map/ppermute | solution.py:270
  6.8 0.8 subtract_add_fusion
  7.6 0.7 compare_convert_fusion.live_ref
  8.3 3.2 %collective-permute-done = bf16[8,15360]{1,0:T(8,128)(2,1)S(1)} collective-permute-done((bf16[8,15360]{1,0:T(8,128)(2,1)S(1)}, bf16[8,15360]{1,0:T(8,128)(2,1)S(1)}, u32[]{:S(2)}, u32[]{:S(2)}) %collective-permute-start) | collective-permute-done | bytes 245792 | tf_op jit(solution)/shard_map/ppermute | solution.py:270
  11.5 2.2 %collective-permute-done.3 = bf16[8,15360]{1,0:T(8,128)(2,1)S(1)} collective-permute-done((bf16[8,15360]{1,0:T(8,128)(2,1)S(1)}, bf16[8,15360]{1,0:T(8,128)(2,1)S(1)}, u32[]{:S(2)}, u32[]{:S(2)}) %collective-permute-start.3) | collective-permute-done | bytes 245792 | tf_op jit(solution)/shard_map/ppermute | solution.py:271
  13.7 2.0 %collective-permute-start.1 = (bf16[8,15360]{1,0:T(8,128)(2,1)S(1)}, bf16[8,15360]{1,0:T(8,128)(2,1)S(1)}, u32[]{:S(2)}, u32[]{:S(2)}) collective-permute-start(bf16[8,15360]{1,0:T(8,128)(2,1)S(1)} %collective-permute-done), channel_id=1, source_target_pairs={{0,4},{1,5},{4,8},{5,9},{8,12},{9,13},{12,14},{13,15},{14,10},{15,... | collective-permute-start | bytes 737288 | tf_op jit(solution)/shard_map/ppermute | solution.py:270
  15.7 1.1 collective-permute-done.8
  16.8 2.1 %collective-permute-start.9 = (bf16[8,15360]{1,0:T(8,128)(2,1)S(1)}, bf16[8,15360]{1,0:T(8,128)(2,1)S(1)}, u32[]{:S(2)}, u32[]{:S(2)}) collective-permute-start(bf16[8,15360]{1,0:T(8,128)(2,1)S(1)} %collective-permute-done.8), channel_id=1, source_target_pairs={{0,4},{1,5},{4,8},{5,9},{8,12},{9,13},{12,14},{13,15},{14,10},{15,... | collective-permute-start | bytes 737288 | tf_op jit(solution)/shard_map/ppermute | solution.py:270
  19.0 5.3 %collective-permute-done.4 = bf16[8,15360]{1,0:T(8,128)(2,1)S(1)} collective-permute-done((bf16[8,15360]{1,0:T(8,128)(2,1)S(1)}, bf16[8,15360]{1,0:T(8,128)(2,1)S(1)}, u32[]{:S(2)}, u32[]{:S(2)}) %collective-permute-start.4) | collective-permute-done | bytes 245792 | tf_op jit(solution)/shard_map/ppermute | solution.py:271
  24.2 2.0 %collective-permute-start.2 = (bf16[8,15360]{1,0:T(8,128)(2,1)S(1)}, bf16[8,15360]{1,0:T(8,128)(2,1)S(1)}, u32[]{:S(2)}, u32[]{:S(2)}) collective-permute-start(bf16[8,15360]{1,0:T(8,128)(2,1)S(1)} %collective-permute-done.1), channel_id=1, source_target_pairs={{0,4},{1,5},{4,8},{5,9},{8,12},{9,13},{12,14},{13,15},{14,10},{15,... | collective-permute-start | bytes 737288 | tf_op jit(solution)/shard_map/ppermute | solution.py:270
  26.3 1.6 %collective-permute-done.9 = bf16[8,15360]{1,0:T(8,128)(2,1)S(1)} collective-permute-done((bf16[8,15360]{1,0:T(8,128)(2,1)S(1)}, bf16[8,15360]{1,0:T(8,128)(2,1)S(1)}, u32[]{:S(2)}, u32[]{:S(2)}) %collective-permute-start.9) | collective-permute-done | bytes 245792 | tf_op jit(solution)/shard_map/ppermute | solution.py:270
  27.9 1.6 %collective-permute-done.7 = bf16[8,15360]{1,0:T(8,128)(2,1)S(1)} collective-permute-done((bf16[8,15360]{1,0:T(8,128)(2,1)S(1)}, bf16[8,15360]{1,0:T(8,128)(2,1)S(1)}, u32[]{:S(2)}, u32[]{:S(2)}) %collective-permute-start.7) | collective-permute-done | bytes 245792 | tf_op jit(solution)/shard_map/ppermute | solution.py:271
  29.5 3.3 %shard_map.59 = (bf16[2,1024,1024]{2,1,0:T(8,128)(2,1)S(1)}, s32[8]{0:T(128)S(1)}) custom-call(s32[8]{0:T(128)S(1)} %get-tuple-element.68.after_ref, bf16[8,1024,1024]{2,1,0:T(8,128)(2,1)} %refs_20_.1), custom_call_target="tpu_custom_call" | custom-call | bytes 4194304 | tf_op jit(solution)/shard_map/pallas_call | solution.py:121
  32.8 1.6 %collective-permute-start.14 = (bf16[8,15360]{1,0:T(8,128)(2,1)S(1)}, bf16[8,15360]{1,0:T(8,128)(2,1)S(1)}, u32[]{:S(2)}, u32[]{:S(2)}) collective-permute-start(bf16[8,15360]{1,0:T(8,128)(2,1)S(1)} %collective-permute-done.9), channel_id=1, source_target_pairs={{0,4},{1,5},{4,8},{5,9},{8,12},{9,13},{12,14},{13,15},{14,10},{15,... | collective-permute-start | bytes 737288 | tf_op jit(solution)/shard_map/ppermute | solution.py:270
  34.5 0.4 collective-permute-start.15
  34.9 1.6 %collective-permute-start.10 = (bf16[8,15360]{1,0:T(8,128)(2,1)S(1)}, bf16[8,15360]{1,0:T(8,128)(2,1)S(1)}, u32[]{:S(2)}, u32[]{:S(2)}) collective-permute-start(bf16[8,15360]{1,0:T(8,128)(2,1)S(1)} %collective-permute-done.2), channel_id=1, source_target_pairs={{0,4},{1,5},{4,8},{5,9},{8,12},{9,13},{12,14},{13,15},{14,10},{15,... | collective-permute-start | bytes 737288 | tf_op jit(solution)/shard_map/ppermute | solution.py:270
  36.5 0.4 collective-permute-start.12
  37.1 3.5 %collective-permute-done.14 = bf16[8,15360]{1,0:T(8,128)(2,1)S(1)} collective-permute-done((bf16[8,15360]{1,0:T(8,128)(2,1)S(1)}, bf16[8,15360]{1,0:T(8,128)(2,1)S(1)}, u32[]{:S(2)}, u32[]{:S(2)}) %collective-permute-start.14) | collective-permute-done | bytes 245792 | tf_op jit(solution)/shard_map/ppermute | solution.py:270
  40.7 1.3 %collective-permute-done.15 = bf16[8,15360]{1,0:T(8,128)(2,1)S(1)} collective-permute-done((bf16[8,15360]{1,0:T(8,128)(2,1)S(1)}, bf16[8,15360]{1,0:T(8,128)(2,1)S(1)}, u32[]{:S(2)}, u32[]{:S(2)}) %collective-permute-start.15) | collective-permute-done | bytes 245792 | tf_op jit(solution)/shard_map/ppermute | solution.py:271
  42.0 1.3 %collective-permute-done.10.refs_9_ = bf16[8,15360]{1,0:T(8,128)(2,1)S(1)} collective-permute-done((bf16[8,15360]{1,0:T(8,128)(2,1)S(1)}, bf16[8,15360]{1,0:T(8,128)(2,1)S(1)}, u32[]{:S(2)}, u32[]{:S(2)}) %collective-permute-start.10) | collective-permute-done | bytes 245792 | tf_op jit(solution)/shard_map/ppermute | solution.py:270
  43.3 1.3 %collective-permute-done.12.refs_10_ = bf16[8,15360]{1,0:T(8,128)(2,1)S(1)} collective-permute-done((bf16[8,15360]{1,0:T(8,128)(2,1)S(1)}, bf16[8,15360]{1,0:T(8,128)(2,1)S(1)}, u32[]{:S(2)}, u32[]{:S(2)}) %collective-permute-start.12) | collective-permute-done | bytes 245792 | tf_op jit(solution)/shard_map/ppermute | solution.py:271
  44.7 0.5 collective-permute-start.13
  45.4 0.8 collective-permute-done.11.refs_0_
  47.3 0.8 collective-permute-done.18.refs_4_
  48.1 0.7 collective-permute-done.17.refs_3_
  48.8 0.7 collective-permute-done.16.refs_2_
  49.5 14.0 %shard_map.60 = (bf16[8,15360]{1,0:T(8,128)(2,1)S(1)}, bf16[8,15360]{1,0:T(8,128)(2,1)S(1)}, bf16[16,15360]{1,0:T(8,128)(2,1)S(1)}, bf16[16,15360]{1,0:T(8,128)(...) custom-call(s32[8]{0:T(128)S(1)} %get-tuple-element.121.first_ref, ...), custom_call_target="tpu_custom_call" | custom-call | flops 8589934592 | bytes 16777216 | tf_op jit(solution)/shard_map/pallas_call | solution.py:139
  64.2 0.9 collective-permute-done.26
  65.5 1.8 %collective-permute-start.29 = (bf16[8,15360]{1,0:T(8,128)(2,1)S(1)}, bf16[8,15360]{1,0:T(8,128)(2,1)S(1)}, u32[]{:S(2)}, u32[]{:S(2)}) collective-permute-start(bf16[8,15360]{1,0:T(8,128)(2,1)S(1)} %add_convert_fusion.7), channel_id=1, source_target_pairs={{0,4},{1,5},{4,8},{5,9},{8,12},{9,13},{12,14},{13,15},{14,10},{15,... | collective-permute-start | bytes 737288 | tf_op jit(solution)/shard_map/ppermute | solution.py:270
  67.4 5.7 %shard_map.61.refs_20_ = f32[8,1024,1024]{2,1,0:T(8,128)} custom-call(s32[8]{0:T(128)S(1)} %get-tuple-element.121.first_ref, s32[8]{0:T(128)S(1)} %get-tuple-element.122.second_ref, s32[8]{0:T(128)S(1)} %compare_convert_fusion.live_ref, bf16[8,15360]{1,0:T(8,128)(2,1)S(1)} %collective-permute-done.11.refs_0_, ...), custom_call_target="tpu_custom_call" | custom-call | flops 671088640 | bytes 10485760 | tf_op jit(solution)/shard_map/pallas_call | solution.py:228
  73.8 0.5 collective-permute-start.30
  74.4 1.7 %collective-permute-start.32 = (bf16[16,15360]{1,0:T(8,128)(2,1)S(1)}, bf16[16,15360]{1,0:T(8,128)(2,1)S(1)}, u32[]{:S(2)}, u32[]{:S(2)}) collective-permute-start(bf16[16,15360]{1,0:T(8,128)(2,1)S(1)} %add_convert_fusion.5), channel_id=1, source_target_pairs={{0,4},{1,5},{4,8},{5,9},{8,12},{9,13},{12,14},{13,15},{14,10},{15,... | collective-permute-start | bytes 1474568 | tf_op jit(solution)/shard_map/ppermute | solution.py:270
  76.0 0.5 collective-permute-start.34
  76.6 8.1 %shard_map.62.refs_20_ = f32[8,1024,1024]{2,1,0:T(8,128)} custom-call(s32[8]{0:T(128)S(1)} %get-tuple-element.121.first_ref, s32[8]{0:T(128)S(1)} %get-tuple-element.122.second_ref, s32[8]{0:T(128)S(1)} %compare_convert_fusion.live_ref, bf16[8,15360]{1,0:T(8,128)(2,1)S(1)} %collective-permute-done.11.refs_0_, ...), custom_call_target="tpu_custom_call", output_to_operand_aliasing={{}: (23, {})} | custom-call | flops 1207959552 | bytes 18874368 | tf_op jit(solution)/shard_map/pallas_call | solution.py:228
  84.6 2.3 %collective-permute-done.30 = bf16[16,15360]{1,0:T(8,128)(2,1)S(1)} collective-permute-done((bf16[16,15360]{1,0:T(8,128)(2,1)S(1)}, bf16[16,15360]{1,0:T(8,128)(2,1)S(1)}, u32[]{:S(2)}, u32[]{:S(2)}) %collective-permute-start.30) | collective-permute-done | bytes 491552 | tf_op jit(solution)/shard_map/ppermute | solution.py:271
  87.3 0.9 collective-permute-start.33
  88.5 1.2 %collective-permute-start.35 = (bf16[16,15360]{1,0:T(8,128)(2,1)S(1)}, bf16[16,15360]{1,0:T(8,128)(2,1)S(1)}, u32[]{:S(2)}, u32[]{:S(2)}) collective-permute-start(bf16[16,15360]{1,0:T(8,128)(2,1)S(1)} %add_convert_fusion.3), channel_id=1, source_target_pairs={{0,4},{1,5},{4,8},{5,9},{8,12},{9,13},{12,14},{13,15},{14,10},{15,... | collective-permute-start | bytes 1474568 | tf_op jit(solution)/shard_map/ppermute | solution.py:270
  89.7 0.5 collective-permute-start.37
  90.2 8.1 %shard_map.63.refs_20_ = f32[8,1024,1024]{2,1,0:T(8,128)} custom-call(s32[8]{0:T(128)S(1)} %get-tuple-element.121.first_ref, s32[8]{0:T(128)S(1)} %get-tuple-element.122.second_ref, s32[8]{0:T(128)S(1)} %compare_convert_fusion.live_ref, bf16[8,15360]{1,0:T(8,128)(2,1)S(1)} %collective-permute-done.11.refs_0_, ...), custom_call_target="tpu_custom_call", output_to_operand_aliasing={{}: (23, {})} | custom-call | flops 1207959552 | bytes 18874368 | tf_op jit(solution)/shard_map/pallas_call | solution.py:228
  98.2 1.2 %collective-permute-done.33 = bf16[16,15360]{1,0:T(8,128)(2,1)S(1)} collective-permute-done((bf16[16,15360]{1,0:T(8,128)(2,1)S(1)}, bf16[16,15360]{1,0:T(8,128)(2,1)S(1)}, u32[]{:S(2)}, u32[]{:S(2)}) %collective-permute-start.33) | collective-permute-done | bytes 491552 | tf_op jit(solution)/shard_map/ppermute | solution.py:271
  99.9 1.5 %collective-permute-start.36 = (bf16[16,15360]{1,0:T(8,128)(2,1)S(1)}, bf16[16,15360]{1,0:T(8,128)(2,1)S(1)}, u32[]{:S(2)}, u32[]{:S(2)}) collective-permute-start(bf16[16,15360]{1,0:T(8,128)(2,1)S(1)} %add_convert_fusion.2), channel_id=1, source_target_pairs={{4,0},{5,1},{8,4},{9,5},{12,8},{13,9},{14,12},{15,13},{10,14},{11,... | collective-permute-start | bytes 1474568 | tf_op jit(solution)/shard_map/ppermute | solution.py:271
  101.6 0.6 collective-permute-start.38
  102.2 8.1 %shard_map.64 = f32[8,1024,1024]{2,1,0:T(8,128)} custom-call(s32[8]{0:T(128)S(1)} %get-tuple-element.121.first_ref, s32[8]{0:T(128)S(1)} %get-tuple-element.122.second_ref, s32[8]{0:T(128)S(1)} %compare_convert_fusion.live_ref, bf16[8,15360]{1,0:T(8,128)(2,1)S(1)} %collective-permute-done.11.refs_0_, ...), custom_call_target="tpu_custom_call", output_to_operand_aliasing={{}: (23, {})} | custom-call | flops 1207959552 | bytes 18874368 | tf_op jit(solution)/shard_map/pallas_call | solution.py:228
  110.3 1.4 %collective-permute-done.36 = bf16[16,15360]{1,0:T(8,128)(2,1)S(1)} collective-permute-done((bf16[16,15360]{1,0:T(8,128)(2,1)S(1)}, bf16[16,15360]{1,0:T(8,128)(2,1)S(1)}, u32[]{:S(2)}, u32[]{:S(2)}) %collective-permute-start.36) | collective-permute-done | bytes 491552 | tf_op jit(solution)/shard_map/ppermute | solution.py:271
  111.6 0.8 collective-permute-done.38
  112.5 1.0 add_convert_fusion
  (62 shorter events, 4.7 us)
Async XLA Ops:
  1.7 9.8 %collective-permute-start = (bf16[8,15360]{1,0:T(8,128)(2,1)S(1)}, bf16[8,15360]{1,0:T(8,128)(2,1)S(1)}, u32[]{:S(2)}, u32[]{:S(2)}) collective-permute-start(bf16[8,15360]{1,0:T(8,128)(2,1)S(1)} %get-tuple-element.133.refs_17_), channel_id=1, source_target_pairs={{0,4},{1,5},{4,8},{5,9},{8,12},{9,13},{12,14},{13,15},{14,10},{15,... | collective-permute-start | bytes 737288 | tf_op jit(solution)/shard_map/ppermute | solution.py:270
  4.8 8.9 %collective-permute-start.3 = (bf16[8,15360]{1,0:T(8,128)(2,1)S(1)}, bf16[8,15360]{1,0:T(8,128)(2,1)S(1)}, u32[]{:S(2)}, u32[]{:S(2)}) collective-permute-start(bf16[8,15360]{1,0:T(8,128)(2,1)S(1)} %get-tuple-element.132.refs_18_), channel_id=1, source_target_pairs={{4,0},{5,1},{8,4},{9,5},{12,8},{13,9},{14,12},{15,13},{10,14},{11,... | collective-permute-start | bytes 737288 | tf_op jit(solution)/shard_map/ppermute | solution.py:271
  4.8 12.0 %collective-permute-start.8 = (bf16[8,15360]{1,0:T(8,128)(2,1)S(1)}, bf16[8,15360]{1,0:T(8,128)(2,1)S(1)}, u32[]{:S(2)}, u32[]{:S(2)}) collective-permute-start(bf16[8,15360]{1,0:T(8,128)(2,1)S(1)} %get-tuple-element.132.refs_18_), channel_id=1, source_target_pairs={{0,4},{1,5},{4,8},{5,9},{8,12},{9,13},{12,14},{13,15},{14,10},{15,... | collective-permute-start | bytes 737288 | tf_op jit(solution)/shard_map/ppermute | solution.py:270
  6.8 12.1 %collective-permute-start.6 = (bf16[8,15360]{1,0:T(8,128)(2,1)S(1)}, bf16[8,15360]{1,0:T(8,128)(2,1)S(1)}, u32[]{:S(2)}, u32[]{:S(2)}) collective-permute-start(bf16[8,15360]{1,0:T(8,128)(2,1)S(1)} %get-tuple-element.133.refs_17_), channel_id=1, source_target_pairs={{4,0},{5,1},{8,4},{9,5},{12,8},{13,9},{14,12},{15,13},{10,14},{11,... | collective-permute-start | bytes 737288 | tf_op jit(solution)/shard_map/ppermute | solution.py:271
  13.7 10.5 %collective-permute-start.4 = (bf16[8,15360]{1,0:T(8,128)(2,1)S(1)}, bf16[8,15360]{1,0:T(8,128)(2,1)S(1)}, u32[]{:S(2)}, u32[]{:S(2)}) collective-permute-start(bf16[8,15360]{1,0:T(8,128)(2,1)S(1)} %collective-permute-done.3), channel_id=1, source_target_pairs={{4,0},{5,1},{8,4},{9,5},{12,8},{13,9},{14,12},{15,13},{10,14},{11,... | collective-permute-start | bytes 737288 | tf_op jit(solution)/shard_map/ppermute | solution.py:271
  13.7 10.5 %collective-permute-start.1 = (bf16[8,15360]{1,0:T(8,128)(2,1)S(1)}, bf16[8,15360]{1,0:T(8,128)(2,1)S(1)}, u32[]{:S(2)}, u32[]{:S(2)}) collective-permute-start(bf16[8,15360]{1,0:T(8,128)(2,1)S(1)} %collective-permute-done), channel_id=1, source_target_pairs={{0,4},{1,5},{4,8},{5,9},{8,12},{9,13},{12,14},{13,15},{14,10},{15,... | collective-permute-start | bytes 737288 | tf_op jit(solution)/shard_map/ppermute | solution.py:270
  16.8 11.1 %collective-permute-start.9 = (bf16[8,15360]{1,0:T(8,128)(2,1)S(1)}, bf16[8,15360]{1,0:T(8,128)(2,1)S(1)}, u32[]{:S(2)}, u32[]{:S(2)}) collective-permute-start(bf16[8,15360]{1,0:T(8,128)(2,1)S(1)} %collective-permute-done.8), channel_id=1, source_target_pairs={{0,4},{1,5},{4,8},{5,9},{8,12},{9,13},{12,14},{13,15},{14,10},{15,... | collective-permute-start | bytes 737288 | tf_op jit(solution)/shard_map/ppermute | solution.py:270
  19.0 10.5 %collective-permute-start.7 = (bf16[8,15360]{1,0:T(8,128)(2,1)S(1)}, bf16[8,15360]{1,0:T(8,128)(2,1)S(1)}, u32[]{:S(2)}, u32[]{:S(2)}) collective-permute-start(bf16[8,15360]{1,0:T(8,128)(2,1)S(1)} %collective-permute-done.6), channel_id=1, source_target_pairs={{4,0},{5,1},{8,4},{9,5},{12,8},{13,9},{14,12},{15,13},{10,14},{11,... | collective-permute-start | bytes 737288 | tf_op jit(solution)/shard_map/ppermute | solution.py:271
  24.2 10.7 %collective-permute-start.5 = (bf16[8,15360]{1,0:T(8,128)(2,1)S(1)}, bf16[8,15360]{1,0:T(8,128)(2,1)S(1)}, u32[]{:S(2)}, u32[]{:S(2)}) collective-permute-start(bf16[8,15360]{1,0:T(8,128)(2,1)S(1)} %collective-permute-done.4), channel_id=1, source_target_pairs={{4,0},{5,1},{8,4},{9,5},{12,8},{13,9},{14,12},{15,13},{10,14},{11,... | collective-permute-start | bytes 737288 | tf_op jit(solution)/shard_map/ppermute | solution.py:271
  24.2 10.7 %collective-permute-start.2 = (bf16[8,15360]{1,0:T(8,128)(2,1)S(1)}, bf16[8,15360]{1,0:T(8,128)(2,1)S(1)}, u32[]{:S(2)}, u32[]{:S(2)}) collective-permute-start(bf16[8,15360]{1,0:T(8,128)(2,1)S(1)} %collective-permute-done.1), channel_id=1, source_target_pairs={{0,4},{1,5},{4,8},{5,9},{8,12},{9,13},{12,14},{13,15},{14,10},{15,... | collective-permute-start | bytes 737288 | tf_op jit(solution)/shard_map/ppermute | solution.py:270
  26.3 19.0 %collective-permute-start.22 = (bf16[16,15360]{1,0:T(8,128)(2,1)}, bf16[16,15360]{1,0:T(8,128)(2,1)S(1)}, u32[]{:S(2)}, u32[]{:S(2)}) collective-permute-start(bf16[16,15360]{1,0:T(8,128)(2,1)} %param.4), channel_id=1, source_target_pairs={{0,1},{1,0},{2,3},{3,2},{4,5},{5,4},{6,7},{7,6},{8,9},{9,8},{10,11... | collective-permute-start | bytes 1474568 | tf_op jit(solution)/shard_map/ppermute | solution.py:272
  32.8 7.8 %collective-permute-start.14 = (bf16[8,15360]{1,0:T(8,128)(2,1)S(1)}, bf16[8,15360]{1,0:T(8,128)(2,1)S(1)}, u32[]{:S(2)}, u32[]{:S(2)}) collective-permute-start(bf16[8,15360]{1,0:T(8,128)(2,1)S(1)} %collective-permute-done.9), channel_id=1, source_target_pairs={{0,4},{1,5},{4,8},{5,9},{8,12},{9,13},{12,14},{13,15},{14,10},{15,... | collective-permute-start | bytes 737288 | tf_op jit(solution)/shard_map/ppermute | solution.py:270
  34.5 7.5 %collective-permute-start.15 = (bf16[8,15360]{1,0:T(8,128)(2,1)S(1)}, bf16[8,15360]{1,0:T(8,128)(2,1)S(1)}, u32[]{:S(2)}, u32[]{:S(2)}) collective-permute-start(bf16[8,15360]{1,0:T(8,128)(2,1)S(1)} %collective-permute-done.7), channel_id=1, source_target_pairs={{4,0},{5,1},{8,4},{9,5},{12,8},{13,9},{14,12},{15,13},{10,14},{11,... | collective-permute-start | bytes 737288 | tf_op jit(solution)/shard_map/ppermute | solution.py:271
  34.9 8.4 %collective-permute-start.10 = (bf16[8,15360]{1,0:T(8,128)(2,1)S(1)}, bf16[8,15360]{1,0:T(8,128)(2,1)S(1)}, u32[]{:S(2)}, u32[]{:S(2)}) collective-permute-start(bf16[8,15360]{1,0:T(8,128)(2,1)S(1)} %collective-permute-done.2), channel_id=1, source_target_pairs={{0,4},{1,5},{4,8},{5,9},{8,12},{9,13},{12,14},{13,15},{14,10},{15,... | collective-permute-start | bytes 737288 | tf_op jit(solution)/shard_map/ppermute | solution.py:270
  36.5 8.1 %collective-permute-start.12 = (bf16[8,15360]{1,0:T(8,128)(2,1)S(1)}, bf16[8,15360]{1,0:T(8,128)(2,1)S(1)}, u32[]{:S(2)}, u32[]{:S(2)}) collective-permute-start(bf16[8,15360]{1,0:T(8,128)(2,1)S(1)} %collective-permute-done.5), channel_id=1, source_target_pairs={{4,0},{5,1},{8,4},{9,5},{12,8},{13,9},{14,12},{15,13},{10,14},{11,... | collective-permute-start | bytes 737288 | tf_op jit(solution)/shard_map/ppermute | solution.py:271
  40.7 6.1 %collective-permute-start.21 = (bf16[16,15360]{1,0:T(8,128)(2,1)S(1)}, bf16[16,15360]{1,0:T(8,128)(2,1)S(1)}, u32[]{:S(2)}, u32[]{:S(2)}) collective-permute-start(bf16[16,15360]{1,0:T(8,128)(2,1)S(1)} %constant_dynamic-update-slice_fusion.10.refs_16_), channel_id=1, source_target_pairs={{0,1},{1,0},{2,3},{3,2},{4,5},{5,4},{6,7},{7,6},{8,9},{9,8},{10,11... | collective-permute-start | bytes 1474568 | tf_op jit(solution)/shard_map/ppermute | solution.py:272
  41.9 5.2 %collective-permute-start.19 = (bf16[16,15360]{1,0:T(8,128)(2,1)S(1)}, bf16[16,15360]{1,0:T(8,128)(2,1)S(1)}, u32[]{:S(2)}, u32[]{:S(2)}) collective-permute-start(bf16[16,15360]{1,0:T(8,128)(2,1)S(1)} %constant_dynamic-update-slice_fusion.6.refs_14_), channel_id=1, source_target_pairs={{0,1},{1,0},{2,3},{3,2},{4,5},{5,4},{6,7},{7,6},{8,9},{9,8},{10,11... | collective-permute-start | bytes 1474568 | tf_op jit(solution)/shard_map/ppermute | solution.py:272
  44.7 1.6 %collective-permute-start.11 = (bf16[8,15360]{1,0:T(8,128)(2,1)S(1)}, bf16[8,15360]{1,0:T(8,128)(2,1)S(1)}, u32[]{:S(2)}, u32[]{:S(2)}) collective-permute-start(bf16[8,15360]{1,0:T(8,128)(2,1)S(1)} %collective-permute-done.10.refs_9_), channel_id=1, source_target_pairs={{0,1},{1,0},{2,3},{3,2},{4,5},{5,4},{6,7},{7,6},{8,9},{9,8},{10,11... | collective-permute-start | bytes 737288 | tf_op jit(solution)/shard_map/ppermute | solution.py:272
  44.7 1.9 %collective-permute-start.13 = (bf16[8,15360]{1,0:T(8,128)(2,1)S(1)}, bf16[8,15360]{1,0:T(8,128)(2,1)S(1)}, u32[]{:S(2)}, u32[]{:S(2)}) collective-permute-start(bf16[8,15360]{1,0:T(8,128)(2,1)S(1)} %collective-permute-done.12.refs_10_), channel_id=1, source_target_pairs={{0,1},{1,0},{2,3},{3,2},{4,5},{5,4},{6,7},{7,6},{8,9},{9,8},{10,11... | collective-permute-start | bytes 737288 | tf_op jit(solution)/shard_map/ppermute | solution.py:272
  45.3 2.0 %collective-permute-start.20 = (bf16[16,15360]{1,0:T(8,128)(2,1)S(1)}, bf16[16,15360]{1,0:T(8,128)(2,1)S(1)}, u32[]{:S(2)}, u32[]{:S(2)}) collective-permute-start(bf16[16,15360]{1,0:T(8,128)(2,1)S(1)} %constant_dynamic-update-slice_fusion.8.refs_15_), channel_id=1, source_target_pairs={{0,1},{1,0},{2,3},{3,2},{4,5},{5,4},{6,7},{7,6},{8,9},{9,8},{10,11... | collective-permute-start | bytes 1474568 | tf_op jit(solution)/shard_map/ppermute | solution.py:272
  46.2 1.9 %collective-permute-start.18 = (bf16[16,15360]{1,0:T(8,128)(2,1)S(1)}, bf16[16,15360]{1,0:T(8,128)(2,1)S(1)}, u32[]{:S(2)}, u32[]{:S(2)}) collective-permute-start(bf16[16,15360]{1,0:T(8,128)(2,1)S(1)} %constant_dynamic-update-slice_fusion.4.refs_13_), channel_id=1, source_target_pairs={{0,1},{1,0},{2,3},{3,2},{4,5},{5,4},{6,7},{7,6},{8,9},{9,8},{10,11... | collective-permute-start | bytes 1474568 | tf_op jit(solution)/shard_map/ppermute | solution.py:272
  46.6 2.2 %collective-permute-start.17 = (bf16[16,15360]{1,0:T(8,128)(2,1)S(1)}, bf16[16,15360]{1,0:T(8,128)(2,1)S(1)}, u32[]{:S(2)}, u32[]{:S(2)}) collective-permute-start(bf16[16,15360]{1,0:T(8,128)(2,1)S(1)} %constant_dynamic-update-slice_fusion.2.refs_12_), channel_id=1, source_target_pairs={{0,1},{1,0},{2,3},{3,2},{4,5},{5,4},{6,7},{7,6},{8,9},{9,8},{10,11... | collective-permute-start | bytes 1474568 | tf_op jit(solution)/shard_map/ppermute | solution.py:272
  46.8 2.8 %collective-permute-start.16 = (bf16[16,15360]{1,0:T(8,128)(2,1)S(1)}, bf16[16,15360]{1,0:T(8,128)(2,1)S(1)}, u32[]{:S(2)}, u32[]{:S(2)}) collective-permute-start(bf16[16,15360]{1,0:T(8,128)(2,1)S(1)} %constant_dynamic-update-slice_fusion.refs_11_), channel_id=1, source_target_pairs={{0,1},{1,0},{2,3},{3,2},{4,5},{5,4},{6,7},{7,6},{8,9},{9,8},{10,11... | collective-permute-start | bytes 1474568 | tf_op jit(solution)/shard_map/ppermute | solution.py:272
  63.5 1.6 %collective-permute-start.26 = (bf16[8,15360]{1,0:T(8,128)(2,1)S(1)}, bf16[8,15360]{1,0:T(8,128)(2,1)S(1)}, u32[]{:S(2)}, u32[]{:S(2)}) collective-permute-start(bf16[8,15360]{1,0:T(8,128)(2,1)S(1)} %get-tuple-element.95), channel_id=1, source_target_pairs={{0,1},{1,0},{2,3},{3,2},{4,5},{5,4},{6,7},{7,6},{8,9},{9,8},{10,11... | collective-permute-start | bytes 737288 | tf_op jit(solution)/shard_map/ppermute | solution.py:272
  63.7 1.8 %collective-permute-start.28 = (bf16[8,15360]{1,0:T(8,128)(2,1)S(1)}, bf16[8,15360]{1,0:T(8,128)(2,1)S(1)}, u32[]{:S(2)}, u32[]{:S(2)}) collective-permute-start(bf16[8,15360]{1,0:T(8,128)(2,1)S(1)} %get-tuple-element.97), channel_id=1, source_target_pairs={{0,1},{1,0},{2,3},{3,2},{4,5},{5,4},{6,7},{7,6},{8,9},{9,8},{10,11... | collective-permute-start | bytes 737288 | tf_op jit(solution)/shard_map/ppermute | solution.py:272
  64.1 9.5 %collective-permute-start.25 = (bf16[16,15360]{1,0:T(8,128)(2,1)S(1)}, bf16[16,15360]{1,0:T(8,128)(2,1)S(1)}, u32[]{:S(2)}, u32[]{:S(2)}) collective-permute-start(bf16[16,15360]{1,0:T(8,128)(2,1)S(1)} %get-tuple-element.93), channel_id=1, source_target_pairs={{0,1},{1,0},{2,3},{3,2},{4,5},{5,4},{6,7},{7,6},{8,9},{9,8},{10,11... | collective-permute-start | bytes 1474568 | tf_op jit(solution)/shard_map/ppermute | solution.py:272
  65.2 8.0 %collective-permute-start.27 = (bf16[8,15360]{1,0:T(8,128)(2,1)S(1)}, bf16[8,15360]{1,0:T(8,128)(2,1)S(1)}, u32[]{:S(2)}, u32[]{:S(2)}) collective-permute-start(bf16[8,15360]{1,0:T(8,128)(2,1)S(1)} %add_convert_fusion.8), channel_id=1, source_target_pairs={{4,0},{5,1},{8,4},{9,5},{12,8},{13,9},{14,12},{15,13},{10,14},{11,... | collective-permute-start | bytes 737288 | tf_op jit(solution)/shard_map/ppermute | solution.py:271
  65.5 8.1 %collective-permute-start.29 = (bf16[8,15360]{1,0:T(8,128)(2,1)S(1)}, bf16[8,15360]{1,0:T(8,128)(2,1)S(1)}, u32[]{:S(2)}, u32[]{:S(2)}) collective-permute-start(bf16[8,15360]{1,0:T(8,128)(2,1)S(1)} %add_convert_fusion.7), channel_id=1, source_target_pairs={{0,4},{1,5},{4,8},{5,9},{8,12},{9,13},{12,14},{13,15},{14,10},{15,... | collective-permute-start | bytes 737288 | tf_op jit(solution)/shard_map/ppermute | solution.py:270
  67.4 6.9 %collective-permute-start.31 = (bf16[16,15360]{1,0:T(8,128)(2,1)S(1)}, bf16[16,15360]{1,0:T(8,128)(2,1)S(1)}, u32[]{:S(2)}, u32[]{:S(2)}) collective-permute-start(bf16[16,15360]{1,0:T(8,128)(2,1)S(1)} %get-tuple-element.103), channel_id=1, source_target_pairs={{0,1},{1,0},{2,3},{3,2},{4,5},{5,4},{6,7},{7,6},{8,9},{9,8},{10,11... | collective-permute-start | bytes 1474568 | tf_op jit(solution)/shard_map/ppermute | solution.py:272
  73.8 13.2 %collective-permute-start.30 = (bf16[16,15360]{1,0:T(8,128)(2,1)S(1)}, bf16[16,15360]{1,0:T(8,128)(2,1)S(1)}, u32[]{:S(2)}, u32[]{:S(2)}) collective-permute-start(bf16[16,15360]{1,0:T(8,128)(2,1)S(1)} %add_convert_fusion.6), channel_id=1, source_target_pairs={{4,0},{5,1},{8,4},{9,5},{12,8},{13,9},{14,12},{15,13},{10,14},{11,... | collective-permute-start | bytes 1474568 | tf_op jit(solution)/shard_map/ppermute | solution.py:271
  74.4 12.8 %collective-permute-start.32 = (bf16[16,15360]{1,0:T(8,128)(2,1)S(1)}, bf16[16,15360]{1,0:T(8,128)(2,1)S(1)}, u32[]{:S(2)}, u32[]{:S(2)}) collective-permute-start(bf16[16,15360]{1,0:T(8,128)(2,1)S(1)} %add_convert_fusion.5), channel_id=1, source_target_pairs={{0,4},{1,5},{4,8},{5,9},{8,12},{9,13},{12,14},{13,15},{14,10},{15,... | collective-permute-start | bytes 1474568 | tf_op jit(solution)/shard_map/ppermute | solution.py:270
  76.0 11.1 %collective-permute-start.24 = (bf16[16,15360]{1,0:T(8,128)(2,1)S(1)}, bf16[16,15360]{1,0:T(8,128)(2,1)S(1)}, u32[]{:S(2)}, u32[]{:S(2)}) collective-permute-start(bf16[16,15360]{1,0:T(8,128)(2,1)S(1)} %get-tuple-element.91), channel_id=1, source_target_pairs={{0,1},{1,0},{2,3},{3,2},{4,5},{5,4},{6,7},{7,6},{8,9},{9,8},{10,11... | collective-permute-start | bytes 1474568 | tf_op jit(solution)/shard_map/ppermute | solution.py:272
  76.0 12.2 %collective-permute-start.34 = (bf16[16,15360]{1,0:T(8,128)(2,1)S(1)}, bf16[16,15360]{1,0:T(8,128)(2,1)S(1)}, u32[]{:S(2)}, u32[]{:S(2)}) collective-permute-start(bf16[16,15360]{1,0:T(8,128)(2,1)S(1)} %get-tuple-element.111), channel_id=1, source_target_pairs={{0,1},{1,0},{2,3},{3,2},{4,5},{5,4},{6,7},{7,6},{8,9},{9,8},{10,11... | collective-permute-start | bytes 1474568 | tf_op jit(solution)/shard_map/ppermute | solution.py:272
  87.3 12.1 %collective-permute-start.33 = (bf16[16,15360]{1,0:T(8,128)(2,1)S(1)}, bf16[16,15360]{1,0:T(8,128)(2,1)S(1)}, u32[]{:S(2)}, u32[]{:S(2)}) collective-permute-start(bf16[16,15360]{1,0:T(8,128)(2,1)S(1)} %add_convert_fusion.4), channel_id=1, source_target_pairs={{4,0},{5,1},{8,4},{9,5},{12,8},{13,9},{14,12},{15,13},{10,14},{11,... | collective-permute-start | bytes 1474568 | tf_op jit(solution)/shard_map/ppermute | solution.py:271
  88.5 11.2 %collective-permute-start.35 = (bf16[16,15360]{1,0:T(8,128)(2,1)S(1)}, bf16[16,15360]{1,0:T(8,128)(2,1)S(1)}, u32[]{:S(2)}, u32[]{:S(2)}) collective-permute-start(bf16[16,15360]{1,0:T(8,128)(2,1)S(1)} %add_convert_fusion.3), channel_id=1, source_target_pairs={{0,4},{1,5},{4,8},{5,9},{8,12},{9,13},{12,14},{13,15},{14,10},{15,... | collective-permute-start | bytes 1474568 | tf_op jit(solution)/shard_map/ppermute | solution.py:270
  89.7 10.0 %collective-permute-start.23 = (bf16[16,15360]{1,0:T(8,128)(2,1)S(1)}, bf16[16,15360]{1,0:T(8,128)(2,1)S(1)}, u32[]{:S(2)}, u32[]{:S(2)}) collective-permute-start(bf16[16,15360]{1,0:T(8,128)(2,1)S(1)} %get-tuple-element.89), channel_id=1, source_target_pairs={{0,1},{1,0},{2,3},{3,2},{4,5},{5,4},{6,7},{7,6},{8,9},{9,8},{10,11... | collective-permute-start | bytes 1474568 | tf_op jit(solution)/shard_map/ppermute | solution.py:272
  89.7 11.7 %collective-permute-start.37 = (bf16[16,15360]{1,0:T(8,128)(2,1)S(1)}, bf16[16,15360]{1,0:T(8,128)(2,1)S(1)}, u32[]{:S(2)}, u32[]{:S(2)}) collective-permute-start(bf16[16,15360]{1,0:T(8,128)(2,1)S(1)} %get-tuple-element.119), channel_id=1, source_target_pairs={{0,1},{1,0},{2,3},{3,2},{4,5},{5,4},{6,7},{7,6},{8,9},{9,8},{10,11... | collective-permute-start | bytes 1474568 | tf_op jit(solution)/shard_map/ppermute | solution.py:272
  99.9 11.8 %collective-permute-start.36 = (bf16[16,15360]{1,0:T(8,128)(2,1)S(1)}, bf16[16,15360]{1,0:T(8,128)(2,1)S(1)}, u32[]{:S(2)}, u32[]{:S(2)}) collective-permute-start(bf16[16,15360]{1,0:T(8,128)(2,1)S(1)} %add_convert_fusion.2), channel_id=1, source_target_pairs={{4,0},{5,1},{8,4},{9,5},{12,8},{13,9},{14,12},{15,13},{10,14},{11,... | collective-permute-start | bytes 1474568 | tf_op jit(solution)/shard_map/ppermute | solution.py:271
  101.6 10.9 %collective-permute-start.38 = (bf16[16,15360]{1,0:T(8,128)(2,1)S(1)}, bf16[16,15360]{1,0:T(8,128)(2,1)S(1)}, u32[]{:S(2)}, u32[]{:S(2)}) collective-permute-start(bf16[16,15360]{1,0:T(8,128)(2,1)S(1)} %add_convert_fusion.1), channel_id=1, source_target_pairs={{0,4},{1,5},{4,8},{5,9},{8,12},{9,13},{12,14},{13,15},{14,10},{15,... | collective-permute-start | bytes 1474568 | tf_op jit(solution)/shard_map/ppermute | solution.py:270
  102.2 10.3 %collective-permute-start.39 = (bf16[16,15360]{1,0:T(8,128)(2,1)S(1)}, bf16[16,15360]{1,0:T(8,128)(2,1)S(1)}, u32[]{:S(2)}, u32[]{:S(2)}) collective-permute-start(bf16[16,15360]{1,0:T(8,128)(2,1)S(1)} %get-tuple-element.127), channel_id=1, source_target_pairs={{0,1},{1,0},{2,3},{3,2},{4,5},{5,4},{6,7},{7,6},{8,9},{9,8},{10,11... | collective-permute-start | bytes 1474568 | tf_op jit(solution)/shard_map/ppermute | solution.py:272

commit v4 on v3

--- a/solution.py
+++ b/solution.py
@@ -289,14 +289,17 @@
 
     def join(step, *after):
         halves = low[-step], high[-step], low[step], high[step]
-        halves = lax.optimization_barrier((*halves, *after))[:4]
+        if after:
+            halves = lax.optimization_barrier((*halves, *after))[:4]
         chunk[-step], chunk[step] = jnp.concatenate(halves[:2], 0), jnp.concatenate(halves[2:], 0)
         other[-step], other[step] = swap(chunk[-step]), swap(chunk[step])
 
     for step in range(1, reach):
         join(step, low[-reach], high[reach])
+    join(reach)
+    last = lax.optimization_barrier((chunk["low"], chunk["high"], other[-reach], other[reach]))
+    chunk["low"], chunk["high"], other[-reach], other[reach] = last
     other["low"], other["high"] = swap(chunk["low"]), swap(chunk["high"])
-    join(reach, chunk["low"], chunk["high"])
     names = ["low", "high", *[k for step in range(reach, 0, -1) for k in (-step, step)], 0]
     rows = [other[k] for k in names] + [chunk[k] for k in names[:-1]] + [low[0], high[0]]
     heights = [other[k].shape[0] for k in names]

time: 114 us -> 114 us (level)
  starting transfers between devices: 26.9 us -> 28.7 us
  Pallas kernels: 47.2 us -> 46 us
    ppermute x11, waiting for transfers between devices: 12.4 us -> 9.58 us  [body(): ahead = lambda v: lax.ppermute(v, 'row', forward)]
    ppermute x11, waiting for transfers between devices: 16.7 us -> 19.4 us  [body(): back = lambda v: lax.ppermute(v, 'row', backward)]
    ppermute x18, starting transfers between devices: 3.06 us -> 5 us  [body(): lax.ppermute(v, 'row', [(i, i ^ 1) for i in range(devices)])]
    pallas_call x1, Pallas kernels: 14 us -> 12.5 us  [partial_sums(): pl.pallas_call(functools.partial(part_kernel, len(grads)), out_shape=[jax...]
    ppermute x11, starting transfers between devices: 19.8 us -> 18.4 us  [body(): ahead = lambda v: lax.ppermute(v, 'row', forward)]
    ppermute x11, starting transfers between devices: 4.02 us -> 5.3 us  [body(): back = lambda v: lax.ppermute(v, 'row', backward)]
  transfers between devices with their start and end apart: 40 -> 40, of which waited for: 26 -> 25; matrix products, arithmetic and copies ran while one was open for 2% -> 2% of each run, Pallas kernels for 29% -> 30%
where the time goes in v4:
time: 114 us; the launch traced here: 113 us
  Pallas kernels  46 us (40%)
  waiting for transfers between devices  32.7 us (29%)
  starting transfers between devices  28.7 us (25%)
  other arithmetic  3.63 us (3%)
  local copies, waits for them, and re-layouts  1.31 us (1%)
    pallas_call x4, Pallas kernels, update_stats(): pl.pallas_call(functools.partial(stat_kernel, len(grads), base, length),...  30.2 us
    ppermute x11, waiting for transfers between devices, body(): back = lambda v: lax.ppermute(v, 'row', backward)  19.4 us
    ppermute x11, starting transfers between devices, body(): ahead = lambda v: lax.ppermute(v, 'row', forward)  18.4 us
    pallas_call x1, Pallas kernels, partial_sums(): pl.pallas_call(functools.partial(part_kernel, len(grads)), out_shape=[jax...  12.5 us
    ppermute x11, waiting for transfers between devices, body(): ahead = lambda v: lax.ppermute(v, 'row', forward)  9.58 us
    ppermute x11, starting transfers between devices, body(): back = lambda v: lax.ppermute(v, 'row', backward)  5.3 us
    ppermute x18, starting transfers between devices, body(): lax.ppermute(v, 'row', [(i, i ^ 1) for i in range(devices)])  5 us
    ppermute x18, waiting for transfers between devices, body(): lax.ppermute(v, 'row', [(i, i ^ 1) for i in range(devices)])  3.7 us
  transfers between devices with their start and end apart: 40, of which 25 were waited for; matrix products, arithmetic and copies ran while one was open for 2% of the time, Pallas kernels for 30%

profile of v4, /device:TPU:0, one launch (start us, length us, event | category | flops | bytes accessed | tf_op | source)
XLA Modules:
  0.0 113.3 jit_solution(17071675992619858024)
XLA Ops:
  0.6 1.1 fusion.14
  1.7 3.1 %collective-permute-start = (bf16[8,15360]{1,0:T(8,128)(2,1)S(1)}, bf16[8,15360]{1,0:T(8,128)(2,1)S(1)}, u32[]{:S(2)}, u32[]{:S(2)}) collective-permute-start(bf16[8,15360]{1,0:T(8,128)(2,1)S(1)} %get-tuple-element.133.refs_17_), channel_id=1, source_target_pairs={{0,4},{1,5},{4,8},{5,9},{8,12},{9,13},{12,14},{13,15},{14,10},{15,... | collective-permute-start | bytes 737288 | tf_op jit(solution)/shard_map/ppermute | solution.py:270
  4.8 2.0 %collective-permute-start.8 = (bf16[8,15360]{1,0:T(8,128)(2,1)S(1)}, bf16[8,15360]{1,0:T(8,128)(2,1)S(1)}, u32[]{:S(2)}, u32[]{:S(2)}) collective-permute-start(bf16[8,15360]{1,0:T(8,128)(2,1)S(1)} %get-tuple-element.132.refs_18_), channel_id=1, source_target_pairs={{0,4},{1,5},{4,8},{5,9},{8,12},{9,13},{12,14},{13,15},{14,10},{15,... | collective-permute-start | bytes 737288 | tf_op jit(solution)/shard_map/ppermute | solution.py:270
  6.8 0.8 subtract_add_fusion
  7.6 0.7 compare_convert_fusion.live_ref
  8.3 3.2 %collective-permute-done = bf16[8,15360]{1,0:T(8,128)(2,1)S(1)} collective-permute-done((bf16[8,15360]{1,0:T(8,128)(2,1)S(1)}, bf16[8,15360]{1,0:T(8,128)(2,1)S(1)}, u32[]{:S(2)}, u32[]{:S(2)}) %collective-permute-start) | collective-permute-done | bytes 245792 | tf_op jit(solution)/shard_map/ppermute | solution.py:270
  11.5 2.2 %collective-permute-done.3 = bf16[8,15360]{1,0:T(8,128)(2,1)S(1)} collective-permute-done((bf16[8,15360]{1,0:T(8,128)(2,1)S(1)}, bf16[8,15360]{1,0:T(8,128)(2,1)S(1)}, u32[]{:S(2)}, u32[]{:S(2)}) %collective-permute-start.3) | collective-permute-done | bytes 245792 | tf_op jit(solution)/shard_map/ppermute | solution.py:271
  13.7 2.0 %collective-permute-start.1 = (bf16[8,15360]{1,0:T(8,128)(2,1)S(1)}, bf16[8,15360]{1,0:T(8,128)(2,1)S(1)}, u32[]{:S(2)}, u32[]{:S(2)}) collective-permute-start(bf16[8,15360]{1,0:T(8,128)(2,1)S(1)} %collective-permute-done), channel_id=1, source_target_pairs={{0,4},{1,5},{4,8},{5,9},{8,12},{9,13},{12,14},{13,15},{14,10},{15,... | collective-permute-start | bytes 737288 | tf_op jit(solution)/shard_map/ppermute | solution.py:270
  15.7 1.1 collective-permute-done.8
  16.8 2.1 %collective-permute-start.9 = (bf16[8,15360]{1,0:T(8,128)(2,1)S(1)}, bf16[8,15360]{1,0:T(8,128)(2,1)S(1)}, u32[]{:S(2)}, u32[]{:S(2)}) collective-permute-start(bf16[8,15360]{1,0:T(8,128)(2,1)S(1)} %collective-permute-done.8), channel_id=1, source_target_pairs={{0,4},{1,5},{4,8},{5,9},{8,12},{9,13},{12,14},{13,15},{14,10},{15,... | collective-permute-start | bytes 737288 | tf_op jit(solution)/shard_map/ppermute | solution.py:270
  19.0 5.3 %collective-permute-done.4 = bf16[8,15360]{1,0:T(8,128)(2,1)S(1)} collective-permute-done((bf16[8,15360]{1,0:T(8,128)(2,1)S(1)}, bf16[8,15360]{1,0:T(8,128)(2,1)S(1)}, u32[]{:S(2)}, u32[]{:S(2)}) %collective-permute-start.4) | collective-permute-done | bytes 245792 | tf_op jit(solution)/shard_map/ppermute | solution.py:271
  24.2 2.0 %collective-permute-start.2 = (bf16[8,15360]{1,0:T(8,128)(2,1)S(1)}, bf16[8,15360]{1,0:T(8,128)(2,1)S(1)}, u32[]{:S(2)}, u32[]{:S(2)}) collective-permute-start(bf16[8,15360]{1,0:T(8,128)(2,1)S(1)} %collective-permute-done.1), channel_id=1, source_target_pairs={{0,4},{1,5},{4,8},{5,9},{8,12},{9,13},{12,14},{13,15},{14,10},{15,... | collective-permute-start | bytes 737288 | tf_op jit(solution)/shard_map/ppermute | solution.py:270
  26.3 1.6 %collective-permute-done.9 = bf16[8,15360]{1,0:T(8,128)(2,1)S(1)} collective-permute-done((bf16[8,15360]{1,0:T(8,128)(2,1)S(1)}, bf16[8,15360]{1,0:T(8,128)(2,1)S(1)}, u32[]{:S(2)}, u32[]{:S(2)}) %collective-permute-start.9) | collective-permute-done | bytes 245792 | tf_op jit(solution)/shard_map/ppermute | solution.py:270
  27.9 1.6 %collective-permute-done.7 = bf16[8,15360]{1,0:T(8,128)(2,1)S(1)} collective-permute-done((bf16[8,15360]{1,0:T(8,128)(2,1)S(1)}, bf16[8,15360]{1,0:T(8,128)(2,1)S(1)}, u32[]{:S(2)}, u32[]{:S(2)}) %collective-permute-start.7) | collective-permute-done | bytes 245792 | tf_op jit(solution)/shard_map/ppermute | solution.py:271
  29.5 3.3 %shard_map.59 = (bf16[2,1024,1024]{2,1,0:T(8,128)(2,1)S(1)}, s32[8]{0:T(128)S(1)}) custom-call(s32[8]{0:T(128)S(1)} %get-tuple-element.68.after_ref, bf16[8,1024,1024]{2,1,0:T(8,128)(2,1)} %refs_20_.1), custom_call_target="tpu_custom_call" | custom-call | bytes 4194304 | tf_op jit(solution)/shard_map/pallas_call | solution.py:121
  32.8 1.6 %collective-permute-start.12 = (bf16[8,15360]{1,0:T(8,128)(2,1)S(1)}, bf16[8,15360]{1,0:T(8,128)(2,1)S(1)}, u32[]{:S(2)}, u32[]{:S(2)}) collective-permute-start(bf16[8,15360]{1,0:T(8,128)(2,1)S(1)} %collective-permute-done.9), channel_id=1, source_target_pairs={{0,4},{1,5},{4,8},{5,9},{8,12},{9,13},{12,14},{13,15},{14,10},{15,... | collective-permute-start | bytes 737288 | tf_op jit(solution)/shard_map/ppermute | solution.py:270
  34.5 0.4 collective-permute-start.14
  34.9 1.6 %collective-permute-start.10 = (bf16[8,15360]{1,0:T(8,128)(2,1)S(1)}, bf16[8,15360]{1,0:T(8,128)(2,1)S(1)}, u32[]{:S(2)}, u32[]{:S(2)}) collective-permute-start(bf16[8,15360]{1,0:T(8,128)(2,1)S(1)} %collective-permute-done.2), channel_id=1, source_target_pairs={{0,4},{1,5},{4,8},{5,9},{8,12},{9,13},{12,14},{13,15},{14,10},{15,... | collective-permute-start | bytes 737288 | tf_op jit(solution)/shard_map/ppermute | solution.py:270
  36.5 0.5 collective-permute-start.11
  37.0 4.9 %collective-permute-done.14 = bf16[8,15360]{1,0:T(8,128)(2,1)S(1)} collective-permute-done((bf16[8,15360]{1,0:T(8,128)(2,1)S(1)}, bf16[8,15360]{1,0:T(8,128)(2,1)S(1)}, u32[]{:S(2)}, u32[]{:S(2)}) %collective-permute-start.14) | collective-permute-done | bytes 245792 | tf_op jit(solution)/shard_map/ppermute | solution.py:271
  42.2 0.6 collective-permute-start.21
  42.8 0.4 collective-permute-done.10.refs_9_
  43.3 1.3 %collective-permute-done.11.refs_10_ = bf16[8,15360]{1,0:T(8,128)(2,1)S(1)} collective-permute-done((bf16[8,15360]{1,0:T(8,128)(2,1)S(1)}, bf16[8,15360]{1,0:T(8,128)(2,1)S(1)}, u32[]{:S(2)}, u32[]{:S(2)}) %collective-permute-start.11) | collective-permute-done | bytes 245792 | tf_op jit(solution)/shard_map/ppermute | solution.py:271
  44.6 0.5 collective-permute-start.20
  46.4 0.7 collective-permute-done.20.refs_6_
  47.1 0.7 collective-permute-done.18.refs_4_
  48.6 12.5 %shard_map.60 = (bf16[8,15360]{1,0:T(8,128)(2,1)S(1)}, bf16[8,15360]{1,0:T(8,128)(2,1)S(1)}, bf16[16,15360]{1,0:T(8,128)(2,1)S(1)}, bf16[16,15360]{1,0:T(8,128)(...) custom-call(s32[8]{0:T(128)S(1)} %get-tuple-element.121.first_ref, ...), custom_call_target="tpu_custom_call" | custom-call | flops 8589934592 | bytes 16777216 | tf_op jit(solution)/shard_map/pallas_call | solution.py:139
  61.1 1.7 %collective-permute-start.26 = (bf16[8,15360]{1,0:T(8,128)(2,1)S(1)}, bf16[8,15360]{1,0:T(8,128)(2,1)S(1)}, u32[]{:S(2)}, u32[]{:S(2)}) collective-permute-start(bf16[8,15360]{1,0:T(8,128)(2,1)S(1)} %get-tuple-element.95), channel_id=1, source_target_pairs={{0,1},{1,0},{2,3},{3,2},{4,5},{5,4},{6,7},{7,6},{8,9},{9,8},{10,11... | collective-permute-start | bytes 737288 | tf_op jit(solution)/shard_map/ppermute | solution.py:272
  62.8 0.4 collective-permute-start.25
  63.3 0.6 collective-permute-done.26
  64.3 1.8 %collective-permute-start.29 = (bf16[8,15360]{1,0:T(8,128)(2,1)S(1)}, bf16[8,15360]{1,0:T(8,128)(2,1)S(1)}, u32[]{:S(2)}, u32[]{:S(2)}) collective-permute-start(bf16[8,15360]{1,0:T(8,128)(2,1)S(1)} %add_convert_fusion.7), channel_id=1, source_target_pairs={{0,4},{1,5},{4,8},{5,9},{8,12},{9,13},{12,14},{13,15},{14,10},{15,... | collective-permute-start | bytes 737288 | tf_op jit(solution)/shard_map/ppermute | solution.py:270
  66.2 5.7 %shard_map.61.refs_20_ = f32[8,1024,1024]{2,1,0:T(8,128)} custom-call(s32[8]{0:T(128)S(1)} %get-tuple-element.121.first_ref, s32[8]{0:T(128)S(1)} %get-tuple-element.122.second_ref, s32[8]{0:T(128)S(1)} %compare_convert_fusion.live_ref, bf16[8,15360]{1,0:T(8,128)(2,1)S(1)} %collective-permute-done.16.refs_0_, ...), custom_call_target="tpu_custom_call" | custom-call | flops 671088640 | bytes 10485760 | tf_op jit(solution)/shard_map/pallas_call | solution.py:228
  72.7 1.2 %collective-permute-start.30 = (bf16[16,15360]{1,0:T(8,128)(2,1)S(1)}, bf16[16,15360]{1,0:T(8,128)(2,1)S(1)}, u32[]{:S(2)}, u32[]{:S(2)}) collective-permute-start(bf16[16,15360]{1,0:T(8,128)(2,1)S(1)} %add_convert_fusion.6), channel_id=1, source_target_pairs={{4,0},{5,1},{8,4},{9,5},{12,8},{13,9},{14,12},{15,13},{10,14},{11,... | collective-permute-start | bytes 1474568 | tf_op jit(solution)/shard_map/ppermute | solution.py:271
  74.1 1.0 collective-permute-start.32
  75.0 0.5 collective-permute-start.34
  75.5 8.1 %shard_map.62.refs_20_ = f32[8,1024,1024]{2,1,0:T(8,128)} custom-call(s32[8]{0:T(128)S(1)} %get-tuple-element.121.first_ref, s32[8]{0:T(128)S(1)} %get-tuple-element.122.second_ref, s32[8]{0:T(128)S(1)} %compare_convert_fusion.live_ref, bf16[8,15360]{1,0:T(8,128)(2,1)S(1)} %collective-permute-done.16.refs_0_, ...), custom_call_target="tpu_custom_call", output_to_operand_aliasing={{}: (23, {})} | custom-call | flops 1207959552 | bytes 18874368 | tf_op jit(solution)/shard_map/pallas_call | solution.py:228
  83.6 2.1 %collective-permute-done.30 = bf16[16,15360]{1,0:T(8,128)(2,1)S(1)} collective-permute-done((bf16[16,15360]{1,0:T(8,128)(2,1)S(1)}, bf16[16,15360]{1,0:T(8,128)(2,1)S(1)}, u32[]{:S(2)}, u32[]{:S(2)}) %collective-permute-start.30) | collective-permute-done | bytes 491552 | tf_op jit(solution)/shard_map/ppermute | solution.py:271
  86.3 1.8 %collective-permute-start.33 = (bf16[16,15360]{1,0:T(8,128)(2,1)S(1)}, bf16[16,15360]{1,0:T(8,128)(2,1)S(1)}, u32[]{:S(2)}, u32[]{:S(2)}) collective-permute-start(bf16[16,15360]{1,0:T(8,128)(2,1)S(1)} %add_convert_fusion.4), channel_id=1, source_target_pairs={{4,0},{5,1},{8,4},{9,5},{12,8},{13,9},{14,12},{15,13},{10,14},{11,... | collective-permute-start | bytes 1474568 | tf_op jit(solution)/shard_map/ppermute | solution.py:271
  88.6 0.5 collective-permute-start.37
  89.1 8.4 %shard_map.63.refs_20_ = f32[8,1024,1024]{2,1,0:T(8,128)} custom-call(s32[8]{0:T(128)S(1)} %get-tuple-element.121.first_ref, s32[8]{0:T(128)S(1)} %get-tuple-element.122.second_ref, s32[8]{0:T(128)S(1)} %compare_convert_fusion.live_ref, bf16[8,15360]{1,0:T(8,128)(2,1)S(1)} %collective-permute-done.16.refs_0_, ...), custom_call_target="tpu_custom_call", output_to_operand_aliasing={{}: (23, {})} | custom-call | flops 1207959552 | bytes 18874368 | tf_op jit(solution)/shard_map/pallas_call | solution.py:228
  97.5 0.8 collective-permute-done.33
  98.2 0.9 collective-permute-done.35
  99.4 1.3 %collective-permute-start.36 = (bf16[16,15360]{1,0:T(8,128)(2,1)S(1)}, bf16[16,15360]{1,0:T(8,128)(2,1)S(1)}, u32[]{:S(2)}, u32[]{:S(2)}) collective-permute-start(bf16[16,15360]{1,0:T(8,128)(2,1)S(1)} %add_convert_fusion.2), channel_id=1, source_target_pairs={{4,0},{5,1},{8,4},{9,5},{12,8},{13,9},{14,12},{15,13},{10,14},{11,... | collective-permute-start | bytes 1474568 | tf_op jit(solution)/shard_map/ppermute | solution.py:271
  100.9 0.8 collective-permute-start.38
  101.7 8.1 %shard_map.64 = f32[8,1024,1024]{2,1,0:T(8,128)} custom-call(s32[8]{0:T(128)S(1)} %get-tuple-element.121.first_ref, s32[8]{0:T(128)S(1)} %get-tuple-element.122.second_ref, s32[8]{0:T(128)S(1)} %compare_convert_fusion.live_ref, bf16[8,15360]{1,0:T(8,128)(2,1)S(1)} %collective-permute-done.16.refs_0_, ...), custom_call_target="tpu_custom_call", output_to_operand_aliasing={{}: (23, {})} | custom-call | flops 1207959552 | bytes 18874368 | tf_op jit(solution)/shard_map/pallas_call | solution.py:228
  109.7 0.8 collective-permute-done.36
  110.6 1.7 %collective-permute-done.38 = bf16[16,15360]{1,0:T(8,128)(2,1)S(1)} collective-permute-done((bf16[16,15360]{1,0:T(8,128)(2,1)S(1)}, bf16[16,15360]{1,0:T(8,128)(2,1)S(1)}, u32[]{:S(2)}, u32[]{:S(2)}) %collective-permute-start.38) | collective-permute-done | bytes 491552 | tf_op jit(solution)/shard_map/ppermute | solution.py:270
  112.3 1.0 add_convert_fusion
  (62 shorter events, 5.4 us)
Async XLA Ops:
  1.7 9.8 %collective-permute-start = (bf16[8,15360]{1,0:T(8,128)(2,1)S(1)}, bf16[8,15360]{1,0:T(8,128)(2,1)S(1)}, u32[]{:S(2)}, u32[]{:S(2)}) collective-permute-start(bf16[8,15360]{1,0:T(8,128)(2,1)S(1)} %get-tuple-element.133.refs_17_), channel_id=1, source_target_pairs={{0,4},{1,5},{4,8},{5,9},{8,12},{9,13},{12,14},{13,15},{14,10},{15,... | collective-permute-start | bytes 737288 | tf_op jit(solution)/shard_map/ppermute | solution.py:270
  4.8 8.9 %collective-permute-start.3 = (bf16[8,15360]{1,0:T(8,128)(2,1)S(1)}, bf16[8,15360]{1,0:T(8,128)(2,1)S(1)}, u32[]{:S(2)}, u32[]{:S(2)}) collective-permute-start(bf16[8,15360]{1,0:T(8,128)(2,1)S(1)} %get-tuple-element.132.refs_18_), channel_id=1, source_target_pairs={{4,0},{5,1},{8,4},{9,5},{12,8},{13,9},{14,12},{15,13},{10,14},{11,... | collective-permute-start | bytes 737288 | tf_op jit(solution)/shard_map/ppermute | solution.py:271
  4.8 12.0 %collective-permute-start.8 = (bf16[8,15360]{1,0:T(8,128)(2,1)S(1)}, bf16[8,15360]{1,0:T(8,128)(2,1)S(1)}, u32[]{:S(2)}, u32[]{:S(2)}) collective-permute-start(bf16[8,15360]{1,0:T(8,128)(2,1)S(1)} %get-tuple-element.132.refs_18_), channel_id=1, source_target_pairs={{0,4},{1,5},{4,8},{5,9},{8,12},{9,13},{12,14},{13,15},{14,10},{15,... | collective-permute-start | bytes 737288 | tf_op jit(solution)/shard_map/ppermute | solution.py:270
  6.8 12.1 %collective-permute-start.6 = (bf16[8,15360]{1,0:T(8,128)(2,1)S(1)}, bf16[8,15360]{1,0:T(8,128)(2,1)S(1)}, u32[]{:S(2)}, u32[]{:S(2)}) collective-permute-start(bf16[8,15360]{1,0:T(8,128)(2,1)S(1)} %get-tuple-element.133.refs_17_), channel_id=1, source_target_pairs={{4,0},{5,1},{8,4},{9,5},{12,8},{13,9},{14,12},{15,13},{10,14},{11,... | collective-permute-start | bytes 737288 | tf_op jit(solution)/shard_map/ppermute | solution.py:271
  13.7 10.5 %collective-permute-start.4 = (bf16[8,15360]{1,0:T(8,128)(2,1)S(1)}, bf16[8,15360]{1,0:T(8,128)(2,1)S(1)}, u32[]{:S(2)}, u32[]{:S(2)}) collective-permute-start(bf16[8,15360]{1,0:T(8,128)(2,1)S(1)} %collective-permute-done.3), channel_id=1, source_target_pairs={{4,0},{5,1},{8,4},{9,5},{12,8},{13,9},{14,12},{15,13},{10,14},{11,... | collective-permute-start | bytes 737288 | tf_op jit(solution)/shard_map/ppermute | solution.py:271
  13.7 10.5 %collective-permute-start.1 = (bf16[8,15360]{1,0:T(8,128)(2,1)S(1)}, bf16[8,15360]{1,0:T(8,128)(2,1)S(1)}, u32[]{:S(2)}, u32[]{:S(2)}) collective-permute-start(bf16[8,15360]{1,0:T(8,128)(2,1)S(1)} %collective-permute-done), channel_id=1, source_target_pairs={{0,4},{1,5},{4,8},{5,9},{8,12},{9,13},{12,14},{13,15},{14,10},{15,... | collective-permute-start | bytes 737288 | tf_op jit(solution)/shard_map/ppermute | solution.py:270
  16.8 11.1 %collective-permute-start.9 = (bf16[8,15360]{1,0:T(8,128)(2,1)S(1)}, bf16[8,15360]{1,0:T(8,128)(2,1)S(1)}, u32[]{:S(2)}, u32[]{:S(2)}) collective-permute-start(bf16[8,15360]{1,0:T(8,128)(2,1)S(1)} %collective-permute-done.8), channel_id=1, source_target_pairs={{0,4},{1,5},{4,8},{5,9},{8,12},{9,13},{12,14},{13,15},{14,10},{15,... | collective-permute-start | bytes 737288 | tf_op jit(solution)/shard_map/ppermute | solution.py:270
  19.0 10.5 %collective-permute-start.7 = (bf16[8,15360]{1,0:T(8,128)(2,1)S(1)}, bf16[8,15360]{1,0:T(8,128)(2,1)S(1)}, u32[]{:S(2)}, u32[]{:S(2)}) collective-permute-start(bf16[8,15360]{1,0:T(8,128)(2,1)S(1)} %collective-permute-done.6), channel_id=1, source_target_pairs={{4,0},{5,1},{8,4},{9,5},{12,8},{13,9},{14,12},{15,13},{10,14},{11,... | collective-permute-start | bytes 737288 | tf_op jit(solution)/shard_map/ppermute | solution.py:271
  24.2 10.7 %collective-permute-start.5 = (bf16[8,15360]{1,0:T(8,128)(2,1)S(1)}, bf16[8,15360]{1,0:T(8,128)(2,1)S(1)}, u32[]{:S(2)}, u32[]{:S(2)}) collective-permute-start(bf16[8,15360]{1,0:T(8,128)(2,1)S(1)} %collective-permute-done.4), channel_id=1, source_target_pairs={{4,0},{5,1},{8,4},{9,5},{12,8},{13,9},{14,12},{15,13},{10,14},{11,... | collective-permute-start | bytes 737288 | tf_op jit(solution)/shard_map/ppermute | solution.py:271
  24.2 10.7 %collective-permute-start.2 = (bf16[8,15360]{1,0:T(8,128)(2,1)S(1)}, bf16[8,15360]{1,0:T(8,128)(2,1)S(1)}, u32[]{:S(2)}, u32[]{:S(2)}) collective-permute-start(bf16[8,15360]{1,0:T(8,128)(2,1)S(1)} %collective-permute-done.1), channel_id=1, source_target_pairs={{0,4},{1,5},{4,8},{5,9},{8,12},{9,13},{12,14},{13,15},{14,10},{15,... | collective-permute-start | bytes 737288 | tf_op jit(solution)/shard_map/ppermute | solution.py:270
  26.3 19.4 %collective-permute-start.22 = (bf16[16,15360]{1,0:T(8,128)(2,1)}, bf16[16,15360]{1,0:T(8,128)(2,1)S(1)}, u32[]{:S(2)}, u32[]{:S(2)}) collective-permute-start(bf16[16,15360]{1,0:T(8,128)(2,1)} %param.4), channel_id=1, source_target_pairs={{0,1},{1,0},{2,3},{3,2},{4,5},{5,4},{6,7},{7,6},{8,9},{9,8},{10,11... | collective-permute-start | bytes 1474568 | tf_op jit(solution)/shard_map/ppermute | solution.py:272
  32.8 9.3 %collective-permute-start.12 = (bf16[8,15360]{1,0:T(8,128)(2,1)S(1)}, bf16[8,15360]{1,0:T(8,128)(2,1)S(1)}, u32[]{:S(2)}, u32[]{:S(2)}) collective-permute-start(bf16[8,15360]{1,0:T(8,128)(2,1)S(1)} %collective-permute-done.9), channel_id=1, source_target_pairs={{0,4},{1,5},{4,8},{5,9},{8,12},{9,13},{12,14},{13,15},{14,10},{15,... | collective-permute-start | bytes 737288 | tf_op jit(solution)/shard_map/ppermute | solution.py:270
  34.5 7.5 %collective-permute-start.14 = (bf16[8,15360]{1,0:T(8,128)(2,1)S(1)}, bf16[8,15360]{1,0:T(8,128)(2,1)S(1)}, u32[]{:S(2)}, u32[]{:S(2)}) collective-permute-start(bf16[8,15360]{1,0:T(8,128)(2,1)S(1)} %collective-permute-done.7), channel_id=1, source_target_pairs={{4,0},{5,1},{8,4},{9,5},{12,8},{13,9},{14,12},{15,13},{10,14},{11,... | collective-permute-start | bytes 737288 | tf_op jit(solution)/shard_map/ppermute | solution.py:271
  34.9 8.4 %collective-permute-start.10 = (bf16[8,15360]{1,0:T(8,128)(2,1)S(1)}, bf16[8,15360]{1,0:T(8,128)(2,1)S(1)}, u32[]{:S(2)}, u32[]{:S(2)}) collective-permute-start(bf16[8,15360]{1,0:T(8,128)(2,1)S(1)} %collective-permute-done.2), channel_id=1, source_target_pairs={{0,4},{1,5},{4,8},{5,9},{8,12},{9,13},{12,14},{13,15},{14,10},{15,... | collective-permute-start | bytes 737288 | tf_op jit(solution)/shard_map/ppermute | solution.py:270
  36.5 8.1 %collective-permute-start.11 = (bf16[8,15360]{1,0:T(8,128)(2,1)S(1)}, bf16[8,15360]{1,0:T(8,128)(2,1)S(1)}, u32[]{:S(2)}, u32[]{:S(2)}) collective-permute-start(bf16[8,15360]{1,0:T(8,128)(2,1)S(1)} %collective-permute-done.5), channel_id=1, source_target_pairs={{4,0},{5,1},{8,4},{9,5},{12,8},{13,9},{14,12},{15,13},{10,14},{11,... | collective-permute-start | bytes 737288 | tf_op jit(solution)/shard_map/ppermute | solution.py:271
  42.1 2.5 %collective-permute-start.13 = (bf16[16,15360]{1,0:T(8,128)(2,1)S(1)}, bf16[16,15360]{1,0:T(8,128)(2,1)S(1)}, u32[]{:S(2)}, u32[]{:S(2)}) collective-permute-start(bf16[16,15360]{1,0:T(8,128)(2,1)S(1)} %constant_dynamic-update-slice_fusion.refs_11_), channel_id=1, source_target_pairs={{0,1},{1,0},{2,3},{3,2},{4,5},{5,4},{6,7},{7,6},{8,9},{9,8},{10,11... | collective-permute-start | bytes 1474568 | tf_op jit(solution)/shard_map/ppermute | solution.py:272
  42.2 3.7 %collective-permute-start.21 = (bf16[16,15360]{1,0:T(8,128)(2,1)S(1)}, bf16[16,15360]{1,0:T(8,128)(2,1)S(1)}, u32[]{:S(2)}, u32[]{:S(2)}) collective-permute-start(bf16[16,15360]{1,0:T(8,128)(2,1)S(1)} %constant_dynamic-update-slice_fusion.10.refs_16_), channel_id=1, source_target_pairs={{0,1},{1,0},{2,3},{3,2},{4,5},{5,4},{6,7},{7,6},{8,9},{9,8},{10,11... | collective-permute-start | bytes 1474568 | tf_op jit(solution)/shard_map/ppermute | solution.py:272
  43.3 2.2 %collective-permute-start.15 = (bf16[16,15360]{1,0:T(8,128)(2,1)S(1)}, bf16[16,15360]{1,0:T(8,128)(2,1)S(1)}, u32[]{:S(2)}, u32[]{:S(2)}) collective-permute-start(bf16[16,15360]{1,0:T(8,128)(2,1)S(1)} %constant_dynamic-update-slice_fusion.2.refs_12_), channel_id=1, source_target_pairs={{0,1},{1,0},{2,3},{3,2},{4,5},{5,4},{6,7},{7,6},{8,9},{9,8},{10,11... | collective-permute-start | bytes 1474568 | tf_op jit(solution)/shard_map/ppermute | solution.py:272
  44.6 1.9 %collective-permute-start.19 = (bf16[16,15360]{1,0:T(8,128)(2,1)S(1)}, bf16[16,15360]{1,0:T(8,128)(2,1)S(1)}, u32[]{:S(2)}, u32[]{:S(2)}) collective-permute-start(bf16[16,15360]{1,0:T(8,128)(2,1)S(1)} %constant_dynamic-update-slice_fusion.6.refs_14_), channel_id=1, source_target_pairs={{0,1},{1,0},{2,3},{3,2},{4,5},{5,4},{6,7},{7,6},{8,9},{9,8},{10,11... | collective-permute-start | bytes 1474568 | tf_op jit(solution)/shard_map/ppermute | solution.py:272
  44.6 2.6 %collective-permute-start.20 = (bf16[16,15360]{1,0:T(8,128)(2,1)S(1)}, bf16[16,15360]{1,0:T(8,128)(2,1)S(1)}, u32[]{:S(2)}, u32[]{:S(2)}) collective-permute-start(bf16[16,15360]{1,0:T(8,128)(2,1)S(1)} %constant_dynamic-update-slice_fusion.8.refs_15_), channel_id=1, source_target_pairs={{0,1},{1,0},{2,3},{3,2},{4,5},{5,4},{6,7},{7,6},{8,9},{9,8},{10,11... | collective-permute-start | bytes 1474568 | tf_op jit(solution)/shard_map/ppermute | solution.py:272
  45.5 2.4 %collective-permute-start.18 = (bf16[16,15360]{1,0:T(8,128)(2,1)S(1)}, bf16[16,15360]{1,0:T(8,128)(2,1)S(1)}, u32[]{:S(2)}, u32[]{:S(2)}) collective-permute-start(bf16[16,15360]{1,0:T(8,128)(2,1)S(1)} %constant_dynamic-update-slice_fusion.4.refs_13_), channel_id=1, source_target_pairs={{0,1},{1,0},{2,3},{3,2},{4,5},{5,4},{6,7},{7,6},{8,9},{9,8},{10,11... | collective-permute-start | bytes 1474568 | tf_op jit(solution)/shard_map/ppermute | solution.py:272
  45.6 2.6 %collective-permute-start.16 = (bf16[8,15360]{1,0:T(8,128)(2,1)S(1)}, bf16[8,15360]{1,0:T(8,128)(2,1)S(1)}, u32[]{:S(2)}, u32[]{:S(2)}) collective-permute-start(bf16[8,15360]{1,0:T(8,128)(2,1)S(1)} %collective-permute-done.10.refs_9_), channel_id=1, source_target_pairs={{0,1},{1,0},{2,3},{3,2},{4,5},{5,4},{6,7},{7,6},{8,9},{9,8},{10,11... | collective-permute-start | bytes 737288 | tf_op jit(solution)/shard_map/ppermute | solution.py:272
  46.0 2.6 %collective-permute-start.17 = (bf16[8,15360]{1,0:T(8,128)(2,1)S(1)}, bf16[8,15360]{1,0:T(8,128)(2,1)S(1)}, u32[]{:S(2)}, u32[]{:S(2)}) collective-permute-start(bf16[8,15360]{1,0:T(8,128)(2,1)S(1)} %collective-permute-done.11.refs_10_), channel_id=1, source_target_pairs={{0,1},{1,0},{2,3},{3,2},{4,5},{5,4},{6,7},{7,6},{8,9},{9,8},{10,11... | collective-permute-start | bytes 737288 | tf_op jit(solution)/shard_map/ppermute | solution.py:272
  61.1 2.8 %collective-permute-start.26 = (bf16[8,15360]{1,0:T(8,128)(2,1)S(1)}, bf16[8,15360]{1,0:T(8,128)(2,1)S(1)}, u32[]{:S(2)}, u32[]{:S(2)}) collective-permute-start(bf16[8,15360]{1,0:T(8,128)(2,1)S(1)} %get-tuple-element.95), channel_id=1, source_target_pairs={{0,1},{1,0},{2,3},{3,2},{4,5},{5,4},{6,7},{7,6},{8,9},{9,8},{10,11... | collective-permute-start | bytes 737288 | tf_op jit(solution)/shard_map/ppermute | solution.py:272
  62.8 1.5 %collective-permute-start.28 = (bf16[8,15360]{1,0:T(8,128)(2,1)S(1)}, bf16[8,15360]{1,0:T(8,128)(2,1)S(1)}, u32[]{:S(2)}, u32[]{:S(2)}) collective-permute-start(bf16[8,15360]{1,0:T(8,128)(2,1)S(1)} %get-tuple-element.97), channel_id=1, source_target_pairs={{0,1},{1,0},{2,3},{3,2},{4,5},{5,4},{6,7},{7,6},{8,9},{9,8},{10,11... | collective-permute-start | bytes 737288 | tf_op jit(solution)/shard_map/ppermute | solution.py:272
  62.8 9.8 %collective-permute-start.25 = (bf16[16,15360]{1,0:T(8,128)(2,1)S(1)}, bf16[16,15360]{1,0:T(8,128)(2,1)S(1)}, u32[]{:S(2)}, u32[]{:S(2)}) collective-permute-start(bf16[16,15360]{1,0:T(8,128)(2,1)S(1)} %get-tuple-element.93), channel_id=1, source_target_pairs={{0,1},{1,0},{2,3},{3,2},{4,5},{5,4},{6,7},{7,6},{8,9},{9,8},{10,11... | collective-permute-start | bytes 1474568 | tf_op jit(solution)/shard_map/ppermute | solution.py:272
  64.0 8.3 %collective-permute-start.27 = (bf16[8,15360]{1,0:T(8,128)(2,1)S(1)}, bf16[8,15360]{1,0:T(8,128)(2,1)S(1)}, u32[]{:S(2)}, u32[]{:S(2)}) collective-permute-start(bf16[8,15360]{1,0:T(8,128)(2,1)S(1)} %add_convert_fusion.8), channel_id=1, source_target_pairs={{4,0},{5,1},{8,4},{9,5},{12,8},{13,9},{14,12},{15,13},{10,14},{11,... | collective-permute-start | bytes 737288 | tf_op jit(solution)/shard_map/ppermute | solution.py:271
  64.3 8.3 %collective-permute-start.29 = (bf16[8,15360]{1,0:T(8,128)(2,1)S(1)}, bf16[8,15360]{1,0:T(8,128)(2,1)S(1)}, u32[]{:S(2)}, u32[]{:S(2)}) collective-permute-start(bf16[8,15360]{1,0:T(8,128)(2,1)S(1)} %add_convert_fusion.7), channel_id=1, source_target_pairs={{0,4},{1,5},{4,8},{5,9},{8,12},{9,13},{12,14},{13,15},{14,10},{15,... | collective-permute-start | bytes 737288 | tf_op jit(solution)/shard_map/ppermute | solution.py:270
  66.2 7.8 %collective-permute-start.31 = (bf16[16,15360]{1,0:T(8,128)(2,1)S(1)}, bf16[16,15360]{1,0:T(8,128)(2,1)S(1)}, u32[]{:S(2)}, u32[]{:S(2)}) collective-permute-start(bf16[16,15360]{1,0:T(8,128)(2,1)S(1)} %get-tuple-element.103), channel_id=1, source_target_pairs={{0,1},{1,0},{2,3},{3,2},{4,5},{5,4},{6,7},{7,6},{8,9},{9,8},{10,11... | collective-permute-start | bytes 1474568 | tf_op jit(solution)/shard_map/ppermute | solution.py:272
  72.7 13.0 %collective-permute-start.30 = (bf16[16,15360]{1,0:T(8,128)(2,1)S(1)}, bf16[16,15360]{1,0:T(8,128)(2,1)S(1)}, u32[]{:S(2)}, u32[]{:S(2)}) collective-permute-start(bf16[16,15360]{1,0:T(8,128)(2,1)S(1)} %add_convert_fusion.6), channel_id=1, source_target_pairs={{4,0},{5,1},{8,4},{9,5},{12,8},{13,9},{14,12},{15,13},{10,14},{11,... | collective-permute-start | bytes 1474568 | tf_op jit(solution)/shard_map/ppermute | solution.py:271
  74.1 12.0 %collective-permute-start.32 = (bf16[16,15360]{1,0:T(8,128)(2,1)S(1)}, bf16[16,15360]{1,0:T(8,128)(2,1)S(1)}, u32[]{:S(2)}, u32[]{:S(2)}) collective-permute-start(bf16[16,15360]{1,0:T(8,128)(2,1)S(1)} %add_convert_fusion.5), channel_id=1, source_target_pairs={{0,4},{1,5},{4,8},{5,9},{8,12},{9,13},{12,14},{13,15},{14,10},{15,... | collective-permute-start | bytes 1474568 | tf_op jit(solution)/shard_map/ppermute | solution.py:270
  75.0 11.0 %collective-permute-start.24 = (bf16[16,15360]{1,0:T(8,128)(2,1)S(1)}, bf16[16,15360]{1,0:T(8,128)(2,1)S(1)}, u32[]{:S(2)}, u32[]{:S(2)}) collective-permute-start(bf16[16,15360]{1,0:T(8,128)(2,1)S(1)} %get-tuple-element.91), channel_id=1, source_target_pairs={{0,1},{1,0},{2,3},{3,2},{4,5},{5,4},{6,7},{7,6},{8,9},{9,8},{10,11... | collective-permute-start | bytes 1474568 | tf_op jit(solution)/shard_map/ppermute | solution.py:272
  75.0 13.0 %collective-permute-start.34 = (bf16[16,15360]{1,0:T(8,128)(2,1)S(1)}, bf16[16,15360]{1,0:T(8,128)(2,1)S(1)}, u32[]{:S(2)}, u32[]{:S(2)}) collective-permute-start(bf16[16,15360]{1,0:T(8,128)(2,1)S(1)} %get-tuple-element.111), channel_id=1, source_target_pairs={{0,1},{1,0},{2,3},{3,2},{4,5},{5,4},{6,7},{7,6},{8,9},{9,8},{10,11... | collective-permute-start | bytes 1474568 | tf_op jit(solution)/shard_map/ppermute | solution.py:272
  86.3 12.0 %collective-permute-start.33 = (bf16[16,15360]{1,0:T(8,128)(2,1)S(1)}, bf16[16,15360]{1,0:T(8,128)(2,1)S(1)}, u32[]{:S(2)}, u32[]{:S(2)}) collective-permute-start(bf16[16,15360]{1,0:T(8,128)(2,1)S(1)} %add_convert_fusion.4), channel_id=1, source_target_pairs={{4,0},{5,1},{8,4},{9,5},{12,8},{13,9},{14,12},{15,13},{10,14},{11,... | collective-permute-start | bytes 1474568 | tf_op jit(solution)/shard_map/ppermute | solution.py:271
  88.2 10.9 %collective-permute-start.35 = (bf16[16,15360]{1,0:T(8,128)(2,1)S(1)}, bf16[16,15360]{1,0:T(8,128)(2,1)S(1)}, u32[]{:S(2)}, u32[]{:S(2)}) collective-permute-start(bf16[16,15360]{1,0:T(8,128)(2,1)S(1)} %add_convert_fusion.3), channel_id=1, source_target_pairs={{0,4},{1,5},{4,8},{5,9},{8,12},{9,13},{12,14},{13,15},{14,10},{15,... | collective-permute-start | bytes 1474568 | tf_op jit(solution)/shard_map/ppermute | solution.py:270
  88.6 10.6 %collective-permute-start.23 = (bf16[16,15360]{1,0:T(8,128)(2,1)S(1)}, bf16[16,15360]{1,0:T(8,128)(2,1)S(1)}, u32[]{:S(2)}, u32[]{:S(2)}) collective-permute-start(bf16[16,15360]{1,0:T(8,128)(2,1)S(1)} %get-tuple-element.89), channel_id=1, source_target_pairs={{0,1},{1,0},{2,3},{3,2},{4,5},{5,4},{6,7},{7,6},{8,9},{9,8},{10,11... | collective-permute-start | bytes 1474568 | tf_op jit(solution)/shard_map/ppermute | solution.py:272
  88.6 12.1 %collective-permute-start.37 = (bf16[16,15360]{1,0:T(8,128)(2,1)S(1)}, bf16[16,15360]{1,0:T(8,128)(2,1)S(1)}, u32[]{:S(2)}, u32[]{:S(2)}) collective-permute-start(bf16[16,15360]{1,0:T(8,128)(2,1)S(1)} %get-tuple-element.119), channel_id=1, source_target_pairs={{0,1},{1,0},{2,3},{3,2},{4,5},{5,4},{6,7},{7,6},{8,9},{9,8},{10,11... | collective-permute-start | bytes 1474568 | tf_op jit(solution)/shard_map/ppermute | solution.py:272
  99.4 11.2 %collective-permute-start.36 = (bf16[16,15360]{1,0:T(8,128)(2,1)S(1)}, bf16[16,15360]{1,0:T(8,128)(2,1)S(1)}, u32[]{:S(2)}, u32[]{:S(2)}) collective-permute-start(bf16[16,15360]{1,0:T(8,128)(2,1)S(1)} %add_convert_fusion.2), channel_id=1, source_target_pairs={{4,0},{5,1},{8,4},{9,5},{12,8},{13,9},{14,12},{15,13},{10,14},{11,... | collective-permute-start | bytes 1474568 | tf_op jit(solution)/shard_map/ppermute | solution.py:271
  100.9 11.4 %collective-permute-start.38 = (bf16[16,15360]{1,0:T(8,128)(2,1)S(1)}, bf16[16,15360]{1,0:T(8,128)(2,1)S(1)}, u32[]{:S(2)}, u32[]{:S(2)}) collective-permute-start(bf16[16,15360]{1,0:T(8,128)(2,1)S(1)} %add_convert_fusion.1), channel_id=1, source_target_pairs={{0,4},{1,5},{4,8},{5,9},{8,12},{9,13},{12,14},{13,15},{14,10},{15,... | collective-permute-start | bytes 1474568 | tf_op jit(solution)/shard_map/ppermute | solution.py:270
  101.7 10.6 %collective-permute-start.39 = (bf16[16,15360]{1,0:T(8,128)(2,1)S(1)}, bf16[16,15360]{1,0:T(8,128)(2,1)S(1)}, u32[]{:S(2)}, u32[]{:S(2)}) collective-permute-start(bf16[16,15360]{1,0:T(8,128)(2,1)S(1)} %get-tuple-element.127), channel_id=1, source_target_pairs={{0,1},{1,0},{2,3},{3,2},{4,5},{5,4},{6,7},{7,6},{8,9},{9,8},{10,11... | collective-permute-start | bytes 1474568 | tf_op jit(solution)/shard_map/ppermute | solution.py:272

commit v5 on v4

--- a/solution.py
+++ b/solution.py
@@ -63,12 +63,11 @@
         @pl.when(live_ref[slot] > 0)
         def _():
             rows = slab(grads, second * tile, tile)
-            add(first, lax.dot_general(rows, root[...], (((1,), (1,)), ((), ())), preferred_element_type=F32))
-
-        @pl.when((live_ref[slot] > 0) & (first != second))
-        def _():
+            part = lax.dot_general(rows, root[...], (((1,), (1,)), ((), ())), preferred_element_type=F32)
             rows = slab(grads, first * tile, tile)
-            add(second, lax.dot_general(rows, root[...], (((1,), (0,)), ((), ())), preferred_element_type=F32))
+            other = lax.dot_general(rows, root[...], (((1,), (0,)), ((), ())), preferred_element_type=F32)
+            add(first, part)
+            add(second, jnp.where(first != second, other, 0.0))
 
     def early_step(slot, _):
         use(slot, early_ref.at[slot])

time: 114 us -> 113 us (level)
  starting transfers between devices: 28.7 us -> 27.4 us
    ppermute x18, starting transfers between devices: 5 us -> 3.46 us  [body(): lax.ppermute(v, 'row', [(i, i ^ 1) for i in range(devices)])]
  transfers between devices with their start and end apart: 40 -> 40, of which waited for: 25 -> 24; matrix products, arithmetic and copies ran while one was open for 2% -> 3% of each run, Pallas kernels for 30% -> 29%
where the time goes in v5:
time: 113 us
  Pallas kernels  46.4 us (41%)
  waiting for transfers between devices  33 us (29%)
  starting transfers between devices  27.4 us (24%)
  other arithmetic  3.63 us (3%)
  local copies, waits for them, and re-layouts  1.31 us (1%)
    pallas_call x4, Pallas kernels, update_stats(): pl.pallas_call(functools.partial(stat_kernel, len(grads), base, length),...  29.9 us
    ppermute x11, waiting for transfers between devices, body(): back = lambda v: lax.ppermute(v, 'row', backward)  19.5 us
    ppermute x11, starting transfers between devices, body(): ahead = lambda v: lax.ppermute(v, 'row', forward)  18 us
    pallas_call x1, Pallas kernels, partial_sums(): pl.pallas_call(functools.partial(part_kernel, len(grads)), out_shape=[jax...  13.2 us
    ppermute x11, waiting for transfers between devices, body(): ahead = lambda v: lax.ppermute(v, 'row', forward)  9.78 us
    ppermute x11, starting transfers between devices, body(): back = lambda v: lax.ppermute(v, 'row', backward)  6 us
    ppermute x18, waiting for transfers between devices, body(): lax.ppermute(v, 'row', [(i, i ^ 1) for i in range(devices)])  3.75 us
    ppermute x18, starting transfers between devices, body(): lax.ppermute(v, 'row', [(i, i ^ 1) for i in range(devices)])  3.46 us
  transfers between devices with their start and end apart: 40, of which 24 were waited for; matrix products, arithmetic and copies ran while one was open for 3% of the time, Pallas kernels for 29%

profile of v5, /device:TPU:0, one launch (start us, length us, event | category | flops | bytes accessed | tf_op | source)
XLA Modules:
  0.0 112.7 jit_solution(3037647633646425150)
XLA Ops:
  0.6 1.1 fusion.14
  1.7 3.1 %collective-permute-start = (bf16[8,15360]{1,0:T(8,128)(2,1)S(1)}, bf16[8,15360]{1,0:T(8,128)(2,1)S(1)}, u32[]{:S(2)}, u32[]{:S(2)}) collective-permute-start(bf16[8,15360]{1,0:T(8,128)(2,1)S(1)} %get-tuple-element.133.refs_17_), channel_id=1, source_target_pairs={{0,4},{1,5},{4,8},{5,9},{8,12},{9,13},{12,14},{13,15},{14,10},{15,... | collective-permute-start | bytes 737288 | tf_op jit(solution)/shard_map/ppermute | solution.py:269
  4.8 2.0 %collective-permute-start.8 = (bf16[8,15360]{1,0:T(8,128)(2,1)S(1)}, bf16[8,15360]{1,0:T(8,128)(2,1)S(1)}, u32[]{:S(2)}, u32[]{:S(2)}) collective-permute-start(bf16[8,15360]{1,0:T(8,128)(2,1)S(1)} %get-tuple-element.132.refs_18_), channel_id=1, source_target_pairs={{0,4},{1,5},{4,8},{5,9},{8,12},{9,13},{12,14},{13,15},{14,10},{15,... | collective-permute-start | bytes 737288 | tf_op jit(solution)/shard_map/ppermute | solution.py:269
  6.8 0.8 subtract_add_fusion
  7.6 0.7 compare_convert_fusion.live_ref
  8.3 3.2 %collective-permute-done = bf16[8,15360]{1,0:T(8,128)(2,1)S(1)} collective-permute-done((bf16[8,15360]{1,0:T(8,128)(2,1)S(1)}, bf16[8,15360]{1,0:T(8,128)(2,1)S(1)}, u32[]{:S(2)}, u32[]{:S(2)}) %collective-permute-start) | collective-permute-done | bytes 245792 | tf_op jit(solution)/shard_map/ppermute | solution.py:269
  11.5 2.2 %collective-permute-done.3 = bf16[8,15360]{1,0:T(8,128)(2,1)S(1)} collective-permute-done((bf16[8,15360]{1,0:T(8,128)(2,1)S(1)}, bf16[8,15360]{1,0:T(8,128)(2,1)S(1)}, u32[]{:S(2)}, u32[]{:S(2)}) %collective-permute-start.3) | collective-permute-done | bytes 245792 | tf_op jit(solution)/shard_map/ppermute | solution.py:270
  13.7 2.0 %collective-permute-start.1 = (bf16[8,15360]{1,0:T(8,128)(2,1)S(1)}, bf16[8,15360]{1,0:T(8,128)(2,1)S(1)}, u32[]{:S(2)}, u32[]{:S(2)}) collective-permute-start(bf16[8,15360]{1,0:T(8,128)(2,1)S(1)} %collective-permute-done), channel_id=1, source_target_pairs={{0,4},{1,5},{4,8},{5,9},{8,12},{9,13},{12,14},{13,15},{14,10},{15,... | collective-permute-start | bytes 737288 | tf_op jit(solution)/shard_map/ppermute | solution.py:269
  15.7 1.1 collective-permute-done.8
  16.8 2.1 %collective-permute-start.9 = (bf16[8,15360]{1,0:T(8,128)(2,1)S(1)}, bf16[8,15360]{1,0:T(8,128)(2,1)S(1)}, u32[]{:S(2)}, u32[]{:S(2)}) collective-permute-start(bf16[8,15360]{1,0:T(8,128)(2,1)S(1)} %collective-permute-done.8), channel_id=1, source_target_pairs={{0,4},{1,5},{4,8},{5,9},{8,12},{9,13},{12,14},{13,15},{14,10},{15,... | collective-permute-start | bytes 737288 | tf_op jit(solution)/shard_map/ppermute | solution.py:269
  19.0 5.3 %collective-permute-done.4 = bf16[8,15360]{1,0:T(8,128)(2,1)S(1)} collective-permute-done((bf16[8,15360]{1,0:T(8,128)(2,1)S(1)}, bf16[8,15360]{1,0:T(8,128)(2,1)S(1)}, u32[]{:S(2)}, u32[]{:S(2)}) %collective-permute-start.4) | collective-permute-done | bytes 245792 | tf_op jit(solution)/shard_map/ppermute | solution.py:270
  24.2 2.0 %collective-permute-start.2 = (bf16[8,15360]{1,0:T(8,128)(2,1)S(1)}, bf16[8,15360]{1,0:T(8,128)(2,1)S(1)}, u32[]{:S(2)}, u32[]{:S(2)}) collective-permute-start(bf16[8,15360]{1,0:T(8,128)(2,1)S(1)} %collective-permute-done.1), channel_id=1, source_target_pairs={{0,4},{1,5},{4,8},{5,9},{8,12},{9,13},{12,14},{13,15},{14,10},{15,... | collective-permute-start | bytes 737288 | tf_op jit(solution)/shard_map/ppermute | solution.py:269
  26.3 1.6 %collective-permute-done.9 = bf16[8,15360]{1,0:T(8,128)(2,1)S(1)} collective-permute-done((bf16[8,15360]{1,0:T(8,128)(2,1)S(1)}, bf16[8,15360]{1,0:T(8,128)(2,1)S(1)}, u32[]{:S(2)}, u32[]{:S(2)}) %collective-permute-start.9) | collective-permute-done | bytes 245792 | tf_op jit(solution)/shard_map/ppermute | solution.py:269
  27.9 1.6 %collective-permute-done.7 = bf16[8,15360]{1,0:T(8,128)(2,1)S(1)} collective-permute-done((bf16[8,15360]{1,0:T(8,128)(2,1)S(1)}, bf16[8,15360]{1,0:T(8,128)(2,1)S(1)}, u32[]{:S(2)}, u32[]{:S(2)}) %collective-permute-start.7) | collective-permute-done | bytes 245792 | tf_op jit(solution)/shard_map/ppermute | solution.py:270
  29.5 3.3 %shard_map.59 = (bf16[2,1024,1024]{2,1,0:T(8,128)(2,1)S(1)}, s32[8]{0:T(128)S(1)}) custom-call(s32[8]{0:T(128)S(1)} %get-tuple-element.68.after_ref, bf16[8,1024,1024]{2,1,0:T(8,128)(2,1)} %refs_20_.1), custom_call_target="tpu_custom_call" | custom-call | bytes 4194304 | tf_op jit(solution)/shard_map/pallas_call | solution.py:120
  32.8 1.6 %collective-permute-start.12 = (bf16[8,15360]{1,0:T(8,128)(2,1)S(1)}, bf16[8,15360]{1,0:T(8,128)(2,1)S(1)}, u32[]{:S(2)}, u32[]{:S(2)}) collective-permute-start(bf16[8,15360]{1,0:T(8,128)(2,1)S(1)} %collective-permute-done.9), channel_id=1, source_target_pairs={{0,4},{1,5},{4,8},{5,9},{8,12},{9,13},{12,14},{13,15},{14,10},{15,... | collective-permute-start | bytes 737288 | tf_op jit(solution)/shard_map/ppermute | solution.py:269
  34.5 0.4 collective-permute-start.14
  34.9 1.6 %collective-permute-start.10 = (bf16[8,15360]{1,0:T(8,128)(2,1)S(1)}, bf16[8,15360]{1,0:T(8,128)(2,1)S(1)}, u32[]{:S(2)}, u32[]{:S(2)}) collective-permute-start(bf16[8,15360]{1,0:T(8,128)(2,1)S(1)} %collective-permute-done.2), channel_id=1, source_target_pairs={{0,4},{1,5},{4,8},{5,9},{8,12},{9,13},{12,14},{13,15},{14,10},{15,... | collective-permute-start | bytes 737288 | tf_op jit(solution)/shard_map/ppermute | solution.py:269
  36.5 0.5 collective-permute-start.11
  37.0 4.9 %collective-permute-done.14 = bf16[8,15360]{1,0:T(8,128)(2,1)S(1)} collective-permute-done((bf16[8,15360]{1,0:T(8,128)(2,1)S(1)}, bf16[8,15360]{1,0:T(8,128)(2,1)S(1)}, u32[]{:S(2)}, u32[]{:S(2)}) %collective-permute-start.14) | collective-permute-done | bytes 245792 | tf_op jit(solution)/shard_map/ppermute | solution.py:270
  42.2 0.6 collective-permute-start.21
  42.8 0.4 collective-permute-done.10.refs_9_
  43.3 1.3 %collective-permute-done.11.refs_10_ = bf16[8,15360]{1,0:T(8,128)(2,1)S(1)} collective-permute-done((bf16[8,15360]{1,0:T(8,128)(2,1)S(1)}, bf16[8,15360]{1,0:T(8,128)(2,1)S(1)}, u32[]{:S(2)}, u32[]{:S(2)}) %collective-permute-start.11) | collective-permute-done | bytes 245792 | tf_op jit(solution)/shard_map/ppermute | solution.py:270
  44.6 0.5 collective-permute-start.20
  46.4 0.7 collective-permute-done.20.refs_6_
  47.1 0.7 collective-permute-done.18.refs_4_
  48.6 13.2 %shard_map.60 = (bf16[8,15360]{1,0:T(8,128)(2,1)S(1)}, bf16[8,15360]{1,0:T(8,128)(2,1)S(1)}, bf16[16,15360]{1,0:T(8,128)(2,1)S(1)}, bf16[16,15360]{1,0:T(8,128)(...) custom-call(s32[8]{0:T(128)S(1)} %get-tuple-element.121.first_ref, ...), custom_call_target="tpu_custom_call" | custom-call | flops 8589934592 | bytes 16777216 | tf_op jit(solution)/shard_map/pallas_call | solution.py:138
  61.8 0.5 collective-permute-start.28
  62.4 0.9 collective-permute-done.26
  63.4 0.5 collective-permute-start.27
  64.0 1.6 %collective-permute-start.29 = (bf16[8,15360]{1,0:T(8,128)(2,1)S(1)}, bf16[8,15360]{1,0:T(8,128)(2,1)S(1)}, u32[]{:S(2)}, u32[]{:S(2)}) collective-permute-start(bf16[8,15360]{1,0:T(8,128)(2,1)S(1)} %add_convert_fusion.7), channel_id=1, source_target_pairs={{0,4},{1,5},{4,8},{5,9},{8,12},{9,13},{12,14},{13,15},{14,10},{15,... | collective-permute-start | bytes 737288 | tf_op jit(solution)/shard_map/ppermute | solution.py:269
  65.6 5.7 %shard_map.61.refs_20_ = f32[8,1024,1024]{2,1,0:T(8,128)} custom-call(s32[8]{0:T(128)S(1)} %get-tuple-element.121.first_ref, s32[8]{0:T(128)S(1)} %get-tuple-element.122.second_ref, s32[8]{0:T(128)S(1)} %compare_convert_fusion.live_ref, bf16[8,15360]{1,0:T(8,128)(2,1)S(1)} %collective-permute-done.16.refs_0_, ...), custom_call_target="tpu_custom_call" | custom-call | flops 671088640 | bytes 10485760 | tf_op jit(solution)/shard_map/pallas_call | solution.py:227
  72.0 1.4 %collective-permute-start.30 = (bf16[16,15360]{1,0:T(8,128)(2,1)S(1)}, bf16[16,15360]{1,0:T(8,128)(2,1)S(1)}, u32[]{:S(2)}, u32[]{:S(2)}) collective-permute-start(bf16[16,15360]{1,0:T(8,128)(2,1)S(1)} %add_convert_fusion.6), channel_id=1, source_target_pairs={{4,0},{5,1},{8,4},{9,5},{12,8},{13,9},{14,12},{15,13},{10,14},{11,... | collective-permute-start | bytes 1474568 | tf_op jit(solution)/shard_map/ppermute | solution.py:270
  73.5 0.8 collective-permute-start.32
  74.3 0.5 collective-permute-start.34
  74.8 8.1 %shard_map.62.refs_20_ = f32[8,1024,1024]{2,1,0:T(8,128)} custom-call(s32[8]{0:T(128)S(1)} %get-tuple-element.121.first_ref, s32[8]{0:T(128)S(1)} %get-tuple-element.122.second_ref, s32[8]{0:T(128)S(1)} %compare_convert_fusion.live_ref, bf16[8,15360]{1,0:T(8,128)(2,1)S(1)} %collective-permute-done.16.refs_0_, ...), custom_call_target="tpu_custom_call", output_to_operand_aliasing={{}: (23, {})} | custom-call | flops 1207959552 | bytes 18874368 | tf_op jit(solution)/shard_map/pallas_call | solution.py:227
  82.9 2.3 %collective-permute-done.30 = bf16[16,15360]{1,0:T(8,128)(2,1)S(1)} collective-permute-done((bf16[16,15360]{1,0:T(8,128)(2,1)S(1)}, bf16[16,15360]{1,0:T(8,128)(2,1)S(1)}, u32[]{:S(2)}, u32[]{:S(2)}) %collective-permute-start.30) | collective-permute-done | bytes 491552 | tf_op jit(solution)/shard_map/ppermute | solution.py:270
  85.7 1.8 %collective-permute-start.33 = (bf16[16,15360]{1,0:T(8,128)(2,1)S(1)}, bf16[16,15360]{1,0:T(8,128)(2,1)S(1)}, u32[]{:S(2)}, u32[]{:S(2)}) collective-permute-start(bf16[16,15360]{1,0:T(8,128)(2,1)S(1)} %add_convert_fusion.4), channel_id=1, source_target_pairs={{4,0},{5,1},{8,4},{9,5},{12,8},{13,9},{14,12},{15,13},{10,14},{11,... | collective-permute-start | bytes 1474568 | tf_op jit(solution)/shard_map/ppermute | solution.py:270
  88.0 0.5 collective-permute-start.37
  88.5 8.1 %shard_map.63.refs_20_ = f32[8,1024,1024]{2,1,0:T(8,128)} custom-call(s32[8]{0:T(128)S(1)} %get-tuple-element.121.first_ref, s32[8]{0:T(128)S(1)} %get-tuple-element.122.second_ref, s32[8]{0:T(128)S(1)} %compare_convert_fusion.live_ref, bf16[8,15360]{1,0:T(8,128)(2,1)S(1)} %collective-permute-done.16.refs_0_, ...), custom_call_target="tpu_custom_call", output_to_operand_aliasing={{}: (23, {})} | custom-call | flops 1207959552 | bytes 18874368 | tf_op jit(solution)/shard_map/pallas_call | solution.py:227
  96.6 1.0 collective-permute-done.33
  97.6 1.1 collective-permute-done.35
  98.9 1.4 %collective-permute-start.36 = (bf16[16,15360]{1,0:T(8,128)(2,1)S(1)}, bf16[16,15360]{1,0:T(8,128)(2,1)S(1)}, u32[]{:S(2)}, u32[]{:S(2)}) collective-permute-start(bf16[16,15360]{1,0:T(8,128)(2,1)S(1)} %add_convert_fusion.2), channel_id=1, source_target_pairs={{4,0},{5,1},{8,4},{9,5},{12,8},{13,9},{14,12},{15,13},{10,14},{11,... | collective-permute-start | bytes 1474568 | tf_op jit(solution)/shard_map/ppermute | solution.py:270
  100.6 0.7 collective-permute-start.38
  101.3 8.1 %shard_map.64 = f32[8,1024,1024]{2,1,0:T(8,128)} custom-call(s32[8]{0:T(128)S(1)} %get-tuple-element.121.first_ref, s32[8]{0:T(128)S(1)} %get-tuple-element.122.second_ref, s32[8]{0:T(128)S(1)} %compare_convert_fusion.live_ref, bf16[8,15360]{1,0:T(8,128)(2,1)S(1)} %collective-permute-done.16.refs_0_, ...), custom_call_target="tpu_custom_call", output_to_operand_aliasing={{}: (23, {})} | custom-call | flops 1207959552 | bytes 18874368 | tf_op jit(solution)/shard_map/pallas_call | solution.py:227
  109.3 0.7 collective-permute-done.36
  110.0 1.6 %collective-permute-done.38 = bf16[16,15360]{1,0:T(8,128)(2,1)S(1)} collective-permute-done((bf16[16,15360]{1,0:T(8,128)(2,1)S(1)}, bf16[16,15360]{1,0:T(8,128)(2,1)S(1)}, u32[]{:S(2)}, u32[]{:S(2)}) %collective-permute-start.38) | collective-permute-done | bytes 491552 | tf_op jit(solution)/shard_map/ppermute | solution.py:269
  111.7 1.0 add_convert_fusion
  (62 shorter events, 5.0 us)
Async XLA Ops:
  1.7 9.8 %collective-permute-start = (bf16[8,15360]{1,0:T(8,128)(2,1)S(1)}, bf16[8,15360]{1,0:T(8,128)(2,1)S(1)}, u32[]{:S(2)}, u32[]{:S(2)}) collective-permute-start(bf16[8,15360]{1,0:T(8,128)(2,1)S(1)} %get-tuple-element.133.refs_17_), channel_id=1, source_target_pairs={{0,4},{1,5},{4,8},{5,9},{8,12},{9,13},{12,14},{13,15},{14,10},{15,... | collective-permute-start | bytes 737288 | tf_op jit(solution)/shard_map/ppermute | solution.py:269
  4.8 8.9 %collective-permute-start.3 = (bf16[8,15360]{1,0:T(8,128)(2,1)S(1)}, bf16[8,15360]{1,0:T(8,128)(2,1)S(1)}, u32[]{:S(2)}, u32[]{:S(2)}) collective-permute-start(bf16[8,15360]{1,0:T(8,128)(2,1)S(1)} %get-tuple-element.132.refs_18_), channel_id=1, source_target_pairs={{4,0},{5,1},{8,4},{9,5},{12,8},{13,9},{14,12},{15,13},{10,14},{11,... | collective-permute-start | bytes 737288 | tf_op jit(solution)/shard_map/ppermute | solution.py:270
  4.8 12.0 %collective-permute-start.8 = (bf16[8,15360]{1,0:T(8,128)(2,1)S(1)}, bf16[8,15360]{1,0:T(8,128)(2,1)S(1)}, u32[]{:S(2)}, u32[]{:S(2)}) collective-permute-start(bf16[8,15360]{1,0:T(8,128)(2,1)S(1)} %get-tuple-element.132.refs_18_), channel_id=1, source_target_pairs={{0,4},{1,5},{4,8},{5,9},{8,12},{9,13},{12,14},{13,15},{14,10},{15,... | collective-permute-start | bytes 737288 | tf_op jit(solution)/shard_map/ppermute | solution.py:269
  6.8 12.1 %collective-permute-start.6 = (bf16[8,15360]{1,0:T(8,128)(2,1)S(1)}, bf16[8,15360]{1,0:T(8,128)(2,1)S(1)}, u32[]{:S(2)}, u32[]{:S(2)}) collective-permute-start(bf16[8,15360]{1,0:T(8,128)(2,1)S(1)} %get-tuple-element.133.refs_17_), channel_id=1, source_target_pairs={{4,0},{5,1},{8,4},{9,5},{12,8},{13,9},{14,12},{15,13},{10,14},{11,... | collective-permute-start | bytes 737288 | tf_op jit(solution)/shard_map/ppermute | solution.py:270
  13.7 10.5 %collective-permute-start.4 = (bf16[8,15360]{1,0:T(8,128)(2,1)S(1)}, bf16[8,15360]{1,0:T(8,128)(2,1)S(1)}, u32[]{:S(2)}, u32[]{:S(2)}) collective-permute-start(bf16[8,15360]{1,0:T(8,128)(2,1)S(1)} %collective-permute-done.3), channel_id=1, source_target_pairs={{4,0},{5,1},{8,4},{9,5},{12,8},{13,9},{14,12},{15,13},{10,14},{11,... | collective-permute-start | bytes 737288 | tf_op jit(solution)/shard_map/ppermute | solution.py:270
  13.7 10.5 %collective-permute-start.1 = (bf16[8,15360]{1,0:T(8,128)(2,1)S(1)}, bf16[8,15360]{1,0:T(8,128)(2,1)S(1)}, u32[]{:S(2)}, u32[]{:S(2)}) collective-permute-start(bf16[8,15360]{1,0:T(8,128)(2,1)S(1)} %collective-permute-done), channel_id=1, source_target_pairs={{0,4},{1,5},{4,8},{5,9},{8,12},{9,13},{12,14},{13,15},{14,10},{15,... | collective-permute-start | bytes 737288 | tf_op jit(solution)/shard_map/ppermute | solution.py:269
  16.8 11.1 %collective-permute-start.9 = (bf16[8,15360]{1,0:T(8,128)(2,1)S(1)}, bf16[8,15360]{1,0:T(8,128)(2,1)S(1)}, u32[]{:S(2)}, u32[]{:S(2)}) collective-permute-start(bf16[8,15360]{1,0:T(8,128)(2,1)S(1)} %collective-permute-done.8), channel_id=1, source_target_pairs={{0,4},{1,5},{4,8},{5,9},{8,12},{9,13},{12,14},{13,15},{14,10},{15,... | collective-permute-start | bytes 737288 | tf_op jit(solution)/shard_map/ppermute | solution.py:269
  19.0 10.5 %collective-permute-start.7 = (bf16[8,15360]{1,0:T(8,128)(2,1)S(1)}, bf16[8,15360]{1,0:T(8,128)(2,1)S(1)}, u32[]{:S(2)}, u32[]{:S(2)}) collective-permute-start(bf16[8,15360]{1,0:T(8,128)(2,1)S(1)} %collective-permute-done.6), channel_id=1, source_target_pairs={{4,0},{5,1},{8,4},{9,5},{12,8},{13,9},{14,12},{15,13},{10,14},{11,... | collective-permute-start | bytes 737288 | tf_op jit(solution)/shard_map/ppermute | solution.py:270
  24.2 10.7 %collective-permute-start.5 = (bf16[8,15360]{1,0:T(8,128)(2,1)S(1)}, bf16[8,15360]{1,0:T(8,128)(2,1)S(1)}, u32[]{:S(2)}, u32[]{:S(2)}) collective-permute-start(bf16[8,15360]{1,0:T(8,128)(2,1)S(1)} %collective-permute-done.4), channel_id=1, source_target_pairs={{4,0},{5,1},{8,4},{9,5},{12,8},{13,9},{14,12},{15,13},{10,14},{11,... | collective-permute-start | bytes 737288 | tf_op jit(solution)/shard_map/ppermute | solution.py:270
  24.2 10.7 %collective-permute-start.2 = (bf16[8,15360]{1,0:T(8,128)(2,1)S(1)}, bf16[8,15360]{1,0:T(8,128)(2,1)S(1)}, u32[]{:S(2)}, u32[]{:S(2)}) collective-permute-start(bf16[8,15360]{1,0:T(8,128)(2,1)S(1)} %collective-permute-done.1), channel_id=1, source_target_pairs={{0,4},{1,5},{4,8},{5,9},{8,12},{9,13},{12,14},{13,15},{14,10},{15,... | collective-permute-start | bytes 737288 | tf_op jit(solution)/shard_map/ppermute | solution.py:269
  26.3 19.4 %collective-permute-start.22 = (bf16[16,15360]{1,0:T(8,128)(2,1)}, bf16[16,15360]{1,0:T(8,128)(2,1)S(1)}, u32[]{:S(2)}, u32[]{:S(2)}) collective-permute-start(bf16[16,15360]{1,0:T(8,128)(2,1)} %param.4), channel_id=1, source_target_pairs={{0,1},{1,0},{2,3},{3,2},{4,5},{5,4},{6,7},{7,6},{8,9},{9,8},{10,11... | collective-permute-start | bytes 1474568 | tf_op jit(solution)/shard_map/ppermute | solution.py:271
  32.8 9.3 %collective-permute-start.12 = (bf16[8,15360]{1,0:T(8,128)(2,1)S(1)}, bf16[8,15360]{1,0:T(8,128)(2,1)S(1)}, u32[]{:S(2)}, u32[]{:S(2)}) collective-permute-start(bf16[8,15360]{1,0:T(8,128)(2,1)S(1)} %collective-permute-done.9), channel_id=1, source_target_pairs={{0,4},{1,5},{4,8},{5,9},{8,12},{9,13},{12,14},{13,15},{14,10},{15,... | collective-permute-start | bytes 737288 | tf_op jit(solution)/shard_map/ppermute | solution.py:269
  34.5 7.5 %collective-permute-start.14 = (bf16[8,15360]{1,0:T(8,128)(2,1)S(1)}, bf16[8,15360]{1,0:T(8,128)(2,1)S(1)}, u32[]{:S(2)}, u32[]{:S(2)}) collective-permute-start(bf16[8,15360]{1,0:T(8,128)(2,1)S(1)} %collective-permute-done.7), channel_id=1, source_target_pairs={{4,0},{5,1},{8,4},{9,5},{12,8},{13,9},{14,12},{15,13},{10,14},{11,... | collective-permute-start | bytes 737288 | tf_op jit(solution)/shard_map/ppermute | solution.py:270
  34.9 8.4 %collective-permute-start.10 = (bf16[8,15360]{1,0:T(8,128)(2,1)S(1)}, bf16[8,15360]{1,0:T(8,128)(2,1)S(1)}, u32[]{:S(2)}, u32[]{:S(2)}) collective-permute-start(bf16[8,15360]{1,0:T(8,128)(2,1)S(1)} %collective-permute-done.2), channel_id=1, source_target_pairs={{0,4},{1,5},{4,8},{5,9},{8,12},{9,13},{12,14},{13,15},{14,10},{15,... | collective-permute-start | bytes 737288 | tf_op jit(solution)/shard_map/ppermute | solution.py:269
  36.5 8.1 %collective-permute-start.11 = (bf16[8,15360]{1,0:T(8,128)(2,1)S(1)}, bf16[8,15360]{1,0:T(8,128)(2,1)S(1)}, u32[]{:S(2)}, u32[]{:S(2)}) collective-permute-start(bf16[8,15360]{1,0:T(8,128)(2,1)S(1)} %collective-permute-done.5), channel_id=1, source_target_pairs={{4,0},{5,1},{8,4},{9,5},{12,8},{13,9},{14,12},{15,13},{10,14},{11,... | collective-permute-start | bytes 737288 | tf_op jit(solution)/shard_map/ppermute | solution.py:270
  42.1 2.5 %collective-permute-start.13 = (bf16[16,15360]{1,0:T(8,128)(2,1)S(1)}, bf16[16,15360]{1,0:T(8,128)(2,1)S(1)}, u32[]{:S(2)}, u32[]{:S(2)}) collective-permute-start(bf16[16,15360]{1,0:T(8,128)(2,1)S(1)} %constant_dynamic-update-slice_fusion.refs_11_), channel_id=1, source_target_pairs={{0,1},{1,0},{2,3},{3,2},{4,5},{5,4},{6,7},{7,6},{8,9},{9,8},{10,11... | collective-permute-start | bytes 1474568 | tf_op jit(solution)/shard_map/ppermute | solution.py:271
  42.2 3.7 %collective-permute-start.21 = (bf16[16,15360]{1,0:T(8,128)(2,1)S(1)}, bf16[16,15360]{1,0:T(8,128)(2,1)S(1)}, u32[]{:S(2)}, u32[]{:S(2)}) collective-permute-start(bf16[16,15360]{1,0:T(8,128)(2,1)S(1)} %constant_dynamic-update-slice_fusion.10.refs_16_), channel_id=1, source_target_pairs={{0,1},{1,0},{2,3},{3,2},{4,5},{5,4},{6,7},{7,6},{8,9},{9,8},{10,11... | collective-permute-start | bytes 1474568 | tf_op jit(solution)/shard_map/ppermute | solution.py:271
  43.3 2.2 %collective-permute-start.15 = (bf16[16,15360]{1,0:T(8,128)(2,1)S(1)}, bf16[16,15360]{1,0:T(8,128)(2,1)S(1)}, u32[]{:S(2)}, u32[]{:S(2)}) collective-permute-start(bf16[16,15360]{1,0:T(8,128)(2,1)S(1)} %constant_dynamic-update-slice_fusion.2.refs_12_), channel_id=1, source_target_pairs={{0,1},{1,0},{2,3},{3,2},{4,5},{5,4},{6,7},{7,6},{8,9},{9,8},{10,11... | collective-permute-start | bytes 1474568 | tf_op jit(solution)/shard_map/ppermute | solution.py:271
  44.6 1.9 %collective-permute-start.19 = (bf16[16,15360]{1,0:T(8,128)(2,1)S(1)}, bf16[16,15360]{1,0:T(8,128)(2,1)S(1)}, u32[]{:S(2)}, u32[]{:S(2)}) collective-permute-start(bf16[16,15360]{1,0:T(8,128)(2,1)S(1)} %constant_dynamic-update-slice_fusion.6.refs_14_), channel_id=1, source_target_pairs={{0,1},{1,0},{2,3},{3,2},{4,5},{5,4},{6,7},{7,6},{8,9},{9,8},{10,11... | collective-permute-start | bytes 1474568 | tf_op jit(solution)/shard_map/ppermute | solution.py:271
  44.6 2.6 %collective-permute-start.20 = (bf16[16,15360]{1,0:T(8,128)(2,1)S(1)}, bf16[16,15360]{1,0:T(8,128)(2,1)S(1)}, u32[]{:S(2)}, u32[]{:S(2)}) collective-permute-start(bf16[16,15360]{1,0:T(8,128)(2,1)S(1)} %constant_dynamic-update-slice_fusion.8.refs_15_), channel_id=1, source_target_pairs={{0,1},{1,0},{2,3},{3,2},{4,5},{5,4},{6,7},{7,6},{8,9},{9,8},{10,11... | collective-permute-start | bytes 1474568 | tf_op jit(solution)/shard_map/ppermute | solution.py:271
  45.5 2.4 %collective-permute-start.18 = (bf16[16,15360]{1,0:T(8,128)(2,1)S(1)}, bf16[16,15360]{1,0:T(8,128)(2,1)S(1)}, u32[]{:S(2)}, u32[]{:S(2)}) collective-permute-start(bf16[16,15360]{1,0:T(8,128)(2,1)S(1)} %constant_dynamic-update-slice_fusion.4.refs_13_), channel_id=1, source_target_pairs={{0,1},{1,0},{2,3},{3,2},{4,5},{5,4},{6,7},{7,6},{8,9},{9,8},{10,11... | collective-permute-start | bytes 1474568 | tf_op jit(solution)/shard_map/ppermute | solution.py:271
  45.6 2.6 %collective-permute-start.16 = (bf16[8,15360]{1,0:T(8,128)(2,1)S(1)}, bf16[8,15360]{1,0:T(8,128)(2,1)S(1)}, u32[]{:S(2)}, u32[]{:S(2)}) collective-permute-start(bf16[8,15360]{1,0:T(8,128)(2,1)S(1)} %collective-permute-done.10.refs_9_), channel_id=1, source_target_pairs={{0,1},{1,0},{2,3},{3,2},{4,5},{5,4},{6,7},{7,6},{8,9},{9,8},{10,11... | collective-permute-start | bytes 737288 | tf_op jit(solution)/shard_map/ppermute | solution.py:271
  46.0 2.6 %collective-permute-start.17 = (bf16[8,15360]{1,0:T(8,128)(2,1)S(1)}, bf16[8,15360]{1,0:T(8,128)(2,1)S(1)}, u32[]{:S(2)}, u32[]{:S(2)}) collective-permute-start(bf16[8,15360]{1,0:T(8,128)(2,1)S(1)} %collective-permute-done.11.refs_10_), channel_id=1, source_target_pairs={{0,1},{1,0},{2,3},{3,2},{4,5},{5,4},{6,7},{7,6},{8,9},{9,8},{10,11... | collective-permute-start | bytes 737288 | tf_op jit(solution)/shard_map/ppermute | solution.py:271
  61.8 1.6 %collective-permute-start.26 = (bf16[8,15360]{1,0:T(8,128)(2,1)S(1)}, bf16[8,15360]{1,0:T(8,128)(2,1)S(1)}, u32[]{:S(2)}, u32[]{:S(2)}) collective-permute-start(bf16[8,15360]{1,0:T(8,128)(2,1)S(1)} %get-tuple-element.95), channel_id=1, source_target_pairs={{0,1},{1,0},{2,3},{3,2},{4,5},{5,4},{6,7},{7,6},{8,9},{9,8},{10,11... | collective-permute-start | bytes 737288 | tf_op jit(solution)/shard_map/ppermute | solution.py:271
  61.8 2.1 %collective-permute-start.28 = (bf16[8,15360]{1,0:T(8,128)(2,1)S(1)}, bf16[8,15360]{1,0:T(8,128)(2,1)S(1)}, u32[]{:S(2)}, u32[]{:S(2)}) collective-permute-start(bf16[8,15360]{1,0:T(8,128)(2,1)S(1)} %get-tuple-element.97), channel_id=1, source_target_pairs={{0,1},{1,0},{2,3},{3,2},{4,5},{5,4},{6,7},{7,6},{8,9},{9,8},{10,11... | collective-permute-start | bytes 737288 | tf_op jit(solution)/shard_map/ppermute | solution.py:271
  62.3 9.5 %collective-permute-start.25 = (bf16[16,15360]{1,0:T(8,128)(2,1)S(1)}, bf16[16,15360]{1,0:T(8,128)(2,1)S(1)}, u32[]{:S(2)}, u32[]{:S(2)}) collective-permute-start(bf16[16,15360]{1,0:T(8,128)(2,1)S(1)} %get-tuple-element.93), channel_id=1, source_target_pairs={{0,1},{1,0},{2,3},{3,2},{4,5},{5,4},{6,7},{7,6},{8,9},{9,8},{10,11... | collective-permute-start | bytes 1474568 | tf_op jit(solution)/shard_map/ppermute | solution.py:271
  63.4 8.0 %collective-permute-start.27 = (bf16[8,15360]{1,0:T(8,128)(2,1)S(1)}, bf16[8,15360]{1,0:T(8,128)(2,1)S(1)}, u32[]{:S(2)}, u32[]{:S(2)}) collective-permute-start(bf16[8,15360]{1,0:T(8,128)(2,1)S(1)} %add_convert_fusion.8), channel_id=1, source_target_pairs={{4,0},{5,1},{8,4},{9,5},{12,8},{13,9},{14,12},{15,13},{10,14},{11,... | collective-permute-start | bytes 737288 | tf_op jit(solution)/shard_map/ppermute | solution.py:270
  64.0 7.9 %collective-permute-start.29 = (bf16[8,15360]{1,0:T(8,128)(2,1)S(1)}, bf16[8,15360]{1,0:T(8,128)(2,1)S(1)}, u32[]{:S(2)}, u32[]{:S(2)}) collective-permute-start(bf16[8,15360]{1,0:T(8,128)(2,1)S(1)} %add_convert_fusion.7), channel_id=1, source_target_pairs={{0,4},{1,5},{4,8},{5,9},{8,12},{9,13},{12,14},{13,15},{14,10},{15,... | collective-permute-start | bytes 737288 | tf_op jit(solution)/shard_map/ppermute | solution.py:269
  65.6 7.7 %collective-permute-start.31 = (bf16[16,15360]{1,0:T(8,128)(2,1)S(1)}, bf16[16,15360]{1,0:T(8,128)(2,1)S(1)}, u32[]{:S(2)}, u32[]{:S(2)}) collective-permute-start(bf16[16,15360]{1,0:T(8,128)(2,1)S(1)} %get-tuple-element.103), channel_id=1, source_target_pairs={{0,1},{1,0},{2,3},{3,2},{4,5},{5,4},{6,7},{7,6},{8,9},{9,8},{10,11... | collective-permute-start | bytes 1474568 | tf_op jit(solution)/shard_map/ppermute | solution.py:271
  72.0 13.2 %collective-permute-start.30 = (bf16[16,15360]{1,0:T(8,128)(2,1)S(1)}, bf16[16,15360]{1,0:T(8,128)(2,1)S(1)}, u32[]{:S(2)}, u32[]{:S(2)}) collective-permute-start(bf16[16,15360]{1,0:T(8,128)(2,1)S(1)} %add_convert_fusion.6), channel_id=1, source_target_pairs={{4,0},{5,1},{8,4},{9,5},{12,8},{13,9},{14,12},{15,13},{10,14},{11,... | collective-permute-start | bytes 1474568 | tf_op jit(solution)/shard_map/ppermute | solution.py:270
  73.5 12.0 %collective-permute-start.32 = (bf16[16,15360]{1,0:T(8,128)(2,1)S(1)}, bf16[16,15360]{1,0:T(8,128)(2,1)S(1)}, u32[]{:S(2)}, u32[]{:S(2)}) collective-permute-start(bf16[16,15360]{1,0:T(8,128)(2,1)S(1)} %add_convert_fusion.5), channel_id=1, source_target_pairs={{0,4},{1,5},{4,8},{5,9},{8,12},{9,13},{12,14},{13,15},{14,10},{15,... | collective-permute-start | bytes 1474568 | tf_op jit(solution)/shard_map/ppermute | solution.py:269
  74.3 11.2 %collective-permute-start.24 = (bf16[16,15360]{1,0:T(8,128)(2,1)S(1)}, bf16[16,15360]{1,0:T(8,128)(2,1)S(1)}, u32[]{:S(2)}, u32[]{:S(2)}) collective-permute-start(bf16[16,15360]{1,0:T(8,128)(2,1)S(1)} %get-tuple-element.91), channel_id=1, source_target_pairs={{0,1},{1,0},{2,3},{3,2},{4,5},{5,4},{6,7},{7,6},{8,9},{9,8},{10,11... | collective-permute-start | bytes 1474568 | tf_op jit(solution)/shard_map/ppermute | solution.py:271
  74.3 13.2 %collective-permute-start.34 = (bf16[16,15360]{1,0:T(8,128)(2,1)S(1)}, bf16[16,15360]{1,0:T(8,128)(2,1)S(1)}, u32[]{:S(2)}, u32[]{:S(2)}) collective-permute-start(bf16[16,15360]{1,0:T(8,128)(2,1)S(1)} %get-tuple-element.111), channel_id=1, source_target_pairs={{0,1},{1,0},{2,3},{3,2},{4,5},{5,4},{6,7},{7,6},{8,9},{9,8},{10,11... | collective-permute-start | bytes 1474568 | tf_op jit(solution)/shard_map/ppermute | solution.py:271
  85.7 11.9 %collective-permute-start.33 = (bf16[16,15360]{1,0:T(8,128)(2,1)S(1)}, bf16[16,15360]{1,0:T(8,128)(2,1)S(1)}, u32[]{:S(2)}, u32[]{:S(2)}) collective-permute-start(bf16[16,15360]{1,0:T(8,128)(2,1)S(1)} %add_convert_fusion.4), channel_id=1, source_target_pairs={{4,0},{5,1},{8,4},{9,5},{12,8},{13,9},{14,12},{15,13},{10,14},{11,... | collective-permute-start | bytes 1474568 | tf_op jit(solution)/shard_map/ppermute | solution.py:270
  87.6 11.1 %collective-permute-start.35 = (bf16[16,15360]{1,0:T(8,128)(2,1)S(1)}, bf16[16,15360]{1,0:T(8,128)(2,1)S(1)}, u32[]{:S(2)}, u32[]{:S(2)}) collective-permute-start(bf16[16,15360]{1,0:T(8,128)(2,1)S(1)} %add_convert_fusion.3), channel_id=1, source_target_pairs={{0,4},{1,5},{4,8},{5,9},{8,12},{9,13},{12,14},{13,15},{14,10},{15,... | collective-permute-start | bytes 1474568 | tf_op jit(solution)/shard_map/ppermute | solution.py:269
  88.0 10.7 %collective-permute-start.23 = (bf16[16,15360]{1,0:T(8,128)(2,1)S(1)}, bf16[16,15360]{1,0:T(8,128)(2,1)S(1)}, u32[]{:S(2)}, u32[]{:S(2)}) collective-permute-start(bf16[16,15360]{1,0:T(8,128)(2,1)S(1)} %get-tuple-element.89), channel_id=1, source_target_pairs={{0,1},{1,0},{2,3},{3,2},{4,5},{5,4},{6,7},{7,6},{8,9},{9,8},{10,11... | collective-permute-start | bytes 1474568 | tf_op jit(solution)/shard_map/ppermute | solution.py:271
  88.0 12.4 %collective-permute-start.37 = (bf16[16,15360]{1,0:T(8,128)(2,1)S(1)}, bf16[16,15360]{1,0:T(8,128)(2,1)S(1)}, u32[]{:S(2)}, u32[]{:S(2)}) collective-permute-start(bf16[16,15360]{1,0:T(8,128)(2,1)S(1)} %get-tuple-element.119), channel_id=1, source_target_pairs={{0,1},{1,0},{2,3},{3,2},{4,5},{5,4},{6,7},{7,6},{8,9},{9,8},{10,11... | collective-permute-start | bytes 1474568 | tf_op jit(solution)/shard_map/ppermute | solution.py:271
  98.9 11.1 %collective-permute-start.36 = (bf16[16,15360]{1,0:T(8,128)(2,1)S(1)}, bf16[16,15360]{1,0:T(8,128)(2,1)S(1)}, u32[]{:S(2)}, u32[]{:S(2)}) collective-permute-start(bf16[16,15360]{1,0:T(8,128)(2,1)S(1)} %add_convert_fusion.2), channel_id=1, source_target_pairs={{4,0},{5,1},{8,4},{9,5},{12,8},{13,9},{14,12},{15,13},{10,14},{11,... | collective-permute-start | bytes 1474568 | tf_op jit(solution)/shard_map/ppermute | solution.py:270
  100.6 11.1 %collective-permute-start.38 = (bf16[16,15360]{1,0:T(8,128)(2,1)S(1)}, bf16[16,15360]{1,0:T(8,128)(2,1)S(1)}, u32[]{:S(2)}, u32[]{:S(2)}) collective-permute-start(bf16[16,15360]{1,0:T(8,128)(2,1)S(1)} %add_convert_fusion.1), channel_id=1, source_target_pairs={{0,4},{1,5},{4,8},{5,9},{8,12},{9,13},{12,14},{13,15},{14,10},{15,... | collective-permute-start | bytes 1474568 | tf_op jit(solution)/shard_map/ppermute | solution.py:269
  101.3 10.4 %collective-permute-start.39 = (bf16[16,15360]{1,0:T(8,128)(2,1)S(1)}, bf16[16,15360]{1,0:T(8,128)(2,1)S(1)}, u32[]{:S(2)}, u32[]{:S(2)}) collective-permute-start(bf16[16,15360]{1,0:T(8,128)(2,1)S(1)} %get-tuple-element.127), channel_id=1, source_target_pairs={{0,1},{1,0},{2,3},{3,2},{4,5},{5,4},{6,7},{7,6},{8,9},{9,8},{10,11... | collective-permute-start | bytes 1474568 | tf_op jit(solution)/shard_map/ppermute | solution.py:271

commit v6 on v5

--- a/solution.py
+++ b/solution.py
@@ -308,7 +308,7 @@
     here = lambda k: own[k].astype(F32) + swap(other[k]).astype(F32)
     sent = here("low").astype(BF16), here("high").astype(BF16)
     pieces = slots * CUT
-    shares = [0] + [pieces - pieces * 9 * step // 32 for step in range(3, -1, -1)]
+    shares = [0] + [pieces * part // 16 for part in (2, 7, 12, 16)]
     shares = [0] * (reach - 3) + shares if reach >= 3 else [0] * (reach + 1) + [pieces]
     done = None
     for step in range(reach, -1, -1):

time: 113 us -> 114 us (level)
  transfers between devices with their start and end apart: 40 -> 40, of which waited for: 24 -> 23; matrix products, arithmetic and copies ran while one was open for 3% -> 2% of each run, Pallas kernels for 29% -> 30%
where the time goes in v6:
time: 114 us
  Pallas kernels  46.6 us (41%)
  waiting for transfers between devices  33.5 us (29%)
  starting transfers between devices  27.6 us (24%)
  other arithmetic  3.63 us (3%)
  local copies, waits for them, and re-layouts  1.31 us (1%)
    pallas_call x4, Pallas kernels, update_stats(): pl.pallas_call(functools.partial(stat_kernel, len(grads), base, length),...  30.2 us
    ppermute x11, waiting for transfers between devices, body(): back = lambda v: lax.ppermute(v, 'row', backward)  19.8 us
    ppermute x11, starting transfers between devices, body(): ahead = lambda v: lax.ppermute(v, 'row', forward)  17.8 us
    pallas_call x1, Pallas kernels, partial_sums(): pl.pallas_call(functools.partial(part_kernel, len(grads)), out_shape=[jax...  13 us
    ppermute x11, waiting for transfers between devices, body(): ahead = lambda v: lax.ppermute(v, 'row', forward)  10.1 us
    ppermute x11, starting transfers between devices, body(): back = lambda v: lax.ppermute(v, 'row', backward)  6.14 us
    ppermute x18, starting transfers between devices, body(): lax.ppermute(v, 'row', [(i, i ^ 1) for i in range(devices)])  3.65 us
    ppermute x18, waiting for transfers between devices, body(): lax.ppermute(v, 'row', [(i, i ^ 1) for i in range(devices)])  3.57 us
  transfers between devices with their start and end apart: 40, of which 23 were waited for; matrix products, arithmetic and copies ran while one was open for 2% of the time, Pallas kernels for 30%

profile of v6, /device:TPU:0, one launch (start us, length us, event | category | flops | bytes accessed | tf_op | source)
XLA Modules:
  0.0 113.5 jit_solution(8450295047246317096)
XLA Ops:
  0.6 1.1 fusion.14
  1.7 3.1 %collective-permute-start = (bf16[8,15360]{1,0:T(8,128)(2,1)S(1)}, bf16[8,15360]{1,0:T(8,128)(2,1)S(1)}, u32[]{:S(2)}, u32[]{:S(2)}) collective-permute-start(bf16[8,15360]{1,0:T(8,128)(2,1)S(1)} %get-tuple-element.133.refs_17_), channel_id=1, source_target_pairs={{0,4},{1,5},{4,8},{5,9},{8,12},{9,13},{12,14},{13,15},{14,10},{15,... | collective-permute-start | bytes 737288 | tf_op jit(solution)/shard_map/ppermute | solution.py:269
  4.8 2.0 %collective-permute-start.8 = (bf16[8,15360]{1,0:T(8,128)(2,1)S(1)}, bf16[8,15360]{1,0:T(8,128)(2,1)S(1)}, u32[]{:S(2)}, u32[]{:S(2)}) collective-permute-start(bf16[8,15360]{1,0:T(8,128)(2,1)S(1)} %get-tuple-element.132.refs_18_), channel_id=1, source_target_pairs={{0,4},{1,5},{4,8},{5,9},{8,12},{9,13},{12,14},{13,15},{14,10},{15,... | collective-permute-start | bytes 737288 | tf_op jit(solution)/shard_map/ppermute | solution.py:269
  6.8 0.8 subtract_add_fusion
  7.6 0.7 compare_convert_fusion.live_ref
  8.3 3.2 %collective-permute-done = bf16[8,15360]{1,0:T(8,128)(2,1)S(1)} collective-permute-done((bf16[8,15360]{1,0:T(8,128)(2,1)S(1)}, bf16[8,15360]{1,0:T(8,128)(2,1)S(1)}, u32[]{:S(2)}, u32[]{:S(2)}) %collective-permute-start) | collective-permute-done | bytes 245792 | tf_op jit(solution)/shard_map/ppermute | solution.py:269
  11.5 2.2 %collective-permute-done.3 = bf16[8,15360]{1,0:T(8,128)(2,1)S(1)} collective-permute-done((bf16[8,15360]{1,0:T(8,128)(2,1)S(1)}, bf16[8,15360]{1,0:T(8,128)(2,1)S(1)}, u32[]{:S(2)}, u32[]{:S(2)}) %collective-permute-start.3) | collective-permute-done | bytes 245792 | tf_op jit(solution)/shard_map/ppermute | solution.py:270
  13.7 2.0 %collective-permute-start.1 = (bf16[8,15360]{1,0:T(8,128)(2,1)S(1)}, bf16[8,15360]{1,0:T(8,128)(2,1)S(1)}, u32[]{:S(2)}, u32[]{:S(2)}) collective-permute-start(bf16[8,15360]{1,0:T(8,128)(2,1)S(1)} %collective-permute-done), channel_id=1, source_target_pairs={{0,4},{1,5},{4,8},{5,9},{8,12},{9,13},{12,14},{13,15},{14,10},{15,... | collective-permute-start | bytes 737288 | tf_op jit(solution)/shard_map/ppermute | solution.py:269
  15.7 1.1 collective-permute-done.8
  16.8 2.1 %collective-permute-start.9 = (bf16[8,15360]{1,0:T(8,128)(2,1)S(1)}, bf16[8,15360]{1,0:T(8,128)(2,1)S(1)}, u32[]{:S(2)}, u32[]{:S(2)}) collective-permute-start(bf16[8,15360]{1,0:T(8,128)(2,1)S(1)} %collective-permute-done.8), channel_id=1, source_target_pairs={{0,4},{1,5},{4,8},{5,9},{8,12},{9,13},{12,14},{13,15},{14,10},{15,... | collective-permute-start | bytes 737288 | tf_op jit(solution)/shard_map/ppermute | solution.py:269
  19.0 5.3 %collective-permute-done.4 = bf16[8,15360]{1,0:T(8,128)(2,1)S(1)} collective-permute-done((bf16[8,15360]{1,0:T(8,128)(2,1)S(1)}, bf16[8,15360]{1,0:T(8,128)(2,1)S(1)}, u32[]{:S(2)}, u32[]{:S(2)}) %collective-permute-start.4) | collective-permute-done | bytes 245792 | tf_op jit(solution)/shard_map/ppermute | solution.py:270
  24.2 2.0 %collective-permute-start.2 = (bf16[8,15360]{1,0:T(8,128)(2,1)S(1)}, bf16[8,15360]{1,0:T(8,128)(2,1)S(1)}, u32[]{:S(2)}, u32[]{:S(2)}) collective-permute-start(bf16[8,15360]{1,0:T(8,128)(2,1)S(1)} %collective-permute-done.1), channel_id=1, source_target_pairs={{0,4},{1,5},{4,8},{5,9},{8,12},{9,13},{12,14},{13,15},{14,10},{15,... | collective-permute-start | bytes 737288 | tf_op jit(solution)/shard_map/ppermute | solution.py:269
  26.3 1.6 %collective-permute-done.9 = bf16[8,15360]{1,0:T(8,128)(2,1)S(1)} collective-permute-done((bf16[8,15360]{1,0:T(8,128)(2,1)S(1)}, bf16[8,15360]{1,0:T(8,128)(2,1)S(1)}, u32[]{:S(2)}, u32[]{:S(2)}) %collective-permute-start.9) | collective-permute-done | bytes 245792 | tf_op jit(solution)/shard_map/ppermute | solution.py:269
  27.9 1.6 %collective-permute-done.7 = bf16[8,15360]{1,0:T(8,128)(2,1)S(1)} collective-permute-done((bf16[8,15360]{1,0:T(8,128)(2,1)S(1)}, bf16[8,15360]{1,0:T(8,128)(2,1)S(1)}, u32[]{:S(2)}, u32[]{:S(2)}) %collective-permute-start.7) | collective-permute-done | bytes 245792 | tf_op jit(solution)/shard_map/ppermute | solution.py:270
  29.5 3.3 %shard_map.59 = (bf16[2,1024,1024]{2,1,0:T(8,128)(2,1)S(1)}, s32[8]{0:T(128)S(1)}) custom-call(s32[8]{0:T(128)S(1)} %get-tuple-element.68.after_ref, bf16[8,1024,1024]{2,1,0:T(8,128)(2,1)} %refs_20_.1), custom_call_target="tpu_custom_call" | custom-call | bytes 4194304 | tf_op jit(solution)/shard_map/pallas_call | solution.py:120
  32.8 1.6 %collective-permute-start.12 = (bf16[8,15360]{1,0:T(8,128)(2,1)S(1)}, bf16[8,15360]{1,0:T(8,128)(2,1)S(1)}, u32[]{:S(2)}, u32[]{:S(2)}) collective-permute-start(bf16[8,15360]{1,0:T(8,128)(2,1)S(1)} %collective-permute-done.9), channel_id=1, source_target_pairs={{0,4},{1,5},{4,8},{5,9},{8,12},{9,13},{12,14},{13,15},{14,10},{15,... | collective-permute-start | bytes 737288 | tf_op jit(solution)/shard_map/ppermute | solution.py:269
  34.5 0.4 collective-permute-start.14
  34.9 1.6 %collective-permute-start.10 = (bf16[8,15360]{1,0:T(8,128)(2,1)S(1)}, bf16[8,15360]{1,0:T(8,128)(2,1)S(1)}, u32[]{:S(2)}, u32[]{:S(2)}) collective-permute-start(bf16[8,15360]{1,0:T(8,128)(2,1)S(1)} %collective-permute-done.2), channel_id=1, source_target_pairs={{0,4},{1,5},{4,8},{5,9},{8,12},{9,13},{12,14},{13,15},{14,10},{15,... | collective-permute-start | bytes 737288 | tf_op jit(solution)/shard_map/ppermute | solution.py:269
  36.5 0.5 collective-permute-start.11
  37.0 4.9 %collective-permute-done.14 = bf16[8,15360]{1,0:T(8,128)(2,1)S(1)} collective-permute-done((bf16[8,15360]{1,0:T(8,128)(2,1)S(1)}, bf16[8,15360]{1,0:T(8,128)(2,1)S(1)}, u32[]{:S(2)}, u32[]{:S(2)}) %collective-permute-start.14) | collective-permute-done | bytes 245792 | tf_op jit(solution)/shard_map/ppermute | solution.py:270
  42.2 0.6 collective-permute-start.21
  42.8 0.4 collective-permute-done.10.refs_9_
  43.3 1.3 %collective-permute-done.11.refs_10_ = bf16[8,15360]{1,0:T(8,128)(2,1)S(1)} collective-permute-done((bf16[8,15360]{1,0:T(8,128)(2,1)S(1)}, bf16[8,15360]{1,0:T(8,128)(2,1)S(1)}, u32[]{:S(2)}, u32[]{:S(2)}) %collective-permute-start.11) | collective-permute-done | bytes 245792 | tf_op jit(solution)/shard_map/ppermute | solution.py:270
  44.6 0.5 collective-permute-start.20
  46.4 0.7 collective-permute-done.20.refs_6_
  47.1 0.7 collective-permute-done.18.refs_4_
  48.6 13.0 %shard_map.60 = (bf16[8,15360]{1,0:T(8,128)(2,1)S(1)}, bf16[8,15360]{1,0:T(8,128)(2,1)S(1)}, bf16[16,15360]{1,0:T(8,128)(2,1)S(1)}, bf16[16,15360]{1,0:T(8,128)(...) custom-call(s32[8]{0:T(128)S(1)} %get-tuple-element.121.first_ref, ...), custom_call_target="tpu_custom_call" | custom-call | flops 8589934592 | bytes 16777216 | tf_op jit(solution)/shard_map/pallas_call | solution.py:138
  62.4 0.7 collective-permute-done.26
  63.2 0.6 collective-permute-start.27
  63.8 1.6 %collective-permute-start.29 = (bf16[8,15360]{1,0:T(8,128)(2,1)S(1)}, bf16[8,15360]{1,0:T(8,128)(2,1)S(1)}, u32[]{:S(2)}, u32[]{:S(2)}) collective-permute-start(bf16[8,15360]{1,0:T(8,128)(2,1)S(1)} %add_convert_fusion.7), channel_id=1, source_target_pairs={{0,4},{1,5},{4,8},{5,9},{8,12},{9,13},{12,14},{13,15},{14,10},{15,... | collective-permute-start | bytes 737288 | tf_op jit(solution)/shard_map/ppermute | solution.py:269
  65.4 4.3 %shard_map.61.refs_20_ = f32[8,1024,1024]{2,1,0:T(8,128)} custom-call(s32[8]{0:T(128)S(1)} %get-tuple-element.121.first_ref, s32[8]{0:T(128)S(1)} %get-tuple-element.122.second_ref, s32[8]{0:T(128)S(1)} %compare_convert_fusion.live_ref, bf16[8,15360]{1,0:T(8,128)(2,1)S(1)} %collective-permute-done.16.refs_0_, ...), custom_call_target="tpu_custom_call" | custom-call | flops 536870912 | bytes 8388608 | tf_op jit(solution)/shard_map/pallas_call | solution.py:227
  69.7 1.6 %collective-permute-done.27 = bf16[8,15360]{1,0:T(8,128)(2,1)S(1)} collective-permute-done((bf16[8,15360]{1,0:T(8,128)(2,1)S(1)}, bf16[8,15360]{1,0:T(8,128)(2,1)S(1)}, u32[]{:S(2)}, u32[]{:S(2)}) %collective-permute-start.27) | collective-permute-done | bytes 245792 | tf_op jit(solution)/shard_map/ppermute | solution.py:270
  71.9 1.2 %collective-permute-start.30 = (bf16[16,15360]{1,0:T(8,128)(2,1)S(1)}, bf16[16,15360]{1,0:T(8,128)(2,1)S(1)}, u32[]{:S(2)}, u32[]{:S(2)}) collective-permute-start(bf16[16,15360]{1,0:T(8,128)(2,1)S(1)} %add_convert_fusion.6), channel_id=1, source_target_pairs={{4,0},{5,1},{8,4},{9,5},{12,8},{13,9},{14,12},{15,13},{10,14},{11,... | collective-permute-start | bytes 1474568 | tf_op jit(solution)/shard_map/ppermute | solution.py:270
  73.2 1.0 collective-permute-start.32
  74.2 0.5 collective-permute-start.34
  74.7 9.1 %shard_map.62.refs_20_ = f32[8,1024,1024]{2,1,0:T(8,128)} custom-call(s32[8]{0:T(128)S(1)} %get-tuple-element.121.first_ref, s32[8]{0:T(128)S(1)} %get-tuple-element.122.second_ref, s32[8]{0:T(128)S(1)} %compare_convert_fusion.live_ref, bf16[8,15360]{1,0:T(8,128)(2,1)S(1)} %collective-permute-done.16.refs_0_, ...), custom_call_target="tpu_custom_call", output_to_operand_aliasing={{}: (23, {})} | custom-call | flops 1342177280 | bytes 20971520 | tf_op jit(solution)/shard_map/pallas_call | solution.py:227
  83.8 0.6 collective-permute-done.30
  84.4 0.9 collective-permute-done.32
  85.5 1.8 %collective-permute-start.33 = (bf16[16,15360]{1,0:T(8,128)(2,1)S(1)}, bf16[16,15360]{1,0:T(8,128)(2,1)S(1)}, u32[]{:S(2)}, u32[]{:S(2)}) collective-permute-start(bf16[16,15360]{1,0:T(8,128)(2,1)S(1)} %add_convert_fusion.4), channel_id=1, source_target_pairs={{4,0},{5,1},{8,4},{9,5},{12,8},{13,9},{14,12},{15,13},{10,14},{11,... | collective-permute-start | bytes 1474568 | tf_op jit(solution)/shard_map/ppermute | solution.py:270
  87.8 0.5 collective-permute-start.37
  88.3 9.1 %shard_map.63.refs_20_ = f32[8,1024,1024]{2,1,0:T(8,128)} custom-call(s32[8]{0:T(128)S(1)} %get-tuple-element.121.first_ref, s32[8]{0:T(128)S(1)} %get-tuple-element.122.second_ref, s32[8]{0:T(128)S(1)} %compare_convert_fusion.live_ref, bf16[8,15360]{1,0:T(8,128)(2,1)S(1)} %collective-permute-done.16.refs_0_, ...), custom_call_target="tpu_custom_call", output_to_operand_aliasing={{}: (23, {})} | custom-call | flops 1342177280 | bytes 20971520 | tf_op jit(solution)/shard_map/pallas_call | solution.py:227
  97.4 0.9 collective-permute-done.35
  98.6 1.6 %collective-permute-start.36 = (bf16[16,15360]{1,0:T(8,128)(2,1)S(1)}, bf16[16,15360]{1,0:T(8,128)(2,1)S(1)}, u32[]{:S(2)}, u32[]{:S(2)}) collective-permute-start(bf16[16,15360]{1,0:T(8,128)(2,1)S(1)} %add_convert_fusion.2), channel_id=1, source_target_pairs={{4,0},{5,1},{8,4},{9,5},{12,8},{13,9},{14,12},{15,13},{10,14},{11,... | collective-permute-start | bytes 1474568 | tf_op jit(solution)/shard_map/ppermute | solution.py:270
  100.4 0.5 collective-permute-start.38
  100.9 7.7 %shard_map.64 = f32[8,1024,1024]{2,1,0:T(8,128)} custom-call(s32[8]{0:T(128)S(1)} %get-tuple-element.121.first_ref, s32[8]{0:T(128)S(1)} %get-tuple-element.122.second_ref, s32[8]{0:T(128)S(1)} %compare_convert_fusion.live_ref, bf16[8,15360]{1,0:T(8,128)(2,1)S(1)} %collective-permute-done.16.refs_0_, ...), custom_call_target="tpu_custom_call", output_to_operand_aliasing={{}: (23, {})} | custom-call | flops 1073741824 | bytes 16777216 | tf_op jit(solution)/shard_map/pallas_call | solution.py:227
  108.5 2.3 %collective-permute-done.36 = bf16[16,15360]{1,0:T(8,128)(2,1)S(1)} collective-permute-done((bf16[16,15360]{1,0:T(8,128)(2,1)S(1)}, bf16[16,15360]{1,0:T(8,128)(2,1)S(1)}, u32[]{:S(2)}, u32[]{:S(2)}) %collective-permute-start.36) | collective-permute-done | bytes 491552 | tf_op jit(solution)/shard_map/ppermute | solution.py:270
  110.8 1.7 %collective-permute-done.38 = bf16[16,15360]{1,0:T(8,128)(2,1)S(1)} collective-permute-done((bf16[16,15360]{1,0:T(8,128)(2,1)S(1)}, bf16[16,15360]{1,0:T(8,128)(2,1)S(1)}, u32[]{:S(2)}, u32[]{:S(2)}) %collective-permute-start.38) | collective-permute-done | bytes 491552 | tf_op jit(solution)/shard_map/ppermute | solution.py:269
  112.5 1.0 add_convert_fusion
  (62 shorter events, 5.1 us)
Async XLA Ops:
  1.7 9.8 %collective-permute-start = (bf16[8,15360]{1,0:T(8,128)(2,1)S(1)}, bf16[8,15360]{1,0:T(8,128)(2,1)S(1)}, u32[]{:S(2)}, u32[]{:S(2)}) collective-permute-start(bf16[8,15360]{1,0:T(8,128)(2,1)S(1)} %get-tuple-element.133.refs_17_), channel_id=1, source_target_pairs={{0,4},{1,5},{4,8},{5,9},{8,12},{9,13},{12,14},{13,15},{14,10},{15,... | collective-permute-start | bytes 737288 | tf_op jit(solution)/shard_map/ppermute | solution.py:269
  4.8 8.9 %collective-permute-start.3 = (bf16[8,15360]{1,0:T(8,128)(2,1)S(1)}, bf16[8,15360]{1,0:T(8,128)(2,1)S(1)}, u32[]{:S(2)}, u32[]{:S(2)}) collective-permute-start(bf16[8,15360]{1,0:T(8,128)(2,1)S(1)} %get-tuple-element.132.refs_18_), channel_id=1, source_target_pairs={{4,0},{5,1},{8,4},{9,5},{12,8},{13,9},{14,12},{15,13},{10,14},{11,... | collective-permute-start | bytes 737288 | tf_op jit(solution)/shard_map/ppermute | solution.py:270
  4.8 12.0 %collective-permute-start.8 = (bf16[8,15360]{1,0:T(8,128)(2,1)S(1)}, bf16[8,15360]{1,0:T(8,128)(2,1)S(1)}, u32[]{:S(2)}, u32[]{:S(2)}) collective-permute-start(bf16[8,15360]{1,0:T(8,128)(2,1)S(1)} %get-tuple-element.132.refs_18_), channel_id=1, source_target_pairs={{0,4},{1,5},{4,8},{5,9},{8,12},{9,13},{12,14},{13,15},{14,10},{15,... | collective-permute-start | bytes 737288 | tf_op jit(solution)/shard_map/ppermute | solution.py:269
  6.8 12.1 %collective-permute-start.6 = (bf16[8,15360]{1,0:T(8,128)(2,1)S(1)}, bf16[8,15360]{1,0:T(8,128)(2,1)S(1)}, u32[]{:S(2)}, u32[]{:S(2)}) collective-permute-start(bf16[8,15360]{1,0:T(8,128)(2,1)S(1)} %get-tuple-element.133.refs_17_), channel_id=1, source_target_pairs={{4,0},{5,1},{8,4},{9,5},{12,8},{13,9},{14,12},{15,13},{10,14},{11,... | collective-permute-start | bytes 737288 | tf_op jit(solution)/shard_map/ppermute | solution.py:270
  13.7 10.5 %collective-permute-start.4 = (bf16[8,15360]{1,0:T(8,128)(2,1)S(1)}, bf16[8,15360]{1,0:T(8,128)(2,1)S(1)}, u32[]{:S(2)}, u32[]{:S(2)}) collective-permute-start(bf16[8,15360]{1,0:T(8,128)(2,1)S(1)} %collective-permute-done.3), channel_id=1, source_target_pairs={{4,0},{5,1},{8,4},{9,5},{12,8},{13,9},{14,12},{15,13},{10,14},{11,... | collective-permute-start | bytes 737288 | tf_op jit(solution)/shard_map/ppermute | solution.py:270
  13.7 10.5 %collective-permute-start.1 = (bf16[8,15360]{1,0:T(8,128)(2,1)S(1)}, bf16[8,15360]{1,0:T(8,128)(2,1)S(1)}, u32[]{:S(2)}, u32[]{:S(2)}) collective-permute-start(bf16[8,15360]{1,0:T(8,128)(2,1)S(1)} %collective-permute-done), channel_id=1, source_target_pairs={{0,4},{1,5},{4,8},{5,9},{8,12},{9,13},{12,14},{13,15},{14,10},{15,... | collective-permute-start | bytes 737288 | tf_op jit(solution)/shard_map/ppermute | solution.py:269
  16.8 11.1 %collective-permute-start.9 = (bf16[8,15360]{1,0:T(8,128)(2,1)S(1)}, bf16[8,15360]{1,0:T(8,128)(2,1)S(1)}, u32[]{:S(2)}, u32[]{:S(2)}) collective-permute-start(bf16[8,15360]{1,0:T(8,128)(2,1)S(1)} %collective-permute-done.8), channel_id=1, source_target_pairs={{0,4},{1,5},{4,8},{5,9},{8,12},{9,13},{12,14},{13,15},{14,10},{15,... | collective-permute-start | bytes 737288 | tf_op jit(solution)/shard_map/ppermute | solution.py:269
  19.0 10.5 %collective-permute-start.7 = (bf16[8,15360]{1,0:T(8,128)(2,1)S(1)}, bf16[8,15360]{1,0:T(8,128)(2,1)S(1)}, u32[]{:S(2)}, u32[]{:S(2)}) collective-permute-start(bf16[8,15360]{1,0:T(8,128)(2,1)S(1)} %collective-permute-done.6), channel_id=1, source_target_pairs={{4,0},{5,1},{8,4},{9,5},{12,8},{13,9},{14,12},{15,13},{10,14},{11,... | collective-permute-start | bytes 737288 | tf_op jit(solution)/shard_map/ppermute | solution.py:270
  24.2 10.7 %collective-permute-start.5 = (bf16[8,15360]{1,0:T(8,128)(2,1)S(1)}, bf16[8,15360]{1,0:T(8,128)(2,1)S(1)}, u32[]{:S(2)}, u32[]{:S(2)}) collective-permute-start(bf16[8,15360]{1,0:T(8,128)(2,1)S(1)} %collective-permute-done.4), channel_id=1, source_target_pairs={{4,0},{5,1},{8,4},{9,5},{12,8},{13,9},{14,12},{15,13},{10,14},{11,... | collective-permute-start | bytes 737288 | tf_op jit(solution)/shard_map/ppermute | solution.py:270
  24.2 10.7 %collective-permute-start.2 = (bf16[8,15360]{1,0:T(8,128)(2,1)S(1)}, bf16[8,15360]{1,0:T(8,128)(2,1)S(1)}, u32[]{:S(2)}, u32[]{:S(2)}) collective-permute-start(bf16[8,15360]{1,0:T(8,128)(2,1)S(1)} %collective-permute-done.1), channel_id=1, source_target_pairs={{0,4},{1,5},{4,8},{5,9},{8,12},{9,13},{12,14},{13,15},{14,10},{15,... | collective-permute-start | bytes 737288 | tf_op jit(solution)/shard_map/ppermute | solution.py:269
  26.3 19.4 %collective-permute-start.22 = (bf16[16,15360]{1,0:T(8,128)(2,1)}, bf16[16,15360]{1,0:T(8,128)(2,1)S(1)}, u32[]{:S(2)}, u32[]{:S(2)}) collective-permute-start(bf16[16,15360]{1,0:T(8,128)(2,1)} %param.4), channel_id=1, source_target_pairs={{0,1},{1,0},{2,3},{3,2},{4,5},{5,4},{6,7},{7,6},{8,9},{9,8},{10,11... | collective-permute-start | bytes 1474568 | tf_op jit(solution)/shard_map/ppermute | solution.py:271
  32.8 9.3 %collective-permute-start.12 = (bf16[8,15360]{1,0:T(8,128)(2,1)S(1)}, bf16[8,15360]{1,0:T(8,128)(2,1)S(1)}, u32[]{:S(2)}, u32[]{:S(2)}) collective-permute-start(bf16[8,15360]{1,0:T(8,128)(2,1)S(1)} %collective-permute-done.9), channel_id=1, source_target_pairs={{0,4},{1,5},{4,8},{5,9},{8,12},{9,13},{12,14},{13,15},{14,10},{15,... | collective-permute-start | bytes 737288 | tf_op jit(solution)/shard_map/ppermute | solution.py:269
  34.5 7.5 %collective-permute-start.14 = (bf16[8,15360]{1,0:T(8,128)(2,1)S(1)}, bf16[8,15360]{1,0:T(8,128)(2,1)S(1)}, u32[]{:S(2)}, u32[]{:S(2)}) collective-permute-start(bf16[8,15360]{1,0:T(8,128)(2,1)S(1)} %collective-permute-done.7), channel_id=1, source_target_pairs={{4,0},{5,1},{8,4},{9,5},{12,8},{13,9},{14,12},{15,13},{10,14},{11,... | collective-permute-start | bytes 737288 | tf_op jit(solution)/shard_map/ppermute | solution.py:270
  34.9 8.4 %collective-permute-start.10 = (bf16[8,15360]{1,0:T(8,128)(2,1)S(1)}, bf16[8,15360]{1,0:T(8,128)(2,1)S(1)}, u32[]{:S(2)}, u32[]{:S(2)}) collective-permute-start(bf16[8,15360]{1,0:T(8,128)(2,1)S(1)} %collective-permute-done.2), channel_id=1, source_target_pairs={{0,4},{1,5},{4,8},{5,9},{8,12},{9,13},{12,14},{13,15},{14,10},{15,... | collective-permute-start | bytes 737288 | tf_op jit(solution)/shard_map/ppermute | solution.py:269
  36.5 8.1 %collective-permute-start.11 = (bf16[8,15360]{1,0:T(8,128)(2,1)S(1)}, bf16[8,15360]{1,0:T(8,128)(2,1)S(1)}, u32[]{:S(2)}, u32[]{:S(2)}) collective-permute-start(bf16[8,15360]{1,0:T(8,128)(2,1)S(1)} %collective-permute-done.5), channel_id=1, source_target_pairs={{4,0},{5,1},{8,4},{9,5},{12,8},{13,9},{14,12},{15,13},{10,14},{11,... | collective-permute-start | bytes 737288 | tf_op jit(solution)/shard_map/ppermute | solution.py:270
  42.1 2.5 %collective-permute-start.13 = (bf16[16,15360]{1,0:T(8,128)(2,1)S(1)}, bf16[16,15360]{1,0:T(8,128)(2,1)S(1)}, u32[]{:S(2)}, u32[]{:S(2)}) collective-permute-start(bf16[16,15360]{1,0:T(8,128)(2,1)S(1)} %constant_dynamic-update-slice_fusion.refs_11_), channel_id=1, source_target_pairs={{0,1},{1,0},{2,3},{3,2},{4,5},{5,4},{6,7},{7,6},{8,9},{9,8},{10,11... | collective-permute-start | bytes 1474568 | tf_op jit(solution)/shard_map/ppermute | solution.py:271
  42.2 3.7 %collective-permute-start.21 = (bf16[16,15360]{1,0:T(8,128)(2,1)S(1)}, bf16[16,15360]{1,0:T(8,128)(2,1)S(1)}, u32[]{:S(2)}, u32[]{:S(2)}) collective-permute-start(bf16[16,15360]{1,0:T(8,128)(2,1)S(1)} %constant_dynamic-update-slice_fusion.10.refs_16_), channel_id=1, source_target_pairs={{0,1},{1,0},{2,3},{3,2},{4,5},{5,4},{6,7},{7,6},{8,9},{9,8},{10,11... | collective-permute-start | bytes 1474568 | tf_op jit(solution)/shard_map/ppermute | solution.py:271
  43.3 2.2 %collective-permute-start.15 = (bf16[16,15360]{1,0:T(8,128)(2,1)S(1)}, bf16[16,15360]{1,0:T(8,128)(2,1)S(1)}, u32[]{:S(2)}, u32[]{:S(2)}) collective-permute-start(bf16[16,15360]{1,0:T(8,128)(2,1)S(1)} %constant_dynamic-update-slice_fusion.2.refs_12_), channel_id=1, source_target_pairs={{0,1},{1,0},{2,3},{3,2},{4,5},{5,4},{6,7},{7,6},{8,9},{9,8},{10,11... | collective-permute-start | bytes 1474568 | tf_op jit(solution)/shard_map/ppermute | solution.py:271
  44.6 1.9 %collective-permute-start.19 = (bf16[16,15360]{1,0:T(8,128)(2,1)S(1)}, bf16[16,15360]{1,0:T(8,128)(2,1)S(1)}, u32[]{:S(2)}, u32[]{:S(2)}) collective-permute-start(bf16[16,15360]{1,0:T(8,128)(2,1)S(1)} %constant_dynamic-update-slice_fusion.6.refs_14_), channel_id=1, source_target_pairs={{0,1},{1,0},{2,3},{3,2},{4,5},{5,4},{6,7},{7,6},{8,9},{9,8},{10,11... | collective-permute-start | bytes 1474568 | tf_op jit(solution)/shard_map/ppermute | solution.py:271
  44.6 2.6 %collective-permute-start.20 = (bf16[16,15360]{1,0:T(8,128)(2,1)S(1)}, bf16[16,15360]{1,0:T(8,128)(2,1)S(1)}, u32[]{:S(2)}, u32[]{:S(2)}) collective-permute-start(bf16[16,15360]{1,0:T(8,128)(2,1)S(1)} %constant_dynamic-update-slice_fusion.8.refs_15_), channel_id=1, source_target_pairs={{0,1},{1,0},{2,3},{3,2},{4,5},{5,4},{6,7},{7,6},{8,9},{9,8},{10,11... | collective-permute-start | bytes 1474568 | tf_op jit(solution)/shard_map/ppermute | solution.py:271
  45.5 2.4 %collective-permute-start.18 = (bf16[16,15360]{1,0:T(8,128)(2,1)S(1)}, bf16[16,15360]{1,0:T(8,128)(2,1)S(1)}, u32[]{:S(2)}, u32[]{:S(2)}) collective-permute-start(bf16[16,15360]{1,0:T(8,128)(2,1)S(1)} %constant_dynamic-update-slice_fusion.4.refs_13_), channel_id=1, source_target_pairs={{0,1},{1,0},{2,3},{3,2},{4,5},{5,4},{6,7},{7,6},{8,9},{9,8},{10,11... | collective-permute-start | bytes 1474568 | tf_op jit(solution)/shard_map/ppermute | solution.py:271
  45.6 2.6 %collective-permute-start.16 = (bf16[8,15360]{1,0:T(8,128)(2,1)S(1)}, bf16[8,15360]{1,0:T(8,128)(2,1)S(1)}, u32[]{:S(2)}, u32[]{:S(2)}) collective-permute-start(bf16[8,15360]{1,0:T(8,128)(2,1)S(1)} %collective-permute-done.10.refs_9_), channel_id=1, source_target_pairs={{0,1},{1,0},{2,3},{3,2},{4,5},{5,4},{6,7},{7,6},{8,9},{9,8},{10,11... | collective-permute-start | bytes 737288 | tf_op jit(solution)/shard_map/ppermute | solution.py:271
  46.0 2.6 %collective-permute-start.17 = (bf16[8,15360]{1,0:T(8,128)(2,1)S(1)}, bf16[8,15360]{1,0:T(8,128)(2,1)S(1)}, u32[]{:S(2)}, u32[]{:S(2)}) collective-permute-start(bf16[8,15360]{1,0:T(8,128)(2,1)S(1)} %collective-permute-done.11.refs_10_), channel_id=1, source_target_pairs={{0,1},{1,0},{2,3},{3,2},{4,5},{5,4},{6,7},{7,6},{8,9},{9,8},{10,11... | collective-permute-start | bytes 737288 | tf_op jit(solution)/shard_map/ppermute | solution.py:271
  61.6 1.6 %collective-permute-start.26 = (bf16[8,15360]{1,0:T(8,128)(2,1)S(1)}, bf16[8,15360]{1,0:T(8,128)(2,1)S(1)}, u32[]{:S(2)}, u32[]{:S(2)}) collective-permute-start(bf16[8,15360]{1,0:T(8,128)(2,1)S(1)} %get-tuple-element.95), channel_id=1, source_target_pairs={{0,1},{1,0},{2,3},{3,2},{4,5},{5,4},{6,7},{7,6},{8,9},{9,8},{10,11... | collective-permute-start | bytes 737288 | tf_op jit(solution)/shard_map/ppermute | solution.py:271
  61.9 1.9 %collective-permute-start.28 = (bf16[8,15360]{1,0:T(8,128)(2,1)S(1)}, bf16[8,15360]{1,0:T(8,128)(2,1)S(1)}, u32[]{:S(2)}, u32[]{:S(2)}) collective-permute-start(bf16[8,15360]{1,0:T(8,128)(2,1)S(1)} %get-tuple-element.97), channel_id=1, source_target_pairs={{0,1},{1,0},{2,3},{3,2},{4,5},{5,4},{6,7},{7,6},{8,9},{9,8},{10,11... | collective-permute-start | bytes 737288 | tf_op jit(solution)/shard_map/ppermute | solution.py:271
  62.1 9.6 %collective-permute-start.25 = (bf16[16,15360]{1,0:T(8,128)(2,1)S(1)}, bf16[16,15360]{1,0:T(8,128)(2,1)S(1)}, u32[]{:S(2)}, u32[]{:S(2)}) collective-permute-start(bf16[16,15360]{1,0:T(8,128)(2,1)S(1)} %get-tuple-element.93), channel_id=1, source_target_pairs={{0,1},{1,0},{2,3},{3,2},{4,5},{5,4},{6,7},{7,6},{8,9},{9,8},{10,11... | collective-permute-start | bytes 1474568 | tf_op jit(solution)/shard_map/ppermute | solution.py:271
  63.2 8.2 %collective-permute-start.27 = (bf16[8,15360]{1,0:T(8,128)(2,1)S(1)}, bf16[8,15360]{1,0:T(8,128)(2,1)S(1)}, u32[]{:S(2)}, u32[]{:S(2)}) collective-permute-start(bf16[8,15360]{1,0:T(8,128)(2,1)S(1)} %add_convert_fusion.8), channel_id=1, source_target_pairs={{4,0},{5,1},{8,4},{9,5},{12,8},{13,9},{14,12},{15,13},{10,14},{11,... | collective-permute-start | bytes 737288 | tf_op jit(solution)/shard_map/ppermute | solution.py:270
  63.8 7.9 %collective-permute-start.29 = (bf16[8,15360]{1,0:T(8,128)(2,1)S(1)}, bf16[8,15360]{1,0:T(8,128)(2,1)S(1)}, u32[]{:S(2)}, u32[]{:S(2)}) collective-permute-start(bf16[8,15360]{1,0:T(8,128)(2,1)S(1)} %add_convert_fusion.7), channel_id=1, source_target_pairs={{0,4},{1,5},{4,8},{5,9},{8,12},{9,13},{12,14},{13,15},{14,10},{15,... | collective-permute-start | bytes 737288 | tf_op jit(solution)/shard_map/ppermute | solution.py:269
  65.4 7.7 %collective-permute-start.31 = (bf16[16,15360]{1,0:T(8,128)(2,1)S(1)}, bf16[16,15360]{1,0:T(8,128)(2,1)S(1)}, u32[]{:S(2)}, u32[]{:S(2)}) collective-permute-start(bf16[16,15360]{1,0:T(8,128)(2,1)S(1)} %get-tuple-element.103), channel_id=1, source_target_pairs={{0,1},{1,0},{2,3},{3,2},{4,5},{5,4},{6,7},{7,6},{8,9},{9,8},{10,11... | collective-permute-start | bytes 1474568 | tf_op jit(solution)/shard_map/ppermute | solution.py:271
  71.9 12.5 %collective-permute-start.30 = (bf16[16,15360]{1,0:T(8,128)(2,1)S(1)}, bf16[16,15360]{1,0:T(8,128)(2,1)S(1)}, u32[]{:S(2)}, u32[]{:S(2)}) collective-permute-start(bf16[16,15360]{1,0:T(8,128)(2,1)S(1)} %add_convert_fusion.6), channel_id=1, source_target_pairs={{4,0},{5,1},{8,4},{9,5},{12,8},{13,9},{14,12},{15,13},{10,14},{11,... | collective-permute-start | bytes 1474568 | tf_op jit(solution)/shard_map/ppermute | solution.py:270
  73.2 12.0 %collective-permute-start.32 = (bf16[16,15360]{1,0:T(8,128)(2,1)S(1)}, bf16[16,15360]{1,0:T(8,128)(2,1)S(1)}, u32[]{:S(2)}, u32[]{:S(2)}) collective-permute-start(bf16[16,15360]{1,0:T(8,128)(2,1)S(1)} %add_convert_fusion.5), channel_id=1, source_target_pairs={{0,4},{1,5},{4,8},{5,9},{8,12},{9,13},{12,14},{13,15},{14,10},{15,... | collective-permute-start | bytes 1474568 | tf_op jit(solution)/shard_map/ppermute | solution.py:269
  74.2 11.1 %collective-permute-start.24 = (bf16[16,15360]{1,0:T(8,128)(2,1)S(1)}, bf16[16,15360]{1,0:T(8,128)(2,1)S(1)}, u32[]{:S(2)}, u32[]{:S(2)}) collective-permute-start(bf16[16,15360]{1,0:T(8,128)(2,1)S(1)} %get-tuple-element.91), channel_id=1, source_target_pairs={{0,1},{1,0},{2,3},{3,2},{4,5},{5,4},{6,7},{7,6},{8,9},{9,8},{10,11... | collective-permute-start | bytes 1474568 | tf_op jit(solution)/shard_map/ppermute | solution.py:271
  74.2 13.1 %collective-permute-start.34 = (bf16[16,15360]{1,0:T(8,128)(2,1)S(1)}, bf16[16,15360]{1,0:T(8,128)(2,1)S(1)}, u32[]{:S(2)}, u32[]{:S(2)}) collective-permute-start(bf16[16,15360]{1,0:T(8,128)(2,1)S(1)} %get-tuple-element.111), channel_id=1, source_target_pairs={{0,1},{1,0},{2,3},{3,2},{4,5},{5,4},{6,7},{7,6},{8,9},{9,8},{10,11... | collective-permute-start | bytes 1474568 | tf_op jit(solution)/shard_map/ppermute | solution.py:271
  85.5 12.0 %collective-permute-start.33 = (bf16[16,15360]{1,0:T(8,128)(2,1)S(1)}, bf16[16,15360]{1,0:T(8,128)(2,1)S(1)}, u32[]{:S(2)}, u32[]{:S(2)}) collective-permute-start(bf16[16,15360]{1,0:T(8,128)(2,1)S(1)} %add_convert_fusion.4), channel_id=1, source_target_pairs={{4,0},{5,1},{8,4},{9,5},{12,8},{13,9},{14,12},{15,13},{10,14},{11,... | collective-permute-start | bytes 1474568 | tf_op jit(solution)/shard_map/ppermute | solution.py:270
  87.4 10.9 %collective-permute-start.35 = (bf16[16,15360]{1,0:T(8,128)(2,1)S(1)}, bf16[16,15360]{1,0:T(8,128)(2,1)S(1)}, u32[]{:S(2)}, u32[]{:S(2)}) collective-permute-start(bf16[16,15360]{1,0:T(8,128)(2,1)S(1)} %add_convert_fusion.3), channel_id=1, source_target_pairs={{0,4},{1,5},{4,8},{5,9},{8,12},{9,13},{12,14},{13,15},{14,10},{15,... | collective-permute-start | bytes 1474568 | tf_op jit(solution)/shard_map/ppermute | solution.py:269
  87.8 10.6 %collective-permute-start.23 = (bf16[16,15360]{1,0:T(8,128)(2,1)S(1)}, bf16[16,15360]{1,0:T(8,128)(2,1)S(1)}, u32[]{:S(2)}, u32[]{:S(2)}) collective-permute-start(bf16[16,15360]{1,0:T(8,128)(2,1)S(1)} %get-tuple-element.89), channel_id=1, source_target_pairs={{0,1},{1,0},{2,3},{3,2},{4,5},{5,4},{6,7},{7,6},{8,9},{9,8},{10,11... | collective-permute-start | bytes 1474568 | tf_op jit(solution)/shard_map/ppermute | solution.py:271
  87.8 12.4 %collective-permute-start.37 = (bf16[16,15360]{1,0:T(8,128)(2,1)S(1)}, bf16[16,15360]{1,0:T(8,128)(2,1)S(1)}, u32[]{:S(2)}, u32[]{:S(2)}) collective-permute-start(bf16[16,15360]{1,0:T(8,128)(2,1)S(1)} %get-tuple-element.119), channel_id=1, source_target_pairs={{0,1},{1,0},{2,3},{3,2},{4,5},{5,4},{6,7},{7,6},{8,9},{9,8},{10,11... | collective-permute-start | bytes 1474568 | tf_op jit(solution)/shard_map/ppermute | solution.py:271
  98.6 12.3 %collective-permute-start.36 = (bf16[16,15360]{1,0:T(8,128)(2,1)S(1)}, bf16[16,15360]{1,0:T(8,128)(2,1)S(1)}, u32[]{:S(2)}, u32[]{:S(2)}) collective-permute-start(bf16[16,15360]{1,0:T(8,128)(2,1)S(1)} %add_convert_fusion.2), channel_id=1, source_target_pairs={{4,0},{5,1},{8,4},{9,5},{12,8},{13,9},{14,12},{15,13},{10,14},{11,... | collective-permute-start | bytes 1474568 | tf_op jit(solution)/shard_map/ppermute | solution.py:270
  100.4 12.1 %collective-permute-start.38 = (bf16[16,15360]{1,0:T(8,128)(2,1)S(1)}, bf16[16,15360]{1,0:T(8,128)(2,1)S(1)}, u32[]{:S(2)}, u32[]{:S(2)}) collective-permute-start(bf16[16,15360]{1,0:T(8,128)(2,1)S(1)} %add_convert_fusion.1), channel_id=1, source_target_pairs={{0,4},{1,5},{4,8},{5,9},{8,12},{9,13},{12,14},{13,15},{14,10},{15,... | collective-permute-start | bytes 1474568 | tf_op jit(solution)/shard_map/ppermute | solution.py:269
  100.9 11.6 %collective-permute-start.39 = (bf16[16,15360]{1,0:T(8,128)(2,1)S(1)}, bf16[16,15360]{1,0:T(8,128)(2,1)S(1)}, u32[]{:S(2)}, u32[]{:S(2)}) collective-permute-start(bf16[16,15360]{1,0:T(8,128)(2,1)S(1)} %get-tuple-element.127), channel_id=1, source_target_pairs={{0,1},{1,0},{2,3},{3,2},{4,5},{5,4},{6,7},{7,6},{8,9},{9,8},{10,11... | collective-permute-start | bytes 1474568 | tf_op jit(solution)/shard_map/ppermute | solution.py:271
